TPU v7x, 256 devices: a whole 4x4x8 slice. The times are simulated.
256 devices in a mesh: dp: 8 (over x, core), vocab: 32 (over z, y).
Axes of the slice: x: 4, y: 4, z: 8, core: 2. Of those that a mesh axis runs over, the one named last changes fastest.
Arguments:
- hidden: bfloat16 [1024, 8192], P('dp', 'vocab'), may hold values from -500 to 500, as said below
- norm_gain: float32 [8192], replicated, may hold values from 0.5 to 1.5
- head_weight: bfloat16 [65536, 8192], P('vocab', 'dp'), may hold values from -1 to 1
- target_logits: bfloat16 [1024, 65536], P('dp', 'vocab'), may hold values from -20 to 400
- valid_rows: int32 [1024], P('dp'), may hold values from 0 to 1, as said below
- parents: int32 [1024], P('dp'), may hold values from 0 to 62, as said below
- features: bfloat16 [1024, 24576], P('dp', 'vocab'), may hold values from -0.29882812 to 0.29882812
Outputs:
- grad_hidden: bfloat16 [1024, 8192], P('vocab', 'dp')
- grad_joining: float32 [8192, 24576], P('dp', 'vocab')
Inputs may be any that keep to these rules, and one draw needn't show every extreme that they name: hidden is finite; in some draws a few rows are far from the others. `valid_rows`: row 0 is always valid. `parents`: rows form trees of 64 rows aligned on multiples of 64; a tree's first row has parent 0, every other row a parent before it in its tree, and the last row of each tree has parent 64 - 2.
All inputs are finite; a program needn't handle non-finite values.
Results may differ from a plain program's by a relative error of at most 0.007.
Values may be sent and summed in bfloat16 or wider, within the bound.
A program may use at most 64 MiB of HBM per device.

v0:
```python
import jax
import jax.numpy as jnp
from jax import lax
from jax.sharding import PartitionSpec as P

TREE = 64


def row_logits(normed_rows, head_weight):
    return lax.dot_general(
        normed_rows, head_weight, (((1,), (1,)), ((), ())), preferred_element_type=jnp.float32
    )


def body(hidden, norm_gain, head_weight, target_logits, valid_rows, parents, features):
    group_index = lax.axis_index("dp")
    vocab_index = lax.axis_index("vocab")
    group_rows = hidden.shape[0]
    whole_rows = lax.all_gather(hidden, "vocab", axis=1, tiled=True)
    model_width = whole_rows.shape[1]
    slice_rows = lax.all_to_all(whole_rows, "dp", split_axis=1, concat_axis=0, tiled=True)
    all_rows = slice_rows.shape[0]
    slice_width = slice_rows.shape[1]
    share_rows = all_rows // lax.axis_size("vocab")
    gain_slice = lax.dynamic_slice_in_dim(norm_gain, group_index * slice_width, slice_width)
    live_rows = (valid_rows == 1).astype(jnp.float32)
    square_part = jnp.sum(jnp.square(slice_rows.astype(jnp.float32)), axis=1)
    squares, valid_count = lax.psum((square_part, jnp.sum(live_rows)), "dp")
    row_factor = lax.rsqrt(squares / model_width + 1e-05)
    normed = (slice_rows.astype(jnp.float32) * row_factor[:, None] * gain_slice).astype(
        jnp.bfloat16
    )
    logits = lax.psum_scatter(
        row_logits(normed, head_weight), "dp", scatter_dimension=0, tiled=True
    )
    targets = target_logits.astype(jnp.float32)
    draft_max, target_max = lax.pmax((jnp.max(logits, axis=1), jnp.max(targets, axis=1)), "vocab")
    draft_total, target_total = lax.psum(
        (
            jnp.sum(jnp.exp(logits - draft_max[:, None]), axis=1),
            jnp.sum(jnp.exp(targets - target_max[:, None]), axis=1),
        ),
        "vocab",
    )
    row_weight = 1048576.0 * live_rows / valid_count
    draft_probs = jnp.exp(logits - draft_max[:, None]) / draft_total[:, None]
    target_probs = jnp.exp(targets - target_max[:, None]) / target_total[:, None]
    logit_grad = (row_weight[:, None] * (draft_probs - target_probs)).astype(jnp.bfloat16)
    partial_grad = jnp.dot(
        lax.all_gather(logit_grad, "dp", axis=0, tiled=True),
        head_weight,
        preferred_element_type=jnp.float32,
    )
    normed_grad = lax.psum(partial_grad, "vocab")
    values = slice_rows.astype(jnp.float32)
    row_dot = lax.psum(jnp.sum(gain_slice * values * normed_grad, axis=1), "dp")
    grad_all = (
        row_factor[:, None] * gain_slice * normed_grad
        - values * (row_factor**3 * row_dot / model_width)[:, None]
    ).astype(jnp.bfloat16)
    grad_share = lax.dynamic_slice_in_dim(grad_all, vocab_index * share_rows, share_rows, 0)
    tree_rows = jnp.arange(group_rows, dtype=jnp.int32) // TREE * TREE + parents
    chosen = jnp.take(features, tree_rows, axis=0)
    grad_joining = lax.dot_general(
        grad_all,
        lax.all_gather(chosen, "dp", axis=0, tiled=True),
        (((0,), (0,)), ((), ())),
        preferred_element_type=jnp.float32,
    )
    return (grad_share, grad_joining)


def solution(mesh):
    placed = (
        P("dp", "vocab"),
        P(),
        P("vocab", "dp"),
        P("dp", "vocab"),
        P("dp"),
        P("dp"),
        P("dp", "vocab"),
    )
    return jax.shard_map(
        body,
        mesh=mesh,
        in_specs=placed,
        out_specs=(P("vocab", "dp"), P("dp", "vocab")),
        check_vma=False,
    )
```

profile of v0, /device:TPU:24, one launch (start us, length us, event | category | flops | bytes accessed | tf_op | source)
XLA Modules:
  0.0 591.5 jit_solution(4355535598762922581)
XLA Ops:
  7.9 79.7 %all-gather.4.cloned.1.call-done = bf16[128,8192]{1,0:T(8,128)(2,1)} async-done(((bf16[128,256]{1,0:T(8,128)(2,1)}), bf16[128,8192]{1,0:T(8,128)(2,1)}) %all-gather.4.cloned.1.call-update) | async-done | bytes 2097168 | tf_op jit(solution)/shard_map/all_gather | solution.py:19
  87.6 3.2 copy.13
  90.8 4.3 all-to-all-start
  96.4 25.8 %all-to-all-done = bf16[128,8,1024]{2,0,1:T(8,128)(2,1)S(1)} async-done(((bf16[128,8,1024]{2,0,1:T(8,128)(2,1)}), bf16[128,8,1024]{2,0,1:T(8,128)(2,1)S(1)}, u32[]{:S(2)}, u32[]{:S(2)}) %all-to-all-start) | async-done | bytes 2097184 | tf_op jit(solution)/shard_map/all_to_all | solution.py:21
  122.7 13.6 %all-reduce.2 = (f32[1024]{0:T(1024)S(1)}, f32[]{:T(128)}) all-reduce(f32[1024]{0:T(1024)S(1)} %bitcast.33, f32[]{:T(128)} %fusion.14), channel_id=1, replica_groups=mesh['dp'=8,'vocab'=32] {'dp'}, use_global_device_ids=true, to_apply=%region_1.0 | all-reduce | flops 1025 | bytes 8200 | tf_op jit(solution)/shard_map/psum | solution.py:28
  136.9 1.6 copy-done.3
  138.5 6.7 %fusion.15 = f32[1024,2048]{1,0:T(8,128)} fusion(bf16[1024,1024]{1,0:T(8,128)(2,1)S(1)} %fusion.2, bf16[2048,1024]{1,0:T(8,128)(2,1)S(1)} %copy-done.3), kind=kOutput, calls=%fused_computation.37 | convolution fusion | flops 4294967296 | bytes 14680064 | tf_op jit(solution)/shard_map/dot_general | solution.py:10
  145.3 1.0 copy-done.1
  147.1 50.2 %reduce-scatter.2.cloned.1.call-done = f32[128,2048]{1,0:T(8,128)} async-done(((f32[1024,2048]{1,0:T(8,128)}), f32[128,2048]{1,0:T(8,128)}) %reduce-scatter.2.cloned.1.call-update) | async-done | bytes 1048592 | tf_op jit(solution)/shard_map/reduce_scatter | solution.py:33
  197.2 1.4 reduce_max.23
  198.6 68.2 %all-reduce.1 = (f32[128]{0:T(128)S(1)}, f32[128]{0:T(128)S(1)}) all-reduce(bf16[128]{0:T(256)(128)(2,1)S(1)} %reduce_max.24, f32[128]{0:T(128)S(1)} %reduce_max.23), channel_id=1, replica_groups=mesh['dp'=8,'vocab'=32] {'vocab'}, use_global_device_ids=true, to_apply=%region_10.0 | all-reduce | flops 256 | bytes 1792 | tf_op jit(solution)/shard_map/pmax | solution.py:37
  266.8 1.7 fusion.7
  268.5 74.1 %all-reduce = (f32[128]{0:T(128)S(1)}, f32[128]{0:T(128)S(1)}) all-reduce(f32[128]{0:T(128)S(1)} %get-tuple-element.10, f32[128]{0:T(128)S(1)} %get-tuple-element.11), channel_id=1, replica_groups=mesh['dp'=8,'vocab'=32] {'vocab'}, use_global_device_ids=true, to_apply=%region_12.0 | all-reduce | flops 256 | bytes 2048 | tf_op jit(solution)/shard_map/psum | solution.py:38
  342.6 2.5 multiply_convert_fusion
  345.2 33.5 %all-gather.6.cloned.1.call-done = bf16[1024,2048]{1,0:T(8,128)(2,1)} async-done(((bf16[128,2048]{1,0:T(8,128)(2,1)}), bf16[1024,2048]{1,0:T(8,128)(2,1)}) %all-gather.6.cloned.1.call-update) | async-done | bytes 4194320 | tf_op jit(solution)/shard_map/all_gather | solution.py:50
  378.6 9.9 %fusion.16 = f32[1024,1024]{1,0:T(8,128)} fusion(bf16[1024,2048]{1,0:T(8,128)(2,1)} %all-gather.6.cloned.1.call-done, bf16[2048,1024]{1,0:T(8,128)(2,1)} %param.9), kind=kOutput, calls=%fused_computation.38 | convolution fusion | flops 4294967296 | bytes 12582912 | tf_op jit(solution)/shard_map/dot_general | solution.py:49
  389.2 0.9 gather_fusion
  390.9 160.5 %all-reduce.5.cloned.1.call-done = f32[1024,1024]{1,0:T(8,128)} async-done(((f32[1024,1024]{1,0:T(8,128)}), f32[1024,1024]{1,0:T(8,128)}) %all-reduce.5.cloned.1.call-update) | async-done | bytes 4194320 | tf_op jit(solution)/shard_map/psum | solution.py:54
  551.4 2.8 fusion.4
  554.2 12.6 %psum.47 = f32[1024]{0:T(1024)S(1)} all-reduce(f32[1024]{0:T(1024)S(1)} %fusion.4), channel_id=1, replica_groups=mesh['dp'=8,'vocab'=32] {'dp'}, use_global_device_ids=true, to_apply=%region_15.0 | all-reduce | flops 1024 | bytes 8192 | tf_op jit(solution)/shard_map/psum | solution.py:56
  566.8 3.0 fusion.6
  569.8 1.3 copy-done.2
  571.8 7.6 %all-gather.8.cloned.1.call-done = bf16[1024,768]{1,0:T(8,128)(2,1)} async-done(((bf16[128,768]{1,0:T(8,128)(2,1)}), bf16[1024,768]{1,0:T(8,128)(2,1)}) %all-gather.8.cloned.1.call-update) | async-done | bytes 1572880 | tf_op jit(solution)/shard_map/all_gather | solution.py:66
  579.4 5.6 fusion.17
  (31 shorter events, 6.1 us)
Async XLA Ops:
  7.2 382.0 %copy-start = (bf16[128,768]{1,0:T(8,128)(2,1)S(1)}, bf16[128,768]{1,0:T(8,128)(2,1)}, u32[]{:S(2)}) copy-start(bf16[128,768]{1,0:T(8,128)(2,1)} %param.13) | copy-start | bytes 589828
  7.2 80.5 %all-gather.4.cloned.1.call-start = ((), (), s32[]{:S(2)}) async-start(), calls=%async_computation.2 | async-start | bytes 2162688 | tf_op jit(solution)/shard_map/all_gather | solution.py:19
  87.6 8.2 %copy-start.4 = (s32[128]{0:T(128)S(1)}, s32[128]{0:T(128)}, u32[]{:S(2)}) copy-start(s32[128]{0:T(128)} %param.11) | copy-start | bytes 1540
  90.8 31.4 %all-to-all-start = ((bf16[128,8,1024]{2,0,1:T(8,128)(2,1)}), bf16[128,8,1024]{2,0,1:T(8,128)(2,1)S(1)}, u32[]{:S(2)}, u32[]{:S(2)}) async-start(bf16[128,8,1024]{2,0,1:T(8,128)(2,1)} %bitcast.31), calls=%async_computation | async-start | bytes 4194304 | tf_op jit(solution)/shard_map/all_to_all | solution.py:21
  95.1 102.2 %reduce-scatter.2.cloned.1.call-start = ((), (), s32[]{:S(2)}) async-start(), calls=%async_computation.3 | async-start | bytes 9437184 | tf_op jit(solution)/shard_map/reduce_scatter | solution.py:33
  136.3 2.2 copy-start.3
  145.2 1.0 copy-start.1
  145.3 233.4 %all-gather.6.cloned.1.call-start = ((), (), s32[]{:S(2)}) async-start(), calls=%async_computation.4 | async-start | bytes 4718592 | tf_op jit(solution)/shard_map/all_gather | solution.py:50
  345.1 206.3 %all-reduce.5.cloned.1.call-start = ((), (), s32[]{:S(2)}) async-start(), calls=%async_computation.5 | async-start | bytes 8388608 | tf_op jit(solution)/shard_map/psum | solution.py:54
  388.5 0.7 copy-start.5
  388.5 190.9 %all-gather.8.cloned.1.call-start = ((), (), s32[]{:S(2)}) async-start(), calls=%async_computation.6 | async-start | bytes 1769472 | tf_op jit(solution)/shard_map/all_gather | solution.py:66
  569.8 1.4 copy-start.2
Sparse Core Ops, SparseCore 0:
  10.5 77.1 all-gather.3
  145.4 51.8 reduce-scatter.1
  345.2 33.3 all-gather.5
  388.7 162.6 all-reduce.4
  553.6 25.7 all-gather.7
where the time goes:
time: 594 us; the launch traced here: 592 us
  waiting for transfers between devices  358 us (60%)
  blocking collectives  168 us (28%)
  matrix products  22.2 us (4%)
  other arithmetic  14.6 us (2%)
  between operations  13.9 us (2%)
  local copies, waits for them, and re-layouts  9.89 us (2%)
    psum x1, waiting for transfers between devices, body(): normed_grad = lax.psum(partial_grad, 'vocab')  161 us
    all_gather x1, waiting for transfers between devices, body(): whole_rows = lax.all_gather(hidden, 'vocab', axis=1, tiled=True)  79.7 us
    psum x1, blocking collectives, body(): lax.psum((jnp.sum(jnp.exp(logits - draft_max[:, None]), axis=1), jnp.sum(...  74.1 us
    pmax x1, blocking collectives, body(): lax.pmax((jnp.max(logits, axis=1), jnp.max(targets, axis=1)), 'vocab')  68.2 us
    reduce_scatter x1, waiting for transfers between devices, body(): lax.psum_scatter(row_logits(normed, head_weight), 'dp', scatter_dimension...  50.2 us
    all_gather x1, waiting for transfers between devices, body(): lax.all_gather(logit_grad, 'dp', axis=0, tiled=True)  33.5 us
    all_to_all x1, waiting for transfers between devices, body(): lax.all_to_all(whole_rows, 'dp', split_axis=1, concat_axis=0, tiled=True)  25.8 us
    psum x1, blocking collectives, body(): squares, valid_count = lax.psum((square_part, jnp.sum(live_rows)), 'dp')  13.6 us
  transfers between devices with their start and end apart: 6, of which 6 were waited for; matrix products, arithmetic and copies ran while one was open for 2% of the time, Pallas kernels for 0%

commit v1 on v0

v1 whole, which is shorter than its diff:
```python
import functools

import jax
import jax.numpy as jnp
from jax import lax
from jax.experimental import pallas as pl
from jax.experimental.pallas import tpu as pltpu
from jax.sharding import PartitionSpec as P

TREE = 64
NX, NC, NY, NZ = 4, 2, 4, 8
F32, BF16 = jnp.float32, jnp.bfloat16
DMA = pltpu.SemaphoreType.DMA


def remote(src, dst, send_sem, recv_sem, device):
    return pltpu.make_async_remote_copy(
        src_ref=src,
        dst_ref=dst,
        send_sem=send_sem,
        recv_sem=recv_sem,
        device_id=device,
        device_id_type=pl.DeviceIdType.MESH,
    )


class Place:
    def __init__(self):
        self.g = lax.axis_index("dp")
        self.v = lax.axis_index("vocab")
        self.x, self.c = self.g // NC, self.g % NC
        self.z, self.y = self.v // NY, self.v % NY

    def dp(self, i):
        return (i, self.v)

    def at_x(self, x):
        return (x * NC + self.c, self.v)

    def partner(self):
        return (self.x * NC + 1 - self.c, self.v)

    def at_y(self, y):
        return (self.g, self.z * NY + y)

    def at_z(self, z):
        return (self.g, z * NY + self.y)


def greet(peers):
    barrier = pltpu.get_barrier_semaphore()
    for peer in peers:
        pl.semaphore_signal(
            barrier, inc=1, device_id=peer, device_id_type=pl.DeviceIdType.MESH
        )
    pl.semaphore_wait(barrier, len(peers))


class Sender:
    def __init__(self, sems):
        self.sems, self.used, self.copies = sems, 0, []

    def __call__(self, src, dst, recv_sem, device):
        copy = remote(src, dst, self.sems.at[self.used], recv_sem, device)
        self.used += 1
        copy.start()
        self.copies.append(copy)

    def drain(self):
        for copy in self.copies:
            copy.wait_send()


def arrived(dst, recv_sem, device, any_sem):
    remote(dst, dst, any_sem, recv_sem, device).wait_recv()


class Gather:
    def __init__(self, at, buf, send, near, far, pair):
        self.at, self.buf, self.send = at, buf, send
        self.near, self.far, self.pair = near, far, pair

    def slot(self, step, core):
        return ((self.at.x + step) % NX) * NC + core

    def start(self, half):
        at, buf = self.at, self.buf
        mine = buf.at[at.g, half]
        self.send(mine, mine, self.near.at[0, half], at.at_x((at.x + 1) % NX))
        self.send(mine, mine, self.near.at[1, half], at.at_x((at.x + 3) % NX))
        self.send(mine, mine, self.pair.at[0, half], at.partner())

    def middle(self):
        at, buf = self.at, self.buf
        for half in range(2):
            for side, step in ((0, 3), (1, 1)):
                block = buf.at[self.slot(step, at.c), half]
                arrived(block, self.near.at[side, half], at.partner(), self.near.at[side, half])
                if half == side:
                    onward = at.at_x((at.x + (1 if side == 0 else 3)) % NX)
                    self.send(block, block, self.far.at[half], onward)
                self.send(block, block, self.pair.at[step, half], at.partner())

    def last(self):
        at, buf = self.at, self.buf
        for half in range(2):
            block = buf.at[self.slot(2, at.c), half]
            arrived(block, self.far.at[half], at.partner(), self.far.at[half])
            self.send(block, block, self.pair.at[2, half], at.partner())

    def paired(self, step):
        at = self.at
        for half in range(2):
            block = self.buf.at[self.slot(step, 1 - at.c), half]
            arrived(block, self.pair.at[step, half], at.partner(), self.pair.at[step, half])


GATHER_SENDS = 14


def row_tile(column):
    return jnp.transpose(jnp.broadcast_to(column, (128, 128)))[0:8]


def column_tile(row):
    return jnp.transpose(jnp.broadcast_to(row, (128, 128)))


def stack_rows(*rows):
    index = lax.broadcasted_iota(jnp.int32, (8, 128), 0)
    tile = jnp.zeros((8, 128), F32)
    for k, row in enumerate(rows):
        tile = jnp.where(index == k, row, tile)
    return tile


def spread_kernel(
    hid, live, gain, feat,
    n_out, vals_out, rf_out, f_out,
    zbuf, xall, stat, cols,
    send_sems, f_sems, zr, xs, xr, yr, y2, sr, fr, own_sems,
    f_near, f_far, f_pair,
):
    at = Place()
    x, c, y, z, g = at.x, at.c, at.y, at.z, at.g
    up_z, down_z = at.at_z((z + 1) % NZ), at.at_z((z + NZ - 1) % NZ)
    up_y, down_y = at.at_y((y + 1) % NY), at.at_y((y + 3) % NY)
    greet(
        [at.dp((g + k) % 8) for k in range(1, 8)]
        + [up_z, down_z]
        + [at.at_y((y + k) % NY) for k in range(1, NY)]
    )
    send = Sender(send_sems)
    spread = Gather(at, f_out, Sender(f_sems), f_near, f_far, f_pair)
    own_feat = pltpu.make_async_copy(feat, f_out.at[g], own_sems.at[0])
    own_feat.start()

    def to_slice(src, j):
        @pl.when(j != g)
        def _():
            remote(src, xall.at[y, g], xs.at[j], xr.at[g], at.dp(j)).start()

        @pl.when(j == g)
        def _():
            pltpu.make_async_copy(src, xall.at[y, g], xs.at[j]).start()

    for step in range(5):
        low, high = (z + NZ - step) % NZ, (z + step) % NZ
        if step > 0:
            arrived(zbuf.at[low], zr.at[low], up_z, zr.at[low])
        src = hid if step == 0 else zbuf.at[low]
        if step < 4:
            send(src, zbuf.at[low], zr.at[low], up_z)
        to_slice(src, low)
        if step == 0:
            send(hid, zbuf.at[high], zr.at[high], down_z)
        elif step < 4:
            arrived(zbuf.at[high], zr.at[high], up_z, zr.at[high])
            if step < 3:
                send(zbuf.at[high], zbuf.at[high], zr.at[high], down_z)
            to_slice(zbuf.at[high], high)

    own_feat.wait()
    for half in range(2):
        spread.start(half)
    squares = jnp.square(hid[...].astype(F32))
    for k in range(1, NZ):
        squares = squares + jnp.square(zbuf[(z + k) % NZ].astype(F32))
    stat[y] = row_tile(jnp.sum(squares, axis=1, keepdims=True))
    for k in range(1, NY):
        send(stat.at[y], stat.at[y], sr.at[y], at.at_y((y + k) % NY))

    for i in range(8):
        block = xall.at[y, i]

        @pl.when(g != i)
        def _():
            arrived(block, xr.at[i], up_y, xr.at[i])

        @pl.when(g == i)
        def _():
            pltpu.make_async_copy(hid, block, xs.at[i]).wait()

        send(block, block, yr.at[0, i], up_y)
        send(block, block, yr.at[1, i], down_y)

    total = stat[y]
    for k in range(1, NY):
        other = (y + k) % NY
        arrived(stat.at[other], sr.at[other], up_y, sr.at[other])
        total = total + stat[other]
    factor = lax.rsqrt(total / (1024.0 * 8) + 1e-05)
    rf_out[g] = stack_rows(factor[0:1], live[...])
    for k in range(1, 8):
        other = (g + k) % 8
        send(rf_out.at[g], rf_out.at[g], fr.at[g], at.dp(other))

    spread.middle()
    for i in range(8):
        for side, step in ((0, 3), (1, 1)):
            block = xall.at[(y + step) % NY, i]
            arrived(block, yr.at[side, i], up_y, yr.at[side, i])
            if (i < 4) == (side == 0):
                send(block, block, y2.at[i], up_y if side == 0 else down_y)
    spread.last()
    for k in range(1, 8):
        other = (g + k) % 8
        arrived(rf_out.at[other], fr.at[other], up_y, fr.at[other])
    for i in range(8):
        cols[i] = column_tile(rf_out[i, 0:1])
    for i in range(8):
        block = xall.at[(y + 2) % NY, i]
        arrived(block, y2.at[i], up_y, y2.at[i])

    @pl.loop(0, 8)
    def _(i):
        scale = cols[i]
        scale = jnp.concatenate([scale, scale], axis=1)
        rows = pl.ds(pl.multiple_of(i * 128, 128), 128)
        for part in range(NY):
            columns = slice(part * 256, part * 256 + 256)
            values = xall[part, i].astype(F32)
            n_out[rows, columns] = (values * scale * gain[:, columns]).astype(BF16)

    for part in range(NY):
        vals_out[:, part * 256 : part * 256 + 256] = xall[
            part, z, pl.ds(pl.multiple_of(y * 32, 32), 32), :
        ]
    for step in range(4):
        spread.paired(step)
    send.drain()
    spread.send.drain()
    for j in range(8):

        @pl.when(g != j)
        def _():
            remote(hid, xall.at[y, g], xs.at[j], xr.at[g], at.dp(j)).wait_send()


def main_kernel(
    normed, weight, targets, rf, vals, gain,
    share_out, grad_out,
    pk, pr, sb, rl, fin, lg, tst, stat_y, stat_z, gbuf, pf, ysb, yrl, yfin,
    qown, qs, zrs, rds, rdr, rfcol,
    pair_s, pair_r, sb_s, rl_r, fin_r,
    send_sems, sty, stz, g_sems, g_near, g_far, g_pair,
    yrl_r, yfin_r, zs_s, zs_r, rd_r, a_z, a_y, a_y2,
):
    at = Place()
    x, c, y, z, g = at.x, at.c, at.y, at.z, at.g
    up_z, down_z = at.at_z((z + 1) % NZ), at.at_z((z + NZ - 1) % NZ)
    up_y, down_y = at.at_y((y + 1) % NY), at.at_y((y + 3) % NY)
    greet(
        [at.dp((g + k) % 8) for k in range(1, 8)]
        + [at.at_z((z + k) % NZ) for k in range(1, NZ)]
        + [at.at_y((y + k) % NY) for k in range(1, NY)]
    )
    send = Sender(send_sems)

    def multiply(t):
        tile = pl.ds(pl.multiple_of(t * 256, 256), 256)
        for d in range(NX):
            part = lax.dot_general(
                normed[d * 256 : d * 256 + 256, :],
                weight[tile, :],
                (((1,), (1,)), ((), ())),
                preferred_element_type=F32,
            )
            pk[t, 0, d] = part[:128]
            pk[t, 1, d] = part[128:]
        remote(
            pk.at[t, 1 - c], pr.at[t], pair_s.at[t], pair_r.at[t], at.partner()
        ).start()

    def hops(t):
        way = 1 + 2 * (t % 2)
        return (x + way) % NX, (x + 4 - way) % NX

    def direct(t, started):
        ahead, back = hops(t)
        return (
            remote(sb.at[t, 0], rl.at[t], sb_s.at[t, 0], rl_r.at[t], at.at_x(ahead)),
            remote(sb.at[t, 1], fin.at[t, 0], sb_s.at[t, 1], fin_r.at[t, 0], at.at_x(back)),
        )

    def onward(t):
        ahead, _ = hops(t)
        return remote(sb.at[t, 2], fin.at[t, 1], sb_s.at[t, 2], fin_r.at[t, 1], at.at_x(ahead))

    def encode(t, k, value):
        top = jnp.max(jnp.abs(value), axis=0, keepdims=True)
        step = (120.0 / jnp.maximum(top, 1e-30)).astype(BF16)
        sb[t, k, 128:] = jnp.broadcast_to(step, (16, 256))
        step = sb[t, k, 128:].astype(F32)[0:1]
        sb[t, k, :128] = jnp.exp2(value * step).astype(BF16)

    def decode(block):
        step = block[128:].astype(F32)[0:1]
        return jnp.log2(block[:128].astype(F32)) * (1.0 / step)

    def pair_sum(t):
        ahead, back = hops(t)
        far = (x + 2) % NX
        arrived(pr.at[t], pair_r.at[t], at.partner(), pair_r.at[t])
        encode(t, 0, pk[t, c, far] + pr[t, far])
        encode(t, 1, pk[t, c, back] + pr[t, back])
        for copy in direct(t, True):
            copy.start()

    def relay(t):
        ahead, _ = hops(t)
        arrived(rl.at[t], rl_r.at[t], at.partner(), rl_r.at[t])
        encode(t, 2, pk[t, c, ahead] + pr[t, ahead] + decode(rl.at[t]))
        onward(t).start()

    def finish(t):
        for k in range(2):
            arrived(fin.at[t, k], fin_r.at[t, k], at.partner(), fin_r.at[t, k])
        lg[t] = pk[t, c, x] + pr[t, x] + decode(fin.at[t, 0]) + decode(fin.at[t, 1])

    @pl.loop(0, 11)
    def _(t):
        @pl.when(t < 8)
        def _():
            multiply(t)

        @pl.when((t >= 1) & (t < 9))
        def _():
            pair_sum(t - 1)

        @pl.when((t >= 2) & (t < 10))
        def _():
            relay(t - 2)

        @pl.when(t >= 3)
        def _():
            finish(t - 3)

        @pl.when(t == 8)
        def _():
            top = jnp.max(targets[...].astype(F32), axis=1, keepdims=True)
            part = jnp.zeros((128, 256), F32)
            for k in range(8):
                part = part + jnp.exp(targets[:, k * 256 : k * 256 + 256].astype(F32) - top)
            tst[...] = stack_rows(
                jnp.zeros((1, 128), F32),
                jnp.zeros((1, 128), F32),
                row_tile(top)[0:1],
                row_tile(jnp.sum(part, axis=1, keepdims=True))[0:1],
            )

    top = lg[0]
    for t in range(1, 8):
        top = jnp.maximum(top, lg[t])
    top = jnp.max(top, axis=1, keepdims=True)
    part = jnp.zeros((128, 256), F32)
    for t in range(8):
        part = part + jnp.exp(lg[t] - top)
    stat_y[y] = stack_rows(
        row_tile(top)[0:1],
        row_tile(jnp.sum(part, axis=1, keepdims=True))[0:1],
        tst[2:3],
        tst[3:4],
    )
    for k in range(1, NY):
        send(stat_y.at[y], stat_y.at[y], sty.at[y], at.at_y((y + k) % NY))

    def combine(tiles):
        out = []
        for k in (0, 2):
            m = tiles[0][k : k + 1]
            for tile in tiles[1:]:
                m = jnp.maximum(m, tile[k : k + 1])
            s = jnp.zeros((1, 128), F32)
            for tile in tiles:
                s = s + tile[k + 1 : k + 2] * jnp.exp(tile[k : k + 1] - m)
            out += [m, s]
        return out

    tiles = [stat_y[y]]
    for k in range(1, NY):
        other = (y + k) % NY
        arrived(stat_y.at[other], sty.at[other], up_y, sty.at[other])
        tiles.append(stat_y[other])
    stat_z[z] = stack_rows(*combine(tiles))
    for k in range(1, NZ):
        send(stat_z.at[z], stat_z.at[z], stz.at[z], at.at_z((z + k) % NZ))
    tiles = [stat_z[z]]
    for k in range(1, NZ):
        other = (z + k) % NZ
        arrived(stat_z.at[other], stz.at[other], up_y, stz.at[other])
        tiles.append(stat_z[other])
    draft_max, draft_sum, target_max, target_sum = combine(tiles)
    live = jnp.zeros((1, 128), F32)
    for i in range(8):
        live = live + rf[i, 1:2]
    count = jnp.sum(live, axis=1, keepdims=True)
    scale = 1048576.0 * rf[g][1:2] / count
    wide = lambda row: jnp.concatenate([column_tile(row)] * 2, axis=1)
    draft_top, target_top = wide(draft_max), wide(target_max)
    draft_scale, target_scale = wide(1.0 / draft_sum), wide(1.0 / target_sum)
    scale = wide(scale)

    gather = Gather(at, gbuf, Sender(g_sems), g_near, g_far, g_pair)
    for t in range(8):
        draft = jnp.exp(lg[t] - draft_top) * draft_scale
        target = (
            jnp.exp(targets[:, t * 256 : t * 256 + 256].astype(F32) - target_top)
            * target_scale
        )
        column = (t % 4) * 256
        gbuf[g, t // 4, :, column : column + 256] = (scale * (draft - target)).astype(BF16)
        if t % 4 == 3:
            gather.start(t // 4)

    def backward(k, step):
        block = pl.ds(((x + step) % NX) * NC, 2)

        @pl.loop(0, 4)
        def _(n):
            columns = pl.ds(pl.multiple_of(n * 256, 256), 256)
            part = jnp.zeros((256, 256), F32)
            for half in range(2):
                part = part + jnp.dot(
                    gbuf[block, half].reshape(256, 1024),
                    weight[half * 1024 : half * 1024 + 1024, columns],
                    preferred_element_type=F32,
                )
            for which in range(2):
                for dest in range(NY):
                    row = which * 128 + dest * 32
                    pf[k, dest, which, :, columns] = part[row : row + 32]

    def y_first(k):
        way = 1 if k % 2 == 0 else 3
        ysb[k, 0] = pf[k, (y + 2) % NY].astype(BF16)
        send(ysb.at[k, 0], yrl.at[k], yrl_r.at[k], at.at_y((y + way) % NY))
        ysb[k, 1] = pf[k, (y + 4 - way) % NY].astype(BF16)
        send(ysb.at[k, 1], yfin.at[k, 0], yfin_r.at[k, 0], at.at_y((y + 4 - way) % NY))

    def y_second(k):
        way = 1 if k % 2 == 0 else 3
        arrived(yrl.at[k], yrl_r.at[k], up_y, yrl_r.at[k])
        ysb[k, 2] = (pf[k, (y + way) % NY] + yrl[k].astype(F32)).astype(BF16)
        send(ysb.at[k, 2], yfin.at[k, 1], yfin_r.at[k, 1], at.at_y((y + way) % NY))

    def z_send(dest):
        return remote(qs.at[dest], zrs.at[z], zs_s.at[dest], zs_r.at[z], at.at_z(dest))

    def y_third(k, step):
        for j in range(2):
            arrived(yfin.at[k, j], yfin_r.at[k, j], up_y, yfin_r.at[k, j])
        for which in range(2):
            dest = ((x + step) % NX) * 2 + which
            value = (
                pf[k, y, which]
                + yfin[k, 0, which].astype(F32)
                + yfin[k, 1, which].astype(F32)
            )

            @pl.when(dest == z)
            def _():
                qown[...] = value

            @pl.when(dest != z)
            def _():
                qs[dest] = value.astype(BF16)
                z_send(dest).start()

    gather.paired(0)
    backward(0, 0)
    y_first(0)
    gather.middle()
    gather.paired(3)
    backward(1, 3)
    y_first(1)
    y_second(0)
    gather.paired(1)
    backward(2, 1)
    y_first(2)
    y_second(1)
    y_third(0, 0)
    gather.last()
    gather.paired(2)
    backward(3, 2)
    y_first(3)
    y_second(2)
    y_third(1, 3)
    y_second(3)
    y_third(2, 1)
    y_third(3, 2)

    values = vals[...].astype(F32)
    rfcol[...] = column_tile(rf[z][0:1])
    factor = rfcol[pl.ds(pl.multiple_of(y * 32, 32), 32), :]
    total = qown[...]
    for k in range(1, NZ):
        other = (z + k) % NZ
        arrived(zrs.at[other], zs_r.at[other], up_y, zs_r.at[other])
        total = total + zrs[other].astype(F32)
    dot = jnp.sum(gain[...] * values * total, axis=1, keepdims=True)
    dot = jnp.broadcast_to(dot, (32, 128))
    rds[...] = dot
    for k in range(1, 8):
        send(rds, rdr.at[g], rd_r.at[g], at.dp((g + k) % 8))
    for k in range(1, 8):
        other = (g + k) % 8
        arrived(rdr.at[other], rd_r.at[other], up_y, rd_r.at[other])
        dot = dot + rdr[other]
    pull = factor * factor * factor * dot / (1024.0 * 8)
    broad = lambda tile: jnp.concatenate([tile] * 8, axis=1)
    grad = (broad(factor) * gain[...] * total - values * broad(pull)).astype(BF16)
    share_out[...] = grad
    grad_out[z, y] = grad

    order = []

    def to_y(block_z):
        k = len(order)
        block = grad_out.at[block_z, y]
        send(block, block, a_y.at[0, k], up_y)
        send(block, block, a_y.at[1, k], down_y)
        order.append(block_z)

    done = [0]

    def pass_y(count):
        while done[0] < count:
            k = done[0]
            for side, step in ((0, 3), (1, 1)):
                block = grad_out.at[order[k], (y + step) % NY]
                arrived(block, a_y.at[side, k], up_y, a_y.at[side, k])
                if k % 2 == side:
                    send(block, block, a_y2.at[k], up_y if side == 0 else down_y)
            done[0] += 1

    for step in range(5):
        low, high = (z + NZ - step) % NZ, (z + step) % NZ
        block = grad_out.at[low, y]
        if step > 0:
            arrived(block, a_z.at[low], up_z, a_z.at[low])
        if step < 4:
            send(block, block, a_z.at[low], up_z)
        if step == 0:
            send(block, block, a_z.at[high], down_z)
        to_y(low)
        if 0 < step < 4:
            block = grad_out.at[high, y]
            arrived(block, a_z.at[high], up_z, a_z.at[high])
            if step < 3:
                send(block, block, a_z.at[high], down_z)
            to_y(high)
        if step > 0:
            pass_y(max(0, 2 * step - 1))
    pass_y(8)
    for k in range(8):
        block = grad_out.at[order[k], (y + 2) % NY]
        arrived(block, a_y2.at[k], up_y, a_y2.at[k])

    @pl.loop(0, 8)
    def _(t):
        remote(
            pk.at[t, 1 - c], pr.at[t], pair_s.at[t], pair_r.at[t], at.partner()
        ).wait_send()
        for copy in direct(t, False):
            copy.wait_send()
        onward(t).wait_send()

    send.drain()
    gather.send.drain()
    for k in range(1, NZ):
        z_send((z + k) % NZ).wait_send()


VMEM = pl.BlockSpec(memory_space=pltpu.VMEM)
LIMIT = 60 * 1024 * 1024


def spread_call(hidden, live, gain, feat):
    return pl.pallas_call(
        spread_kernel,
        out_shape=(
            jax.ShapeDtypeStruct((1024, 1024), BF16),
            jax.ShapeDtypeStruct((32, 1024), BF16),
            jax.ShapeDtypeStruct((8, 8, 128), F32),
            jax.ShapeDtypeStruct((8, 2, 64, 768), BF16),
        ),
        in_specs=[VMEM] * 4,
        out_specs=[VMEM] * 4,
        scratch_shapes=[
            pltpu.VMEM((NZ, 128, 256), BF16),
            pltpu.VMEM((NY, 8, 128, 256), BF16),
            pltpu.VMEM((NY, 8, 128), F32),
            pltpu.VMEM((8, 128, 128), F32),
            DMA((41,)),
            DMA((GATHER_SENDS,)),
            DMA((NZ,)),
            DMA((8,)),
            DMA((8,)),
            DMA((2, 8)),
            DMA((8,)),
            DMA((NY,)),
            DMA((8,)),
            DMA((1,)),
            DMA((2, 2)),
            DMA((2,)),
            DMA((4, 2)),
        ],
        compiler_params=pltpu.CompilerParams(
            collective_id=0, has_side_effects=True, vmem_limit_bytes=LIMIT
        ),
    )(hidden, live, gain, feat)


def main_call(normed, weight, targets, rf, vals, gain):
    return pl.pallas_call(
        main_kernel,
        out_shape=(
            jax.ShapeDtypeStruct((32, 1024), BF16),
            jax.ShapeDtypeStruct((NZ, NY, 32, 1024), BF16),
        ),
        in_specs=[VMEM] * 6,
        out_specs=[VMEM] * 2,
        scratch_shapes=[
            pltpu.VMEM((8, 2, NX, 128, 256), F32),
            pltpu.VMEM((8, NX, 128, 256), F32),
            pltpu.VMEM((8, 3, 144, 256), BF16),
            pltpu.VMEM((8, 144, 256), BF16),
            pltpu.VMEM((8, 2, 144, 256), BF16),
            pltpu.VMEM((8, 128, 256), F32),
            pltpu.VMEM((8, 128), F32),
            pltpu.VMEM((NY, 8, 128), F32),
            pltpu.VMEM((NZ, 8, 128), F32),
            pltpu.VMEM((8, 2, 128, 1024), BF16),
            pltpu.VMEM((4, NY, 2, 32, 1024), F32),
            pltpu.VMEM((4, 3, 2, 32, 1024), BF16),
            pltpu.VMEM((4, 2, 32, 1024), BF16),
            pltpu.VMEM((4, 2, 2, 32, 1024), BF16),
            pltpu.VMEM((32, 1024), F32),
            pltpu.VMEM((NZ, 32, 1024), BF16),
            pltpu.VMEM((NZ, 32, 1024), BF16),
            pltpu.VMEM((32, 128), F32),
            pltpu.VMEM((8, 32, 128), F32),
            pltpu.VMEM((128, 128), F32),
            DMA((8,)),
            DMA((8,)),
            DMA((8, 3)),
            DMA((8,)),
            DMA((8, 2)),
            DMA((60,)),
            DMA((NY,)),
            DMA((NZ,)),
            DMA((GATHER_SENDS,)),
            DMA((2, 2)),
            DMA((2,)),
            DMA((4, 2)),
            DMA((4,)),
            DMA((4, 2)),
            DMA((NZ,)),
            DMA((NZ,)),
            DMA((8,)),
            DMA((NZ,)),
            DMA((2, 8)),
            DMA((8,)),
        ],
        compiler_params=pltpu.CompilerParams(
            collective_id=1, has_side_effects=True, vmem_limit_bytes=LIMIT
        ),
    )(normed, weight, targets, rf, vals, gain)


def body(hidden, norm_gain, head_weight, target_logits, valid_rows, parents, features):
    group_index = lax.axis_index("dp")
    group_rows = hidden.shape[0]
    gain = lax.dynamic_slice_in_dim(norm_gain, group_index * 1024, 1024).reshape(1, 1024)
    live = (valid_rows == 1).astype(F32).reshape(1, 128)
    tree_rows = jnp.arange(group_rows, dtype=jnp.int32) // TREE * TREE + parents
    chosen = jnp.take(features, tree_rows, axis=0).reshape(2, 64, 768)
    normed, vals, rf, parent_features = spread_call(hidden, live, gain, chosen)
    share, grad = main_call(normed, head_weight, target_logits, rf, vals, gain)
    grad_joining = lax.dot_general(
        grad.reshape(1024, 1024),
        parent_features.reshape(1024, 768),
        (((0,), (0,)), ((), ())),
        preferred_element_type=F32,
    )
    return (share, grad_joining)


def solution(mesh):
    placed = (
        P("dp", "vocab"),
        P(),
        P("vocab", "dp"),
        P("dp", "vocab"),
        P("dp"),
        P("dp"),
        P("dp", "vocab"),
    )
    return jax.shard_map(
        body,
        mesh=mesh,
        in_specs=placed,
        out_specs=(P("vocab", "dp"), P("dp", "vocab")),
        check_vma=False,
    )
```

time: 594 us -> 182 us (0.31)
  waiting for transfers between devices: 358 us -> 0 us
  Pallas kernels: 0 us -> 170 us
  blocking collectives: 168 us -> 0 us
  matrix products: 22.2 us -> 5.15 us
  between operations: 13.9 us -> 0.69 us
  other arithmetic: 14.6 us -> 2.65 us
  local copies, waits for them, and re-layouts: 9.89 us -> 2.88 us
    pallas_call x0 -> x2, Pallas kernels: none -> 170 us  [the longest x1 126 us: main_call(): pl.pallas_call(main_kernel, out_shape=(jax.ShapeDtypeStruct((32, 1024), B...]
    psum x1 -> x0, waiting for transfers between devices: 161 us -> none  [body(): normed_grad = lax.psum(partial_grad, 'vocab')]
    all_gather x3 -> x0, waiting for transfers between devices: 121 us -> none  [the longest x1 79.7 us: body(): whole_rows = lax.all_gather(hidden, 'vocab', axis=1, tiled=True)]
    psum x3 -> x0, blocking collectives: 100 us -> none  [the longest x1 74.1 us: body(): lax.psum((jnp.sum(jnp.exp(logits - draft_max[:, None]), axis=1), jnp.sum(...]
    pmax x1 -> x0, blocking collectives: 68.2 us -> none  [body(): lax.pmax((jnp.max(logits, axis=1), jnp.max(targets, axis=1)), 'vocab')]
    reduce_scatter x1 -> x0, waiting for transfers between devices: 50.2 us -> none  [body(): lax.psum_scatter(row_logits(normed, head_weight), 'dp', scatter_dimension...]
    all_to_all x1 -> x0, waiting for transfers between devices: 25.8 us -> none  [body(): lax.all_to_all(whole_rows, 'dp', split_axis=1, concat_axis=0, tiled=True)]
    dot_general x3 -> x1, matrix products: 22.2 us -> 5.15 us  [body(): lax.dot_general(grad.reshape(1024, 1024), parent_features.reshape(1024, 7...]
  transfers between devices with their start and end apart: 6 -> 0, of which waited for: 6 -> 0; matrix products, arithmetic and copies ran while one was open for 2% -> 0% of each run, Pallas kernels for 0% -> 0%
where the time goes in v1:
time: 182 us
  Pallas kernels  170 us (93%)
  matrix products  5.15 us (3%)
  local copies, waits for them, and re-layouts  2.88 us (2%)
  other arithmetic  2.65 us (1%)
    pallas_call x1, Pallas kernels, main_call(): pl.pallas_call(main_kernel, out_shape=(jax.ShapeDtypeStruct((32, 1024), B...  126 us
    pallas_call x1, Pallas kernels, spread_call(): pl.pallas_call(spread_kernel, out_shape=(jax.ShapeDtypeStruct((1024, 1024...  43.8 us
    dot_general x1, matrix products, body(): lax.dot_general(grad.reshape(1024, 1024), parent_features.reshape(1024, 7...  5.15 us

profile of v1, /device:TPU:24, one launch (start us, length us, event | category | flops | bytes accessed | tf_op | source)
XLA Modules:
  0.0 181.5 jit_solution(13518092635122959039)
XLA Ops:
  0.6 0.0 copy-start
  0.7 1.2 fusion.2.live
  1.9 0.7 compare_and_fusion
  2.5 0.1 broadcast_in_dim.14
  2.6 1.3 dynamic_slice.3
  3.9 0.0 copy-done
  3.9 0.9 gather_fusion
  4.8 0.8 broadcast_select_fusion.feat
  5.5 43.8 %shard_map.86 = (bf16[1024,1024]{1,0:T(8,128)(2,1)}, bf16[32,1024]{1,0:T(8,128)(2,1)}, f32[8,8,128]{2,1,0:T(8,128)}, bf16[8,2,64,768]{3,2,1,0:T(8,128)(2,1)}) custom-call(bf16[128,256]{1,0:T(8,128)(2,1)} %hid.1, f32[1,128]{1,0:T(1,128)} %fusion.2.live, f32[1,1024]{1,0:T(1,128)} %bitcast.9, bf16[2,64,768]{2,1,0:T(8,128)(2,1)} %broadcast_select_fusion.feat), custom_call_target="tpu_custom_call" | custom-call | tf_op jit(solution)/shard_map/pallas_call | solution.py:600
  49.4 0.0 copy-start.2
  49.4 126.3 %shard_map.87 = (bf16[32,1024]{1,0:T(8,128)(2,1)}, bf16[8,4,32,1024]{3,2,1,0:T(8,128)(2,1)}) custom-call(bf16[1024,1024]{1,0:T(8,128)(2,1)} %get-tuple-element.8.normed, bf16[2048,1024]{1,0:T(8,128)(2,1)} %weight.1, bf16[128,2048]{1,0:T(8,128)(2,1)} %targets.1, f32[8,8,128]{2,1,0:T(8,128)} %get-tuple-element.9.rf, bf16[32,1024]{1,0:T(8,128)(2,1)} %get-tuple-element.10.vals, ...), custom_call_target="tpu_custom_call" | custom-call | tf_op jit(solution)/shard_map/pallas_call | solution.py:636
  175.7 0.0 copy-done.2
  175.7 0.0 copy-start.1
  175.8 5.1 %fusion.3 = f32[1024,768]{1,0:T(8,128)} fusion(bf16[1024,1024]{1,0:T(8,128)(2,1)} %bitcast.11, bf16[1024,768]{1,0:T(8,128)(2,1)S(1)} %bitcast.12), kind=kOutput, calls=%fused_computation.13 | convolution fusion | flops 1610612736 | bytes 6815744 | tf_op jit(solution)/shard_map/dot_general | solution.py:701
  180.9 0.0 copy-done.1
  180.9 0.6 copy.10
  (1 shorter events, 0.0 us)
Async XLA Ops:
  0.6 3.3 %copy-start = (bf16[128,768]{1,0:T(8,128)(2,1)S(1)}, bf16[128,768]{1,0:T(8,128)(2,1)}, u32[]{:S(2)}) copy-start(bf16[128,768]{1,0:T(8,128)(2,1)} %param.13) | copy-start | bytes 589828
  49.4 126.3 %copy-start.2 = (bf16[8,2,64,768]{3,2,1,0:T(8,128)(2,1)S(1)}, bf16[8,2,64,768]{3,2,1,0:T(8,128)(2,1)}, u32[]{:S(2)}) copy-start(bf16[8,2,64,768]{3,2,1,0:T(8,128)(2,1)} %get-tuple-element.13) | copy-start | bytes 4718596
  175.7 5.2 %copy-start.1 = (bf16[32,1024]{1,0:T(8,128)(2,1)S(1)}, bf16[32,1024]{1,0:T(8,128)(2,1)}, u32[]{:S(2)}) copy-start(bf16[32,1024]{1,0:T(8,128)(2,1)} %get-tuple-element.18) | copy-start | bytes 196612

commit v2 on v0

v2 whole, which is shorter than its diff:
```python
import contextlib

import jax
import jax.numpy as jnp
from jax import lax
from jax.experimental import pallas as pl
from jax.experimental.pallas import tpu as pltpu
from jax.sharding import PartitionSpec as P

TREE = 64
NX, NC, NY, NZ = 4, 2, 4, 8
F32, BF16 = jnp.float32, jnp.bfloat16
DMA = pltpu.SemaphoreType.DMA


def remote(src, dst, send_sem, recv_sem, device):
    return pltpu.make_async_remote_copy(
        src_ref=src,
        dst_ref=dst,
        send_sem=send_sem,
        recv_sem=recv_sem,
        device_id=device,
        device_id_type=pl.DeviceIdType.MESH,
    )


def phase(name):
    return contextlib.nullcontext()


class Place:
    def __init__(self):
        self.g = lax.axis_index("dp")
        self.v = lax.axis_index("vocab")
        self.x, self.c = self.g // NC, self.g % NC
        self.z, self.y = self.v // NY, self.v % NY

    def dp(self, i):
        return (i, self.v)

    def at_x(self, x):
        return (x * NC + self.c, self.v)

    def partner(self):
        return (self.x * NC + 1 - self.c, self.v)

    def at_y(self, y):
        return (self.g, self.z * NY + y)

    def at_z(self, z):
        return (self.g, z * NY + self.y)


def greet(peers):
    barrier = pltpu.get_barrier_semaphore()
    for peer in peers:
        pl.semaphore_signal(
            barrier, inc=1, device_id=peer, device_id_type=pl.DeviceIdType.MESH
        )
    pl.semaphore_wait(barrier, len(peers))


class Sender:
    def __init__(self, sems):
        self.sems, self.used, self.copies = sems, 0, []

    def __call__(self, src, dst, recv_sem, device):
        assert self.used < self.sems.shape[0]
        copy = remote(src, dst, self.sems.at[self.used], recv_sem, device)
        self.used += 1
        copy.start()
        self.copies.append(copy)

    def drain(self):
        for copy in self.copies:
            copy.wait_send()


def arrived(dst, recv_sem, device, any_sem):
    remote(dst, dst, any_sem, recv_sem, device).wait_recv()


class Gather:
    def __init__(self, at, buf, send, near, far, pair):
        self.at, self.buf, self.send = at, buf, send
        self.near, self.far, self.pair = near, far, pair

    def slot(self, step, core):
        return ((self.at.x + step) % NX) * NC + core

    def start(self, half):
        at, buf = self.at, self.buf
        mine = buf.at[at.g, half]
        self.send(mine, mine, self.near.at[0, half], at.at_x((at.x + 1) % NX))
        self.send(mine, mine, self.near.at[1, half], at.at_x((at.x + 3) % NX))
        self.send(mine, mine, self.pair.at[0, half], at.partner())

    def middle(self):
        at, buf = self.at, self.buf
        for half in range(2):
            for side, step in ((0, 3), (1, 1)):
                block = buf.at[self.slot(step, at.c), half]
                arrived(block, self.near.at[side, half], at.partner(), self.near.at[side, half])
                if half == side:
                    onward = at.at_x((at.x + (1 if side == 0 else 3)) % NX)
                    self.send(block, block, self.far.at[half], onward)
                self.send(block, block, self.pair.at[step, half], at.partner())

    def last(self):
        at, buf = self.at, self.buf
        for half in range(2):
            block = buf.at[self.slot(2, at.c), half]
            arrived(block, self.far.at[half], at.partner(), self.far.at[half])
            self.send(block, block, self.pair.at[2, half], at.partner())

    def paired(self, step):
        at = self.at
        for half in range(2):
            block = self.buf.at[self.slot(step, 1 - at.c), half]
            arrived(block, self.pair.at[step, half], at.partner(), self.pair.at[step, half])


GATHER_SENDS = 14


def row_tile(column):
    return jnp.transpose(jnp.broadcast_to(column, (128, 128)))[0:8]


def column_tile(row):
    return jnp.transpose(jnp.broadcast_to(row, (128, 128)))


def stack_rows(*rows):
    index = lax.broadcasted_iota(jnp.int32, (8, 128), 0)
    tile = jnp.zeros((8, 128), F32)
    for k, row in enumerate(rows):
        tile = jnp.where(index == k, row, tile)
    return tile


def kernel(
    hid, valid, parents, feat, gains, weight_hbm, targets_hbm,
    share_out, grad_out, feat_out,
    weight, targets, zbuf, xall, normed, stat, cols, rf, fall, gain,
    pk, pr, sb, rl, fin, lg, tst, stat_y, stat_z, gbuf, pf, ysb, yrl, yfin,
    qs, zrs, tot, vscr, rds, rdr, sscr,
    local_sems, send_sems, f_sems, zr, xs, xr, yr, y2, sr, fr,
    f_near, f_far, f_pair,
    pair_s, pair_r, sb_s, rl_r, fin_r,
    sty, stz, g_sems, g_near, g_far, g_pair,
    yrl_r, yfin_r, zs_s, zs_r, rd_r, a_z, a_y, a_y2, b_y, b_z,
):
    at = Place()
    x, c, y, z, g = at.x, at.c, at.y, at.z, at.g
    up_z, down_z = at.at_z((z + 1) % NZ), at.at_z((z + NZ - 1) % NZ)
    up_y, down_y = at.at_y((y + 1) % NY), at.at_y((y + 3) % NY)
    zz, zr_ = z // 4, z % 4

    load_weight = pltpu.make_async_copy(weight_hbm, weight, local_sems.at[0])
    load_targets = pltpu.make_async_copy(targets_hbm, targets, local_sems.at[1])
    load_weight.start()
    load_targets.start()

    with phase("A_feat"):
        live = (valid[...] == 1).astype(F32)
        row = lax.broadcasted_iota(jnp.int32, (128, 128), 0)
        lane = lax.broadcasted_iota(jnp.int32, (128, 128), 1)
        wanted = column_tile(parents[...].astype(F32)).astype(jnp.int32) + row // TREE * TREE
        pick = (lane == wanted).astype(BF16)
        chosen = jnp.dot(pick, feat[...], preferred_element_type=F32).astype(BF16)
        source = 32 * (row // 8 % 4) + 8 * (row // 32) + row % 8
        shuffle = (lane == source).astype(BF16)
        chosen = jnp.dot(shuffle, chosen, preferred_element_type=F32).astype(BF16)
        fall[g, 0] = chosen[:64]
        fall[g, 1] = chosen[64:]
        own_gain = gains[g]
        gain[...] = jnp.concatenate([own_gain[k : k + 1] for k in range(8)], axis=1)

    with phase("A_greet"):
        greet(
            [at.dp((g + k) % 8) for k in range(1, 8)]
            + [at.at_z((z + k) % NZ) for k in range(1, NZ)]
            + [at.at_y((y + k) % NY) for k in range(1, NY)]
        )
    send = Sender(send_sems)
    spread = Gather(at, fall, Sender(f_sems), f_near, f_far, f_pair)

    def to_slice(src, j):
        @pl.when(j != g)
        def _():
            remote(src, xall.at[y, g], xs.at[j], xr.at[g], at.dp(j)).start()

        @pl.when(j == g)
        def _():
            pltpu.make_async_copy(src, xall.at[y, g], xs.at[j]).start()

    with phase("A_z"):
        for step in range(5):
            low, high = (z + NZ - step) % NZ, (z + step) % NZ
            if step > 0:
                arrived(zbuf.at[low], zr.at[low], up_z, zr.at[low])
            src = hid if step == 0 else zbuf.at[low]
            if step < 4:
                send(src, zbuf.at[low], zr.at[low], up_z)
            if step == 0:
                send(hid, zbuf.at[high], zr.at[high], down_z)
            to_slice(src, low)
            if 0 < step < 4:
                arrived(zbuf.at[high], zr.at[high], up_z, zr.at[high])
                if step < 3:
                    send(zbuf.at[high], zbuf.at[high], zr.at[high], down_z)
                to_slice(zbuf.at[high], high)

    with phase("A_stat"):
        squares = jnp.square(hid[...].astype(F32))
        for k in range(1, NZ):
            squares = squares + jnp.square(zbuf[(z + k) % NZ].astype(F32))
        stat[y] = row_tile(jnp.sum(squares, axis=1, keepdims=True))
        for k in range(1, NY):
            send(stat.at[y], stat.at[y], sr.at[y], at.at_y((y + k) % NY))

    with phase("A_ysend"):
        for i in range(8):
            block = xall.at[y, i]

            @pl.when(g != i)
            def _():
                arrived(block, xr.at[i], up_y, xr.at[i])

            @pl.when(g == i)
            def _():
                pltpu.make_async_copy(hid, block, xs.at[i]).wait()

            send(block, block, yr.at[0, i], up_y)
            send(block, block, yr.at[1, i], down_y)
        for half in range(2):
            spread.start(half)

    with phase("A_rf"):
        total = stat[y]
        for k in range(1, NY):
            other = (y + k) % NY
            arrived(stat.at[other], sr.at[other], up_y, sr.at[other])
            total = total + stat[other]
        factor = lax.rsqrt(total / (1024.0 * 8) + 1e-05)
        rf[g] = stack_rows(factor[0:1], live)
        for k in range(1, 8):
            send(rf.at[g], rf.at[g], fr.at[g], at.dp((g + k) % 8))

    with phase("A_yrelay"):
        for i in range(8):
            for side, step in ((0, 3), (1, 1)):
                block = xall.at[(y + step) % NY, i]
                arrived(block, yr.at[side, i], up_y, yr.at[side, i])
                if (i < 4) == (side == 0):
                    send(block, block, y2.at[i], up_y if side == 0 else down_y)
    with phase("A_featmid"):
        spread.middle()
        for k in range(1, 8):
            other = (g + k) % 8
            arrived(rf.at[other], fr.at[other], up_y, fr.at[other])
        for i in range(8):
            cols[i] = column_tile(rf[i, 0:1])
    with phase("A_yfar"):
        for i in range(8):
            block = xall.at[(y + 2) % NY, i]
            arrived(block, y2.at[i], up_y, y2.at[i])

    with phase("A_norm"):

        @pl.loop(0, 8)
        def _(i):
            scale = cols[i]
            scale = jnp.concatenate([scale, scale], axis=1)
            rows = pl.ds(pl.multiple_of(i * 128, 128), 128)
            for part in range(NY):
                columns = slice(part * 256, part * 256 + 256)
                values = xall[part, i].astype(F32)
                normed[rows, columns] = (values * scale * gain[:, columns]).astype(BF16)

        load_weight.wait()
        load_targets.wait()

    def multiply(t):
        tile = pl.ds(pl.multiple_of(t * 256, 256), 256)
        for d in range(NX):
            part = lax.dot_general(
                normed[d * 256 : d * 256 + 256, :],
                weight[tile, :],
                (((1,), (1,)), ((), ())),
                preferred_element_type=F32,
            )
            pk[t, 0, d] = part[:128]
            pk[t, 1, d] = part[128:]
        remote(
            pk.at[t, 1 - c], pr.at[t], pair_s.at[t], pair_r.at[t], at.partner()
        ).start()

    def hops(t):
        way = 1 + 2 * (t % 2)
        return (x + way) % NX, (x + 4 - way) % NX

    def direct(t):
        ahead, back = hops(t)
        return (
            remote(sb.at[t, 0], rl.at[t], sb_s.at[t, 0], rl_r.at[t], at.at_x(ahead)),
            remote(sb.at[t, 1], fin.at[t, 0], sb_s.at[t, 1], fin_r.at[t, 0], at.at_x(back)),
        )

    def onward(t):
        ahead, _ = hops(t)
        return remote(sb.at[t, 2], fin.at[t, 1], sb_s.at[t, 2], fin_r.at[t, 1], at.at_x(ahead))

    def encode(t, k, value):
        top = jnp.max(jnp.abs(value), axis=0, keepdims=True)
        step = (120.0 / jnp.maximum(top, 1e-30)).astype(BF16)
        sb[t, k, 128:] = jnp.broadcast_to(step, (16, 256))
        step = sb[t, k, 128:].astype(F32)[0:1]
        sb[t, k, :128] = jnp.exp2(value * step).astype(BF16)

    def decode(block):
        step = block[128:].astype(F32)[0:1]
        return jnp.log2(block[:128].astype(F32)) * (1.0 / step)

    def pair_sum(t):
        ahead, back = hops(t)
        far = (x + 2) % NX
        arrived(pr.at[t], pair_r.at[t], at.partner(), pair_r.at[t])
        encode(t, 0, pk[t, c, far] + pr[t, far])
        encode(t, 1, pk[t, c, back] + pr[t, back])
        for copy in direct(t):
            copy.start()

    def relay(t):
        ahead, _ = hops(t)
        arrived(rl.at[t], rl_r.at[t], at.partner(), rl_r.at[t])
        encode(t, 2, pk[t, c, ahead] + pr[t, ahead] + decode(rl.at[t]))
        onward(t).start()

    def finish(t):
        for k in range(2):
            arrived(fin.at[t, k], fin_r.at[t, k], at.partner(), fin_r.at[t, k])
        lg[t] = pk[t, c, x] + pr[t, x] + decode(fin.at[t, 0]) + decode(fin.at[t, 1])

    with phase("B_fwd"):

        @pl.loop(0, 12)
        def _(t):
            @pl.when(t < 8)
            def _():
                multiply(t)

            @pl.when((t >= 1) & (t < 9))
            def _():
                pair_sum(t - 1)

            @pl.when(t >= 4)
            def _():
                relay(t - 4)

    with phase("B_target"):
        top = jnp.max(targets[...].astype(F32), axis=1, keepdims=True)
        part = jnp.zeros((128, 256), F32)
        for k in range(8):
            part = part + jnp.exp(targets[:, k * 256 : k * 256 + 256].astype(F32) - top)
        tst[...] = stack_rows(
            jnp.zeros((1, 128), F32),
            jnp.zeros((1, 128), F32),
            row_tile(top)[0:1],
            row_tile(jnp.sum(part, axis=1, keepdims=True))[0:1],
        )

    with phase("B_fin"):

        @pl.loop(0, 8)
        def _(t):
            finish(t)

    with phase("B_stat"):
        top = lg[0]
        for t in range(1, 8):
            top = jnp.maximum(top, lg[t])
        top = jnp.max(top, axis=1, keepdims=True)
        part = jnp.zeros((128, 256), F32)
        for t in range(8):
            part = part + jnp.exp(lg[t] - top)
        stat_y[y] = stack_rows(
            row_tile(top)[0:1],
            row_tile(jnp.sum(part, axis=1, keepdims=True))[0:1],
            tst[2:3],
            tst[3:4],
        )
        for k in range(1, NY):
            send(stat_y.at[y], stat_y.at[y], sty.at[y], at.at_y((y + k) % NY))

    def combine(tiles):
        out = []
        for k in (0, 2):
            m = tiles[0][k : k + 1]
            for tile in tiles[1:]:
                m = jnp.maximum(m, tile[k : k + 1])
            s = jnp.zeros((1, 128), F32)
            for tile in tiles:
                s = s + tile[k + 1 : k + 2] * jnp.exp(tile[k : k + 1] - m)
            out += [m, s]
        return out

    with phase("B_staty"):
        tiles = [stat_y[y]]
        for k in range(1, NY):
            other = (y + k) % NY
            arrived(stat_y.at[other], sty.at[other], up_y, sty.at[other])
            tiles.append(stat_y[other])
        stat_z[z] = stack_rows(*combine(tiles))
        for k in range(1, NZ):
            send(stat_z.at[z], stat_z.at[z], stz.at[z], at.at_z((z + k) % NZ))
    with phase("B_statz"):
        tiles = [stat_z[z]]
        for k in range(1, NZ):
            other = (z + k) % NZ
            arrived(stat_z.at[other], stz.at[other], up_y, stz.at[other])
            tiles.append(stat_z[other])
        draft_max, draft_sum, target_max, target_sum = combine(tiles)
        count = jnp.zeros((1, 128), F32)
        for i in range(8):
            count = count + rf[i, 1:2]
        count = jnp.sum(count, axis=1, keepdims=True)
        scale = 1048576.0 * rf[g][1:2] / count
        wide = lambda row: jnp.concatenate([column_tile(row)] * 2, axis=1)
        draft_top, target_top = wide(draft_max), wide(target_max)
        draft_scale, target_scale = wide(1.0 / draft_sum), wide(1.0 / target_sum)
        scale = wide(scale)

    gather = Gather(at, gbuf, Sender(g_sems), g_near, g_far, g_pair)
    with phase("B_G"):
        for t in range(8):
            draft = jnp.exp(lg[t] - draft_top) * draft_scale
            target = (
                jnp.exp(targets[:, t * 256 : t * 256 + 256].astype(F32) - target_top)
                * target_scale
            )
            column = (t % 4) * 256
            gbuf[g, t // 4, :, column : column + 256] = (scale * (draft - target)).astype(BF16)
            if t % 4 == 3:
                gather.start(t // 4)

    with phase("B_featlast"):
        spread.last()
        for step in range(4):
            spread.paired(step)

        @pl.loop(0, NZ)
        def _(owner):
            high, low = owner // 4, owner % 4
            rows = pl.ds(pl.multiple_of((low % 2) * 32, 32), 32)
            blocks = [fall[2 * b + high, low // 2, rows, :].astype(F32) for b in range(4)]
            for k in range(NY):
                group = [block[8 * k : 8 * k + 8] for block in blocks]
                feat_out[owner, k] = jnp.concatenate(group, axis=0).astype(BF16)

    def backward(k, step):
        block = pl.ds(((x + step) % NX) * NC, 2)

        @pl.loop(0, 4)
        def _(n):
            columns = pl.ds(pl.multiple_of(n * 256, 256), 256)
            part = jnp.zeros((256, 256), F32)
            for half in range(2):
                part = part + jnp.dot(
                    gbuf[block, half].reshape(256, 1024),
                    weight[half * 1024 : half * 1024 + 1024, columns],
                    preferred_element_type=F32,
                )
            for which in range(2):
                for dest in range(NY):
                    row = which * 128 + dest * 32
                    pf[k, dest, which, :, columns] = part[row : row + 32]

    def y_first(k):
        way = 1 if k % 2 == 0 else 3
        ysb[k, 0] = pf[k, (y + 2) % NY].astype(BF16)
        send(ysb.at[k, 0], yrl.at[k], yrl_r.at[k], at.at_y((y + way) % NY))
        ysb[k, 1] = pf[k, (y + 4 - way) % NY].astype(BF16)
        send(ysb.at[k, 1], yfin.at[k, 0], yfin_r.at[k, 0], at.at_y((y + 4 - way) % NY))

    def y_second(k):
        way = 1 if k % 2 == 0 else 3
        arrived(yrl.at[k], yrl_r.at[k], up_y, yrl_r.at[k])
        ysb[k, 2] = (pf[k, (y + way) % NY] + yrl[k].astype(F32)).astype(BF16)
        send(ysb.at[k, 2], yfin.at[k, 1], yfin_r.at[k, 1], at.at_y((y + way) % NY))

    steps = (0, 3, 1, 2)

    def z_send(k, dest):
        return remote(
            qs.at[k, dest], zrs.at[k, z], zs_s.at[k, dest], zs_r.at[k, z], at.at_z(dest)
        )

    def y_third(k):
        for j in range(2):
            arrived(yfin.at[k, j], yfin_r.at[k, j], up_y, yfin_r.at[k, j])
        value = pf[k, y] + yfin[k, 0].astype(F32) + yfin[k, 1].astype(F32)
        for owner in range(NZ):
            row = 8 * (owner % 4)
            qs[k, owner] = value[owner // 4, row : row + 8]
        for shift in (4, 3, 5, 2, 6, 1, 7):
            z_send(k, (z + shift) % NZ).start()

    with phase("B_p0"):
        gather.paired(0)
    with phase("B_bw0"):
        backward(0, 0)
        y_first(0)
    with phase("B_mid"):
        gather.middle()
        gather.paired(3)
    with phase("B_bw1"):
        backward(1, 3)
        y_first(1)
        y_second(0)
    with phase("B_bw2"):
        gather.paired(1)
        backward(2, 1)
        y_first(2)
        y_second(1)
        y_third(0)
    with phase("B_last"):
        gather.last()
        gather.paired(2)
    with phase("B_bw3"):
        backward(3, 2)
        y_first(3)
        y_second(2)
        y_third(1)
    with phase("B_ytail"):
        y_second(3)
        y_third(2)
        y_third(3)

    with phase("C_sum"):
        for b in range(4):
            for part in range(NY):
                vscr[b, :, part * 256 : part * 256 + 256] = xall[
                    part, 2 * b + zz, pl.ds(pl.multiple_of(y * 32, 32), 32), :
                ].astype(F32)
        eight = pl.ds(pl.multiple_of(zr_ * 8, 8), 8)
        values = jnp.concatenate([vscr[b, eight, :] for b in range(4)], axis=0)
        eight = pl.ds(pl.multiple_of(y * 32 + zr_ * 8, 8), 8)
        factor = jnp.concatenate([cols[2 * b + zz, eight, :] for b in range(4)], axis=0)
        for k in range(4):
            total = qs[k, z]
            for j in range(1, NZ):
                other = (z + j) % NZ
                arrived(zrs.at[k, other], zs_r.at[k, other], up_y, zs_r.at[k, other])
                total = total + zrs[k, other]
            tot[(x + steps[k]) % NX] = total
    with phase("C_dot"):
        total = tot[...].reshape(32, 1024)
        dot = jnp.sum(gain[...] * values * total, axis=1, keepdims=True)
        dot = jnp.broadcast_to(dot, (32, 128))
        rds[...] = dot
        for k in range(1, 8):
            send(rds, rdr.at[g], rd_r.at[g], at.dp((g + k) % 8))
        for k in range(1, 8):
            other = (g + k) % 8
            arrived(rdr.at[other], rd_r.at[other], up_y, rd_r.at[other])
            dot = dot + rdr[other]
        pull = factor * factor * factor * dot / (1024.0 * 8)
        broad = lambda tile: jnp.concatenate([tile] * 8, axis=1)
        grad = (broad(factor) * gain[...] * total - values * broad(pull)).astype(BF16)
        grad_out[z, y] = grad

    left, right = slice(0, SPLIT), slice(SPLIT, 1024)
    order = []

    def to_y(block_z):
        k = len(order)
        block = grad_out.at[block_z, y, :, left]
        send(block, block, a_y.at[0, k], up_y)
        send(block, block, a_y.at[1, k], down_y)
        order.append(block_z)

    done = [0]

    def pass_y(count):
        while done[0] < count:
            k = done[0]
            for side, step in ((0, 3), (1, 1)):
                block = grad_out.at[order[k], (y + step) % NY, :, left]
                arrived(block, a_y.at[side, k], up_y, a_y.at[side, k])
                if k % 2 == side:
                    send(block, block, a_y2.at[k], up_y if side == 0 else down_y)
            done[0] += 1

    with phase("C_ag"):
        mine = grad_out.at[z, y, :, left]
        send(mine, mine, a_z.at[z], up_z)
        send(mine, mine, a_z.at[z], down_z)
        mine = grad_out.at[z, y, :, right]
        for k in range(1, NY):
            send(mine, mine, b_y.at[y], at.at_y((y + k) % NY))
        to_y(z)
        for k in range(1, NY):
            other = (y + k) % NY
            block = grad_out.at[z, other, :, right]
            arrived(block, b_y.at[other], up_y, b_y.at[other])
        mine = grad_out.at[z, :, :, right]
        send(mine, mine, b_z.at[z], up_z)
        send(mine, mine, b_z.at[z], down_z)
        for step in range(1, 5):
            low, high = (z + NZ - step) % NZ, (z + step) % NZ
            for sems, pick in ((a_z, lambda i: grad_out.at[i, y, :, left]), (b_z, lambda i: grad_out.at[i, :, :, right])):
                arrived(pick(low), sems.at[low], up_z, sems.at[low])
                if step < 4:
                    send(pick(low), pick(low), sems.at[low], up_z)
                if step < 4:
                    arrived(pick(high), sems.at[high], up_z, sems.at[high])
                    if step < 3:
                        send(pick(high), pick(high), sems.at[high], down_z)
                if sems is a_z:
                    to_y(low)
                    if step < 4:
                        to_y(high)
                    pass_y(max(0, 2 * step - 1))
        pass_y(8)
    with phase("C_agfar"):
        for k in range(8):
            block = grad_out.at[order[k], (y + 2) % NY, :, left]
            arrived(block, a_y2.at[k], up_y, a_y2.at[k])

    with phase("C_share"):
        for k in range(4):
            sscr[k] = grad_out[4 * (z % 2) + k, y].astype(F32)
        eight = pl.ds(pl.multiple_of((z // 2) * 8, 8), 8)
        share_out[...] = jnp.concatenate([sscr[k, eight, :] for k in range(4)], axis=0).astype(BF16)

    with phase("C_drain"):

        @pl.loop(0, 8)
        def _(t):
            remote(
                pk.at[t, 1 - c], pr.at[t], pair_s.at[t], pair_r.at[t], at.partner()
            ).wait_send()
            for copy in direct(t):
                copy.wait_send()
            onward(t).wait_send()

        send.drain()
        spread.send.drain()
        gather.send.drain()
        for k in range(4):
            for j in range(1, NZ):
                z_send(k, (z + j) % NZ).wait_send()
        for j in range(8):

            @pl.when(g != j)
            def _():
                remote(hid, xall.at[y, g], xs.at[j], xr.at[g], at.dp(j)).wait_send()


SPLIT = 640
VMEM = pl.BlockSpec(memory_space=pltpu.VMEM)
HBM = pl.BlockSpec(memory_space=pl.ANY)
LIMIT = 60 * 1024 * 1024


def call(*operands):
    return pl.pallas_call(
        kernel,
        out_shape=(
            jax.ShapeDtypeStruct((32, 1024), BF16),
            jax.ShapeDtypeStruct((NZ, NY, 32, 1024), BF16),
            jax.ShapeDtypeStruct((NZ, NY, 32, 768), BF16),
        ),
        in_specs=[VMEM] * 5 + [HBM] * 2,
        out_specs=[VMEM] * 3,
        scratch_shapes=[
            pltpu.VMEM((2048, 1024), BF16),
            pltpu.VMEM((128, 2048), BF16),
            pltpu.VMEM((NZ, 128, 256), BF16),
            pltpu.VMEM((NY, 8, 128, 256), BF16),
            pltpu.VMEM((1024, 1024), BF16),
            pltpu.VMEM((NY, 8, 128), F32),
            pltpu.VMEM((8, 128, 128), F32),
            pltpu.VMEM((8, 8, 128), F32),
            pltpu.VMEM((8, 2, 64, 768), BF16),
            pltpu.VMEM((1, 1024), F32),
            pltpu.VMEM((8, 2, NX, 128, 256), F32),
            pltpu.VMEM((8, NX, 128, 256), F32),
            pltpu.VMEM((8, 3, 144, 256), BF16),
            pltpu.VMEM((8, 144, 256), BF16),
            pltpu.VMEM((8, 2, 144, 256), BF16),
            pltpu.VMEM((8, 128, 256), F32),
            pltpu.VMEM((8, 128), F32),
            pltpu.VMEM((NY, 8, 128), F32),
            pltpu.VMEM((NZ, 8, 128), F32),
            pltpu.VMEM((8, 2, 128, 1024), BF16),
            pltpu.VMEM((4, NY, 2, 32, 1024), F32),
            pltpu.VMEM((4, 3, 2, 32, 1024), BF16),
            pltpu.VMEM((4, 2, 32, 1024), BF16),
            pltpu.VMEM((4, 2, 2, 32, 1024), BF16),
            pltpu.VMEM((4, NZ, 8, 1024), F32),
            pltpu.VMEM((4, NZ, 8, 1024), F32),
            pltpu.VMEM((4, 8, 1024), F32),
            pltpu.VMEM((4, 32, 1024), F32),
            pltpu.VMEM((32, 128), F32),
            pltpu.VMEM((8, 32, 128), F32),
            pltpu.VMEM((4, 32, 1024), F32),
            DMA((2,)),
            DMA((112,)),
            DMA((GATHER_SENDS,)),
            DMA((NZ,)),
            DMA((8,)),
            DMA((8,)),
            DMA((2, 8)),
            DMA((8,)),
            DMA((NY,)),
            DMA((8,)),
            DMA((2, 2)),
            DMA((2,)),
            DMA((4, 2)),
            DMA((8,)),
            DMA((8,)),
            DMA((8, 3)),
            DMA((8,)),
            DMA((8, 2)),
            DMA((NY,)),
            DMA((NZ,)),
            DMA((GATHER_SENDS,)),
            DMA((2, 2)),
            DMA((2,)),
            DMA((4, 2)),
            DMA((4,)),
            DMA((4, 2)),
            DMA((4, NZ)),
            DMA((4, NZ)),
            DMA((8,)),
            DMA((NZ,)),
            DMA((2, 8)),
            DMA((8,)),
            DMA((NY,)),
            DMA((NZ,)),
        ],
        compiler_params=pltpu.CompilerParams(
            collective_id=0, has_side_effects=True, vmem_limit_bytes=LIMIT
        ),
    )(*operands)


def body(hidden, norm_gain, head_weight, target_logits, valid_rows, parents, features):
    share, grad, parent_features = call(
        hidden,
        valid_rows.reshape(1, 128),
        parents.reshape(1, 128),
        features,
        norm_gain.reshape(8, 8, 128),
        head_weight,
        target_logits,
    )
    grad_joining = lax.dot_general(
        grad.reshape(1024, 1024),
        parent_features.reshape(1024, 768),
        (((0,), (0,)), ((), ())),
        preferred_element_type=F32,
    )
    return (share, grad_joining)


def solution(mesh):
    placed = (
        P("dp", "vocab"),
        P(),
        P("vocab", "dp"),
        P("dp", "vocab"),
        P("dp"),
        P("dp"),
        P("dp", "vocab"),
    )
    return jax.shard_map(
        body,
        mesh=mesh,
        in_specs=placed,
        out_specs=(P("vocab", "dp"), P("dp", "vocab")),
        check_vma=False,
    )
```

time: 594 us -> 169 us (0.28)
  waiting for transfers between devices: 358 us -> 0 us
  blocking collectives: 168 us -> 0 us
  Pallas kernels: 0 us -> 162 us
  matrix products: 22.2 us -> 5.59 us
  other arithmetic: 14.6 us -> 0 us
  between operations: 13.9 us -> 0.65 us
  local copies, waits for them, and re-layouts: 9.89 us -> 0.63 us
    pallas_call x0 -> x1, Pallas kernels: none -> 162 us  [call(): pl.pallas_call(kernel, out_shape=(jax.ShapeDtypeStruct((32, 1024), BF16),...]
    psum x1 -> x0, waiting for transfers between devices: 161 us -> none  [body(): normed_grad = lax.psum(partial_grad, 'vocab')]
    all_gather x3 -> x0, waiting for transfers between devices: 121 us -> none  [the longest x1 79.7 us: body(): whole_rows = lax.all_gather(hidden, 'vocab', axis=1, tiled=True)]
    psum x3 -> x0, blocking collectives: 100 us -> none  [the longest x1 74.1 us: body(): lax.psum((jnp.sum(jnp.exp(logits - draft_max[:, None]), axis=1), jnp.sum(...]
    pmax x1 -> x0, blocking collectives: 68.2 us -> none  [body(): lax.pmax((jnp.max(logits, axis=1), jnp.max(targets, axis=1)), 'vocab')]
    reduce_scatter x1 -> x0, waiting for transfers between devices: 50.2 us -> none  [body(): lax.psum_scatter(row_logits(normed, head_weight), 'dp', scatter_dimension...]
    all_to_all x1 -> x0, waiting for transfers between devices: 25.8 us -> none  [body(): lax.all_to_all(whole_rows, 'dp', split_axis=1, concat_axis=0, tiled=True)]
    dot_general x3 -> x1, matrix products: 22.2 us -> 5.59 us  [body(): lax.dot_general(grad.reshape(1024, 1024), parent_features.reshape(1024, 7...]
  transfers between devices with their start and end apart: 6 -> 0, of which waited for: 6 -> 0; matrix products, arithmetic and copies ran while one was open for 2% -> 0% of each run, Pallas kernels for 0% -> 0%
where the time goes in v2:
time: 169 us
  Pallas kernels  162 us (96%)
  matrix products  5.59 us (3%)
    pallas_call x1, Pallas kernels, call(): pl.pallas_call(kernel, out_shape=(jax.ShapeDtypeStruct((32, 1024), BF16),...  162 us
    dot_general x1, matrix products, body(): lax.dot_general(grad.reshape(1024, 1024), parent_features.reshape(1024, 7...  5.59 us

profile of v2, /device:TPU:24, one launch (start us, length us, event | category | flops | bytes accessed | tf_op | source)
XLA Modules:
  0.0 168.7 jit_solution(8915839802666721261)
XLA Ops:
  0.6 161.9 %shard_map.86 = (bf16[32,1024]{1,0:T(8,128)(2,1)}, bf16[8,4,32,1024]{3,2,1,0:T(8,128)(2,1)}, bf16[8,4,32,768]{3,2,1,0:T(8,128)(2,1)}) custom-call(bf16[128,256]{1,0:T(8,128)(2,1)} %hid.1, s32[1,128]{1,0:T(1,128)} %bitcast.10, s32[1,128]{1,0:T(1,128)} %bitcast.11, bf16[128,768]{1,0:T(8,128)(2,1)} %feat.1, f32[8,8,128]{2,1,0:T(8,128)} %bitcast.9, ...), custom_call_target="tpu_custom_call" | custom-call | tf_op jit(solution)/shard_map/pallas_call | solution.py:669
  162.5 0.0 copy-start
  162.5 5.6 %convolution_bitcast_fusion = f32[1024,768]{1,0:T(8,128)} fusion(bf16[8,4,32,1024]{3,2,1,0:T(8,128)(2,1)} %get-tuple-element.6, bf16[8,4,32,768]{3,2,1,0:T(8,128)(2,1)} %get-tuple-element.7), kind=kOutput, calls=%fused_computation | convolution fusion | flops 1610612736 | bytes 6815744 | tf_op jit(solution)/shard_map/dot_general | solution.py:761
  168.1 0.0 copy-done
  168.1 0.6 copy.11
Async XLA Ops:
  162.5 5.6 %copy-start = (bf16[32,1024]{1,0:T(8,128)(2,1)S(1)}, bf16[32,1024]{1,0:T(8,128)(2,1)}, u32[]{:S(2)}) copy-start(bf16[32,1024]{1,0:T(8,128)(2,1)} %get-tuple-element.10) | copy-start | bytes 196612

commit v3 on v2

v3 whole, which is shorter than its diff:
```python
import contextlib

import jax
import jax.numpy as jnp
from jax import lax
from jax.experimental import pallas as pl
from jax.experimental.pallas import tpu as pltpu
from jax.sharding import PartitionSpec as P

TREE = 64
NX, NC, NY, NZ = 4, 2, 4, 8
F32, BF16 = jnp.float32, jnp.bfloat16
DMA = pltpu.SemaphoreType.DMA


def remote(src, dst, send_sem, recv_sem, device):
    return pltpu.make_async_remote_copy(
        src_ref=src,
        dst_ref=dst,
        send_sem=send_sem,
        recv_sem=recv_sem,
        device_id=device,
        device_id_type=pl.DeviceIdType.MESH,
    )


def phase(name):
    return contextlib.nullcontext()


class Place:
    def __init__(self):
        self.g = lax.axis_index("dp")
        self.v = lax.axis_index("vocab")
        self.x, self.c = self.g // NC, self.g % NC
        self.z, self.y = self.v // NY, self.v % NY

    def dp(self, i):
        return (i, self.v)

    def at_x(self, x):
        return (x * NC + self.c, self.v)

    def partner(self):
        return (self.x * NC + 1 - self.c, self.v)

    def at_y(self, y):
        return (self.g, self.z * NY + y)

    def at_z(self, z):
        return (self.g, z * NY + self.y)


class Sender:
    def __init__(self, sems):
        self.sems, self.used, self.copies = sems, 0, []

    def __call__(self, src, dst, recv_sem, device):
        assert self.used < self.sems.shape[0]
        copy = remote(src, dst, self.sems.at[self.used], recv_sem, device)
        self.used += 1
        copy.start()
        self.copies.append(copy)

    def drain(self):
        for copy in self.copies:
            copy.wait_send()


def arrived(dst, recv_sem, device, any_sem):
    remote(dst, dst, any_sem, recv_sem, device).wait_recv()


class Gather:
    def __init__(self, at, buf, send, near, far, pair):
        self.at, self.buf, self.send = at, buf, send
        self.near, self.far, self.pair = near, far, pair

    def slot(self, step, core):
        return ((self.at.x + step) % NX) * NC + core

    def start(self):
        at, buf = self.at, self.buf
        up, down = at.at_x((at.x + 1) % NX), at.at_x((at.x + 3) % NX)
        for k in range(2):
            for side, half, device in ((0, k, up), (1, 1 - k, down)):
                mine = buf.at[at.g, half]
                self.send(mine, mine, self.near.at[side, half], device)
            mine = buf.at[at.g, k]
            self.send(mine, mine, self.pair.at[0, k], at.partner())

    def middle(self, first):
        at, buf = self.at, self.buf
        for side, step in ((0, 3), (1, 1)):
            half = side if first else 1 - side
            block = buf.at[self.slot(step, at.c), half]
            arrived(block, self.near.at[side, half], at.partner(), self.near.at[side, half])
            if first:
                onward = at.at_x((at.x + (1 if side == 0 else 3)) % NX)
                self.send(block, block, self.far.at[half], onward)
            self.send(block, block, self.pair.at[step, half], at.partner())

    def last(self):
        at, buf = self.at, self.buf
        for half in range(2):
            block = buf.at[self.slot(2, at.c), half]
            arrived(block, self.far.at[half], at.partner(), self.far.at[half])
            self.send(block, block, self.pair.at[2, half], at.partner())

    def paired(self, step):
        at = self.at
        for half in range(2):
            block = self.buf.at[self.slot(step, 1 - at.c), half]
            arrived(block, self.pair.at[step, half], at.partner(), self.pair.at[step, half])


GATHER_SENDS = 14


def row_tile(column):
    return jnp.transpose(jnp.broadcast_to(column, (128, 128)))[0:8]


def column_tile(row):
    return jnp.transpose(jnp.broadcast_to(row, (128, 128)))


def stack_rows(*rows):
    index = lax.broadcasted_iota(jnp.int32, (8, 128), 0)
    tile = jnp.zeros((8, 128), F32)
    for k, row in enumerate(rows):
        tile = jnp.where(index == k, row, tile)
    return tile


def kernel(
    hid, valid, parents, feat, gains, weight_hbm, targets_hbm,
    share_out, grad_out, fall,
    weight, targets, zbuf, xall, normed, stat, cols, scols, rf, srow, gain,
    pk, pr, sb, rl, fin, lg, tst, stat_v, dot_v, gbuf, pf, ysb, yrl, yfin,
    qf, qs, zrs,
    local_sems, send_sems, f_sems, zr, xs, xr, yr, y2, sr, fr,
    f_near, f_far, f_pair,
    pair_s, pair_r, sb_s, rl_r, fin_r,
    sv_s, sv_r, dv_s, dv_r, sd_r, g_sems, g_near, g_far, g_pair,
    yrl_r, yfin_r, zs_s, zs_r, a_z, a_y, a_y2,
):
    at = Place()
    x, c, y, z, g, v = at.x, at.c, at.y, at.z, at.g, at.v
    up_z, down_z = at.at_z((z + 1) % NZ), at.at_z((z + NZ - 1) % NZ)
    up_y, down_y = at.at_y((y + 1) % NY), at.at_y((y + 3) % NY)

    load_weight = pltpu.make_async_copy(weight_hbm, weight, local_sems.at[0])
    load_targets = pltpu.make_async_copy(targets_hbm, targets, local_sems.at[1])
    load_weight.start()
    load_targets.start()

    with phase("A_feat"):
        live = (valid[...] == 1).astype(F32)
        row = lax.broadcasted_iota(jnp.int32, (128, 128), 0)
        lane = lax.broadcasted_iota(jnp.int32, (128, 128), 1)
        wanted = column_tile(parents[...].astype(F32)).astype(jnp.int32) + row // TREE * TREE
        pick = (lane == wanted).astype(BF16)
        chosen = jnp.dot(pick, feat[...], preferred_element_type=F32).astype(BF16)
        fall[g, 0] = chosen[:64]
        fall[g, 1] = chosen[64:]
        own_gain = gains[g]
        gain[...] = jnp.concatenate([own_gain[k : k + 1] for k in range(8)], axis=1)

    with phase("A_greet"):
        barrier = pltpu.get_barrier_semaphore()

        @pl.loop(1, 32)
        def _(k):
            pl.semaphore_signal(
                barrier,
                inc=1,
                device_id=(g, (v + k) % 32),
                device_id_type=pl.DeviceIdType.MESH,
            )

        @pl.loop(1, 8)
        def _(k):
            pl.semaphore_signal(
                barrier,
                inc=1,
                device_id=((g + k) % 8, v),
                device_id_type=pl.DeviceIdType.MESH,
            )

        pl.semaphore_wait(barrier, 38)
    send = Sender(send_sems)
    spread = Gather(at, fall, Sender(f_sems), f_near, f_far, f_pair)

    def to_slice(src, j):
        @pl.when(j != g)
        def _():
            remote(src, xall.at[y, g], xs.at[j], xr.at[g], at.dp(j)).start()

        @pl.when(j == g)
        def _():
            pltpu.make_async_copy(src, xall.at[y, g], xs.at[j]).start()

    with phase("A_z"):
        for step in range(5):
            low, high = (z + NZ - step) % NZ, (z + step) % NZ
            if step > 0:
                arrived(zbuf.at[low], zr.at[low], up_z, zr.at[low])
            src = hid if step == 0 else zbuf.at[low]
            if step < 4:
                send(src, zbuf.at[low], zr.at[low], up_z)
            if step == 0:
                send(hid, zbuf.at[high], zr.at[high], down_z)
            to_slice(src, low)
            if step == 0:
                spread.start()
            if 0 < step < 4:
                arrived(zbuf.at[high], zr.at[high], up_z, zr.at[high])
                if step < 3:
                    send(zbuf.at[high], zbuf.at[high], zr.at[high], down_z)
                to_slice(zbuf.at[high], high)

    with phase("A_stat"):
        squares = jnp.square(hid[...].astype(F32))
        for k in range(1, NZ):
            squares = squares + jnp.square(zbuf[(z + k) % NZ].astype(F32))
        stat[y] = row_tile(jnp.sum(squares, axis=1, keepdims=True))
        for k in range(1, NY):
            send(stat.at[y], stat.at[y], sr.at[y], at.at_y((y + k) % NY))

    turns = (2, 1, 3, 0)

    def group(k):
        return 2 * ((x + turns[k // 2]) % NX) + k % 2

    def y_send(k):
        block = xall.at[y, group(k)]
        sem = xr.at[group(k)]
        if k < 6:
            arrived(block, sem, up_y, sem)
        else:

            @pl.when(c != k % 2)
            def _():
                arrived(block, sem, up_y, sem)

            @pl.when(c == k % 2)
            def _():
                pltpu.make_async_copy(hid, block, xs.at[g]).wait()

        send(block, block, yr.at[0, k], up_y)
        send(block, block, yr.at[1, k], down_y)

    def y_relay(k):
        for side, step in ((0, 3), (1, 1)):
            block = xall.at[(y + step) % NY, group(k)]
            arrived(block, yr.at[side, k], up_y, yr.at[side, k])
            if k % 2 == side:
                send(block, block, y2.at[k], up_y if side == 0 else down_y)
        if k + 3 < 8:
            y_send(k + 3)

    def y_far(k):
        block = xall.at[(y + 2) % NY, group(k)]
        arrived(block, y2.at[k], up_y, y2.at[k])

    def normalise(k):
        i = group(k)
        scale = cols[i]
        scale = jnp.concatenate([scale, scale], axis=1)
        rows = pl.ds(pl.multiple_of(i * 128, 128), 128)
        for part in range(NY):
            columns = slice(part * 256, part * 256 + 256)
            values = xall[part, i].astype(F32)
            normed[rows, columns] = (values * scale * gain[:, columns]).astype(BF16)

    def pair_copy(step, t):
        return remote(
            pk.at[step, t, 1 - c], pr.at[step, t],
            pair_s.at[step, t], pair_r.at[step, t], at.partner(),
        )

    def multiply(step):
        rows = pl.ds(pl.multiple_of(((x + step) % NX) * 256, 256), 256)

        @pl.loop(0, 8)
        def _(t):
            tile = pl.ds(pl.multiple_of(t * 256, 256), 256)
            part = lax.dot_general(
                normed[rows, :],
                weight[tile, :],
                (((1,), (1,)), ((), ())),
                preferred_element_type=F32,
            )
            pk[step, t, 0] = part[:128]
            pk[step, t, 1] = part[128:]
            pair_copy(step, t).start()

    def total_of(step, t):
        arrived(pr.at[step, t], pair_r.at[step, t], at.partner(), pair_r.at[step, t])
        return pk[step, t, c] + pr[step, t]

    def ways(t):
        way = 1 + 2 * (t % 2)
        return way, 4 - way

    def first_hop(t):
        ahead, _ = ways(t)
        return remote(sb.at[t, 0], rl.at[t], sb_s.at[t, 0], rl_r.at[t], at.at_x((x + ahead) % NX))

    def direct(t):
        _, back = ways(t)
        return remote(
            sb.at[t, 1], fin.at[t, 0], sb_s.at[t, 1], fin_r.at[t, 0], at.at_x((x + back) % NX)
        )

    def onward(t):
        ahead, _ = ways(t)
        return remote(
            sb.at[t, 2], fin.at[t, 1], sb_s.at[t, 2], fin_r.at[t, 1], at.at_x((x + ahead) % NX)
        )

    def encode(t, k, value):
        top = jnp.max(jnp.abs(value), axis=0, keepdims=True)
        step = (120.0 / jnp.maximum(top, 1e-30)).astype(BF16)
        sb[t, k, 128:] = jnp.broadcast_to(step, (16, 256))
        step = sb[t, k, 128:].astype(F32)[0:1]
        sb[t, k, :128] = jnp.exp2(value * step).astype(BF16)

    def decode(block):
        step = block[128:].astype(F32)[0:1]
        return jnp.log2(block[:128].astype(F32)) * (1.0 / step)

    with phase("A_ysend"):
        for k in range(3):
            y_send(k)

    with phase("A_rf"):
        total = stat[y]
        for k in range(1, NY):
            other = (y + k) % NY
            arrived(stat.at[other], sr.at[other], up_y, sr.at[other])
            total = total + stat[other]
        factor = lax.rsqrt(total / (1024.0 * 8) + 1e-05)
        rf[g] = stack_rows(factor[0:1], live)
        for k in range(1, 8):
            send(rf.at[g], rf.at[g], fr.at[g], at.dp((g + k) % 8))

    with phase("A_y0123"):
        y_relay(0)
        y_relay(1)
        spread.middle(True)
        y_relay(2)
        for k in range(1, 8):
            other = (g + k) % 8
            arrived(rf.at[other], fr.at[other], up_y, fr.at[other])
        for i in range(8):
            cols[i] = column_tile(rf[i, 0:1])
        y_relay(3)
        load_weight.wait()
        load_targets.wait()
    with phase("A_far01"):
        y_far(0)
        y_far(1)
        normalise(0)
        normalise(1)
    with phase("F_mul2"):
        multiply(2)
        y_relay(4)
    with phase("F_hop"):

        @pl.loop(0, 8)
        def _(t):
            encode(t, 0, total_of(2, t))
            first_hop(t).start()

    with phase("A_y56"):
        y_relay(5)
        y_relay(6)
    with phase("A_far2345"):
        for k in range(2, 6):
            y_far(k)
            normalise(k)
    with phase("F_mul13"):
        multiply(1)
        multiply(3)
        y_relay(7)
    with phase("F_both"):

        @pl.loop(0, 8)
        def _(t):
            ahead, back = ways(t)
            encode(t, 1, total_of(back, t))
            direct(t).start()
            arrived(rl.at[t], rl_r.at[t], at.partner(), rl_r.at[t])
            encode(t, 2, total_of(ahead, t) + decode(rl.at[t]))
            onward(t).start()

    with phase("A_far67"):
        spread.middle(False)
        for k in range(6, 8):
            y_far(k)
            normalise(k)
    with phase("F_mul0"):
        multiply(0)
        top = jnp.max(targets[...].astype(F32), axis=1, keepdims=True)
        part = jnp.zeros((128, 256), F32)
        for k in range(8):
            part = part + jnp.exp(targets[:, k * 256 : k * 256 + 256].astype(F32) - top)
        tst[...] = stack_rows(
            jnp.zeros((1, 128), F32),
            jnp.zeros((1, 128), F32),
            row_tile(top)[0:1],
            row_tile(jnp.sum(part, axis=1, keepdims=True))[0:1],
        )

    with phase("F_fin"):

        @pl.loop(0, 8)
        def _(t):
            own = total_of(0, t)
            for k in range(2):
                arrived(fin.at[t, k], fin_r.at[t, k], at.partner(), fin_r.at[t, k])
            lg[t] = own + decode(fin.at[t, 0]) + decode(fin.at[t, 1])

    def tell_all(tile, send_sem, recv_sem):
        @pl.loop(1, 32)
        def _(k):
            remote(
                tile.at[v], tile.at[v], send_sem.at[k], recv_sem.at[v], (g, (v + k) % 32)
            ).start()

    def hear_all(tile, recv_sem):
        @pl.loop(1, 32)
        def _(k):
            other = (v + k) % 32
            arrived(tile.at[other], recv_sem.at[other], up_y, recv_sem.at[other])

    with phase("B_stat"):
        top = lg[0]
        for t in range(1, 8):
            top = jnp.maximum(top, lg[t])
        top = jnp.max(top, axis=1, keepdims=True)
        part = jnp.zeros((128, 256), F32)
        for t in range(8):
            part = part + jnp.exp(lg[t] - top)
        stat_v[v] = stack_rows(
            row_tile(top)[0:1],
            row_tile(jnp.sum(part, axis=1, keepdims=True))[0:1],
            tst[2:3],
            tst[3:4],
        )
        tell_all(stat_v, sv_s, sv_r)

    with phase("B_statv"):
        hear_all(stat_v, sv_r)
        wide = lambda row: jnp.concatenate([column_tile(row)] * 2, axis=1)
        tops, scales = [], []
        for k in (0, 2):
            top = jnp.max(stat_v[:, k, :], axis=0, keepdims=True)
            part = stat_v[:, k + 1, :] * jnp.exp(stat_v[:, k, :] - top)
            tops.append(wide(top))
            scales.append(wide(1.0 / jnp.sum(part, axis=0, keepdims=True)))
        count = jnp.zeros((1, 128), F32)
        for i in range(8):
            count = count + rf[i, 1:2]
        count = jnp.sum(count, axis=1, keepdims=True)
        scale = wide(1048576.0 * live / count)

    gather = Gather(at, gbuf, Sender(g_sems), g_near, g_far, g_pair)
    with phase("B_G"):
        acc = jnp.zeros((128, 256), F32)
        for t in range(8):
            draft = jnp.exp(lg[t] - tops[0]) * scales[0]
            target = (
                jnp.exp(targets[:, t * 256 : t * 256 + 256].astype(F32) - tops[1]) * scales[1]
            )
            column = (t % 4) * 256
            value = (scale * (draft - target)).astype(BF16)
            gbuf[g, t // 4, :, column : column + 256] = value
            acc = acc + value.astype(F32) * lg[t]
        gather.start()
        dot_v[v] = row_tile(jnp.sum(acc, axis=1, keepdims=True))
        tell_all(dot_v, dv_s, dv_r)

    steps = (0, 3, 1, 2)

    def block_of(k):
        return (x + steps[k]) % NX

    def backward(k):
        block = pl.ds(block_of(k) * NC, 2)

        @pl.loop(0, 4)
        def _(n):
            columns = pl.ds(pl.multiple_of(n * 256, 256), 256)
            part = jnp.zeros((256, 256), F32)
            for half in range(2):
                part = part + jnp.dot(
                    gbuf[block, half].reshape(256, 1024),
                    weight[half * 1024 : half * 1024 + 1024, columns],
                    preferred_element_type=F32,
                )
            for which in range(2):
                for dest in range(NY):
                    row = which * 128 + dest * 32
                    pf[k, dest, which, :, columns] = part[row : row + 32]

        way = 1 if k % 2 == 0 else 3
        ysb[k, 0] = pf[k, (y + 2) % NY].astype(BF16)
        send(ysb.at[k, 0], yrl.at[k], yrl_r.at[k], at.at_y((y + way) % NY))
        ysb[k, 1] = pf[k, (y + 4 - way) % NY].astype(BF16)
        send(ysb.at[k, 1], yfin.at[k, 0], yfin_r.at[k, 0], at.at_y((y + 4 - way) % NY))

    def y_second(k):
        way = 1 if k % 2 == 0 else 3
        arrived(yrl.at[k], yrl_r.at[k], up_y, yrl_r.at[k])
        ysb[k, 2] = (pf[k, (y + way) % NY] + yrl[k].astype(F32)).astype(BF16)
        send(ysb.at[k, 2], yfin.at[k, 1], yfin_r.at[k, 1], at.at_y((y + way) % NY))

    def z_send(k, dest):
        return remote(
            qs.at[k, dest], zrs.at[k, z], zs_s.at[k, dest], zs_r.at[k, z], at.at_z(dest)
        )

    far_first = (4, 3, 5, 2, 6, 1, 7)

    def y_third(k):
        for j in range(2):
            arrived(yfin.at[k, j], yfin_r.at[k, j], up_y, yfin_r.at[k, j])
        value = pf[k, y] + yfin[k, 0].astype(F32) + yfin[k, 1].astype(F32)
        for owner in range(NZ):
            piece = value[:, :, 128 * owner : 128 * owner + 128]
            qf[k, owner] = piece
            qs[k, owner] = piece.astype(BF16)
        for shift in far_first:
            z_send(k, (z + shift) % NZ).start()

    own_columns = pl.ds(pl.multiple_of(z * 128, 128), 128)

    def piece_of(k, owner):
        columns = pl.ds(pl.multiple_of(owner * 128, 128), 128)
        return grad_out.at[pl.ds(2 * block_of(k), 2), y, :, columns]

    def z_fourth(k):
        total = qf[k, z]
        for j in range(1, NZ):
            other = (z + j) % NZ
            arrived(zrs.at[k, other], zs_r.at[k, other], up_y, zs_r.at[k, other])
            total = total + zrs[k, other].astype(F32)
        rows = pl.ds(pl.multiple_of(y * 32, 32), 32)
        lanes = pl.ds(pl.multiple_of((z % 2) * 128, 128), 128)
        for which in range(2):
            i = 2 * block_of(k) + which
            values = xall[z // 2, i, rows, lanes].astype(F32)
            grad = cols[i, rows, :] * gain[:, own_columns] * total[which]
            grad = grad - values * scols[i, rows, :]
            grad_out[i, y, :, own_columns] = grad.astype(BF16)
        mine = piece_of(k, z)
        for shift in far_first:
            send(mine, mine, a_z.at[k, z], at.at_z((z + shift) % NZ))

    def across(k):
        for j in (1, 7, 2, 6, 3, 5, 4):
            other = (z + j) % NZ
            arrived(piece_of(k, other), a_z.at[k, other], up_y, a_z.at[k, other])
        mine = grad_out.at[pl.ds(2 * block_of(k), 2), y]
        send(mine, mine, a_y.at[0, k], up_y)
        send(mine, mine, a_y.at[1, k], down_y)

    def across_relay(k):
        for side, step in ((0, 3), (1, 1)):
            block = grad_out.at[pl.ds(2 * block_of(k), 2), (y + step) % NY]
            arrived(block, a_y.at[side, k], up_y, a_y.at[side, k])
            half = grad_out.at[2 * block_of(k) + side, (y + step) % NY]
            send(half, half, a_y2.at[side, k], up_y if side == 0 else down_y)

    def across_far(k):
        for side in range(2):
            half = grad_out.at[2 * block_of(k) + side, (y + 2) % NY]
            arrived(half, a_y2.at[side, k], up_y, a_y2.at[side, k])

    with phase("G_bw0"):
        gather.paired(0)
        backward(0)
    with phase("G_feat"):
        spread.last()
        spread.paired(0)
        spread.paired(1)
        spread.paired(3)
    with phase("G_mid"):
        gather.middle(True)
    with phase("G_ys0"):
        y_second(0)
    with phase("G_dot"):
        hear_all(dot_v, dv_r)
        dot = jnp.sum(dot_v[:, 0, :], axis=0, keepdims=True)
        factor = rf[g][0:1]
        srow[g] = jnp.broadcast_to(factor * factor * dot / (1024.0 * 8), (8, 128))
        for k in range(1, 8):
            send(srow.at[g], srow.at[g], sd_r.at[g], at.dp((g + k) % 8))
    with phase("G_yt0"):
        y_third(0)
    with phase("G_mid2"):
        gather.middle(False)
        gather.paired(3)
    with phase("G_bw1"):
        backward(1)
    with phase("G_bw2"):
        gather.paired(1)
        backward(2)
    with phase("G_s"):
        for k in range(1, 8):
            other = (g + k) % 8
            arrived(srow.at[other], sd_r.at[other], up_y, sd_r.at[other])
        for i in range(8):
            scols[i] = column_tile(srow[i, 0:1])
    with phase("G_z0"):
        z_fourth(0)
    with phase("G_last"):
        gather.last()
        y_second(1)
        gather.paired(2)
    with phase("G_bw3"):
        backward(3)
    with phase("H_ax0"):
        across(0)
    with phase("H_ys2"):
        y_second(2)
    with phase("H_yt1"):
        y_third(1)
    with phase("H_ys3"):
        y_second(3)
    with phase("H_ar0"):
        across_relay(0)
    with phase("H_yt2"):
        y_third(2)
    with phase("H_z1"):
        z_fourth(1)
    with phase("H_yt3"):
        y_third(3)
    with phase("H_ax1"):
        across(1)
    with phase("H_z2"):
        z_fourth(2)
    with phase("H_z3"):
        z_fourth(3)
    with phase("H_ax2"):
        across(2)
    with phase("H_ar1"):
        across_relay(1)
    with phase("H_ax3"):
        across(3)
    with phase("H_ar2"):
        across_relay(2)
    with phase("H_ar3"):
        across_relay(3)
    with phase("H_far"):
        for k in range(4):
            across_far(k)
        share_out[...] = grad_out[z, y]
        spread.paired(2)

    with phase("H_drain"):

        @pl.loop(0, 8)
        def _(t):
            for step in range(4):
                pair_copy(step, t).wait_send()
            first_hop(t).wait_send()
            direct(t).wait_send()
            onward(t).wait_send()

        @pl.loop(1, 32)
        def _(k):
            other = (g, (v + k) % 32)
            remote(stat_v.at[v], stat_v.at[v], sv_s.at[k], sv_r.at[v], other).wait_send()
            remote(dot_v.at[v], dot_v.at[v], dv_s.at[k], dv_r.at[v], other).wait_send()

        send.drain()
        spread.send.drain()
        gather.send.drain()
        for k in range(4):
            for j in range(1, NZ):
                z_send(k, (z + j) % NZ).wait_send()
        for j in range(8):

            @pl.when(g != j)
            def _():
                remote(hid, xall.at[y, g], xs.at[j], xr.at[g], at.dp(j)).wait_send()


VMEM = pl.BlockSpec(memory_space=pltpu.VMEM)
HBM = pl.BlockSpec(memory_space=pl.ANY)
LIMIT = 60 * 1024 * 1024


def call(*operands):
    return pl.pallas_call(
        kernel,
        out_shape=(
            jax.ShapeDtypeStruct((32, 1024), BF16),
            jax.ShapeDtypeStruct((8, NY, 32, 1024), BF16),
            jax.ShapeDtypeStruct((8, 2, 64, 768), BF16),
        ),
        in_specs=[VMEM] * 5 + [HBM] * 2,
        out_specs=[VMEM] * 3,
        scratch_shapes=[
            pltpu.VMEM((2048, 1024), BF16),
            pltpu.VMEM((128, 2048), BF16),
            pltpu.VMEM((NZ, 128, 256), BF16),
            pltpu.VMEM((NY, 8, 128, 256), BF16),
            pltpu.VMEM((1024, 1024), BF16),
            pltpu.VMEM((NY, 8, 128), F32),
            pltpu.VMEM((8, 128, 128), F32),
            pltpu.VMEM((8, 128, 128), F32),
            pltpu.VMEM((8, 8, 128), F32),
            pltpu.VMEM((8, 8, 128), F32),
            pltpu.VMEM((1, 1024), F32),
            pltpu.VMEM((NX, 8, 2, 128, 256), F32),
            pltpu.VMEM((NX, 8, 128, 256), F32),
            pltpu.VMEM((8, 3, 144, 256), BF16),
            pltpu.VMEM((8, 144, 256), BF16),
            pltpu.VMEM((8, 2, 144, 256), BF16),
            pltpu.VMEM((8, 128, 256), F32),
            pltpu.VMEM((8, 128), F32),
            pltpu.VMEM((32, 8, 128), F32),
            pltpu.VMEM((32, 8, 128), F32),
            pltpu.VMEM((8, 2, 128, 1024), BF16),
            pltpu.VMEM((4, NY, 2, 32, 1024), F32),
            pltpu.VMEM((4, 3, 2, 32, 1024), BF16),
            pltpu.VMEM((4, 2, 32, 1024), BF16),
            pltpu.VMEM((4, 2, 2, 32, 1024), BF16),
            pltpu.VMEM((4, NZ, 2, 32, 128), F32),
            pltpu.VMEM((4, NZ, 2, 32, 128), BF16),
            pltpu.VMEM((4, NZ, 2, 32, 128), BF16),
            DMA((2,)),
            DMA((120,)),
            DMA((GATHER_SENDS,)),
            DMA((NZ,)),
            DMA((8,)),
            DMA((8,)),
            DMA((2, 8)),
            DMA((8,)),
            DMA((NY,)),
            DMA((8,)),
            DMA((2, 2)),
            DMA((2,)),
            DMA((4, 2)),
            DMA((NX, 8)),
            DMA((NX, 8)),
            DMA((8, 3)),
            DMA((8,)),
            DMA((8, 2)),
            DMA((32,)),
            DMA((32,)),
            DMA((32,)),
            DMA((32,)),
            DMA((8,)),
            DMA((GATHER_SENDS,)),
            DMA((2, 2)),
            DMA((2,)),
            DMA((4, 2)),
            DMA((4,)),
            DMA((4, 2)),
            DMA((4, NZ)),
            DMA((4, NZ)),
            DMA((4, NZ)),
            DMA((2, 4)),
            DMA((2, 4)),
        ],
        compiler_params=pltpu.CompilerParams(
            collective_id=0, has_side_effects=True, vmem_limit_bytes=LIMIT
        ),
    )(*operands)


def body(hidden, norm_gain, head_weight, target_logits, valid_rows, parents, features):
    share, grad, parent_features = call(
        hidden,
        valid_rows.reshape(1, 128),
        parents.reshape(1, 128),
        features,
        norm_gain.reshape(8, 8, 128),
        head_weight,
        target_logits,
    )
    grad_joining = lax.dot_general(
        grad.reshape(1024, 1024),
        parent_features.reshape(1024, 768),
        (((0,), (0,)), ((), ())),
        preferred_element_type=F32,
    )
    return (share, grad_joining)


def solution(mesh):
    placed = (
        P("dp", "vocab"),
        P(),
        P("vocab", "dp"),
        P("dp", "vocab"),
        P("dp"),
        P("dp"),
        P("dp", "vocab"),
    )
    return jax.shard_map(
        body,
        mesh=mesh,
        in_specs=placed,
        out_specs=(P("vocab", "dp"), P("dp", "vocab")),
        check_vma=False,
    )
```

time: 169 us -> 153 us (0.905)
  Pallas kernels: 162 us -> 144 us
    pallas_call x1, Pallas kernels: 162 us -> 144 us  [call(): pl.pallas_call(kernel, out_shape=(jax.ShapeDtypeStruct((32, 1024), BF16),...]
where the time goes in v3:
time: 153 us; the launch traced here: 151 us
  Pallas kernels  144 us (94%)
  matrix products  5.59 us (4%)
    pallas_call x1, Pallas kernels, call(): pl.pallas_call(kernel, out_shape=(jax.ShapeDtypeStruct((32, 1024), BF16),...  144 us
    dot_general x1, matrix products, body(): lax.dot_general(grad.reshape(1024, 1024), parent_features.reshape(1024, 7...  5.59 us

profile of v3, /device:TPU:24, one launch (start us, length us, event | category | flops | bytes accessed | tf_op | source)
XLA Modules:
  0.0 151.3 jit_solution(840847639854618308)
XLA Ops:
  0.6 144.4 %shard_map.86 = (bf16[32,1024]{1,0:T(8,128)(2,1)}, bf16[8,4,32,1024]{3,2,1,0:T(8,128)(2,1)}, bf16[8,2,64,768]{3,2,1,0:T(8,128)(2,1)}) custom-call(bf16[128,256]{1,0:T(8,128)(2,1)} %hid.1, s32[1,128]{1,0:T(1,128)} %bitcast.8, s32[1,128]{1,0:T(1,128)} %bitcast.9, bf16[128,768]{1,0:T(8,128)(2,1)} %feat.1, f32[8,8,128]{2,1,0:T(8,128)} %bitcast.7, ...), custom_call_target="tpu_custom_call" | custom-call | tf_op jit(solution)/shard_map/pallas_call | solution.py:699
  145.1 0.0 copy-start
  145.1 5.6 %fusion = f32[1024,768]{1,0:T(8,128)} fusion(bf16[1024,1024]{1,0:T(8,128)(2,1)} %bitcast.10, bf16[1024,768]{1,0:T(8,128)(2,1)} %bitcast.11), kind=kOutput, calls=%fused_computation | convolution fusion | flops 1610612736 | bytes 6815744 | tf_op jit(solution)/shard_map/dot_general | solution.py:788
  150.7 0.0 copy-done
  150.7 0.6 copy.10
Async XLA Ops:
  145.1 5.6 %copy-start = (bf16[32,1024]{1,0:T(8,128)(2,1)S(1)}, bf16[32,1024]{1,0:T(8,128)(2,1)}, u32[]{:S(2)}) copy-start(bf16[32,1024]{1,0:T(8,128)(2,1)} %get-tuple-element.10) | copy-start | bytes 196612

commit v4 on v3

--- a/solution.py
+++ b/solution.py
@@ -107,11 +107,10 @@
             arrived(block, self.far.at[half], at.partner(), self.far.at[half])
             self.send(block, block, self.pair.at[2, half], at.partner())
 
-    def paired(self, step):
+    def paired(self, step, half):
         at = self.at
-        for half in range(2):
-            block = self.buf.at[self.slot(step, 1 - at.c), half]
-            arrived(block, self.pair.at[step, half], at.partner(), self.pair.at[step, half])
+        block = self.buf.at[self.slot(step, 1 - at.c), half]
+        arrived(block, self.pair.at[step, half], at.partner(), self.pair.at[step, half])
 
 
 GATHER_SENDS = 14
@@ -135,7 +134,8 @@
 
 def kernel(
     hid, valid, parents, feat, gains, weight_hbm, targets_hbm,
-    share_out, grad_out, fall,
+    share_out, grad_hbm, feat_hbm,
+    grad_out, feat_out, fall,
     weight, targets, zbuf, xall, normed, stat, cols, scols, rf, srow, gain,
     pk, pr, sb, rl, fin, lg, tst, stat_v, dot_v, gbuf, pf, ysb, yrl, yfin,
     qf, qs, zrs,
@@ -201,23 +201,28 @@
         def _():
             pltpu.make_async_copy(src, xall.at[y, g], xs.at[j]).start()
 
+    def piece(ref, q):
+        return ref.at[32 * q : 32 * q + 32]
+
     with phase("A_z"):
-        for step in range(5):
+        for q in range(4):
+            send(piece(hid, q), piece(zbuf.at[z], q), zr.at[q, z], up_z)
+            send(piece(hid, q), piece(zbuf.at[z], q), zr.at[q, z], down_z)
+        to_slice(hid, z)
+        spread.start()
+        for step in range(1, 5):
             low, high = (z + NZ - step) % NZ, (z + step) % NZ
-            if step > 0:
-                arrived(zbuf.at[low], zr.at[low], up_z, zr.at[low])
-            src = hid if step == 0 else zbuf.at[low]
+            for q in range(4):
+                block = piece(zbuf.at[low], q)
+                arrived(block, zr.at[q, low], up_z, zr.at[q, low])
+                if step < 4:
+                    send(block, block, zr.at[q, low], up_z)
+                    block = piece(zbuf.at[high], q)
+                    arrived(block, zr.at[q, high], up_z, zr.at[q, high])
+                    if step < 3:
+                        send(block, block, zr.at[q, high], down_z)
+            to_slice(zbuf.at[low], low)
             if step < 4:
-                send(src, zbuf.at[low], zr.at[low], up_z)
-            if step == 0:
-                send(hid, zbuf.at[high], zr.at[high], down_z)
-            to_slice(src, low)
-            if step == 0:
-                spread.start()
-            if 0 < step < 4:
-                arrived(zbuf.at[high], zr.at[high], up_z, zr.at[high])
-                if step < 3:
-                    send(zbuf.at[high], zbuf.at[high], zr.at[high], down_z)
                 to_slice(zbuf.at[high], high)
 
     with phase("A_stat"):
@@ -280,21 +285,18 @@
             pair_s.at[step, t], pair_r.at[step, t], at.partner(),
         )
 
-    def multiply(step):
+    def multiply(step, t):
         rows = pl.ds(pl.multiple_of(((x + step) % NX) * 256, 256), 256)
-
-        @pl.loop(0, 8)
-        def _(t):
-            tile = pl.ds(pl.multiple_of(t * 256, 256), 256)
-            part = lax.dot_general(
-                normed[rows, :],
-                weight[tile, :],
-                (((1,), (1,)), ((), ())),
-                preferred_element_type=F32,
-            )
-            pk[step, t, 0] = part[:128]
-            pk[step, t, 1] = part[128:]
-            pair_copy(step, t).start()
+        tile = pl.ds(pl.multiple_of(t * 256, 256), 256)
+        part = lax.dot_general(
+            normed[rows, :],
+            weight[tile, :],
+            (((1,), (1,)), ((), ())),
+            preferred_element_type=F32,
+        )
+        pk[step, t, 0] = part[:128]
+        pk[step, t, 1] = part[128:]
+        pair_copy(step, t).start()
 
     def total_of(step, t):
         arrived(pr.at[step, t], pair_r.at[step, t], at.partner(), pair_r.at[step, t])
@@ -364,31 +366,30 @@
         y_far(1)
         normalise(0)
         normalise(1)
-    with phase("F_mul2"):
-        multiply(2)
+    with phase("F_hop"):
+
+        @pl.loop(0, 9)
+        def _(t):
+            @pl.when(t < 8)
+            def _():
+                multiply(2, t)
+
+            @pl.when(t > 0)
+            def _():
+                encode(t - 1, 0, total_of(2, t - 1))
+                first_hop(t - 1).start()
+
+    with phase("A_y56"):
         y_relay(4)
-    with phase("F_hop"):
-
-        @pl.loop(0, 8)
-        def _(t):
-            encode(t, 0, total_of(2, t))
-            first_hop(t).start()
-
-    with phase("A_y56"):
         y_relay(5)
         y_relay(6)
     with phase("A_far2345"):
         for k in range(2, 6):
             y_far(k)
             normalise(k)
-    with phase("F_mul13"):
-        multiply(1)
-        multiply(3)
-        y_relay(7)
     with phase("F_both"):
 
-        @pl.loop(0, 8)
-        def _(t):
+        def both(t):
             ahead, back = ways(t)
             encode(t, 1, total_of(back, t))
             direct(t).start()
@@ -396,13 +397,30 @@
             encode(t, 2, total_of(ahead, t) + decode(rl.at[t]))
             onward(t).start()
 
+        @pl.loop(0, 9)
+        def _(t):
+            @pl.when(t < 8)
+            def _():
+                multiply(1, t)
+                multiply(3, t)
+
+            @pl.when(t > 0)
+            def _():
+                both(t - 1)
+
+        y_relay(7)
+
     with phase("A_far67"):
         spread.middle(False)
         for k in range(6, 8):
             y_far(k)
             normalise(k)
     with phase("F_mul0"):
-        multiply(0)
+
+        @pl.loop(0, 8)
+        def _(t):
+            multiply(0, t)
+
         top = jnp.max(targets[...].astype(F32), axis=1, keepdims=True)
         part = jnp.zeros((128, 256), F32)
         for k in range(8):
@@ -475,36 +493,41 @@
             target = (
                 jnp.exp(targets[:, t * 256 : t * 256 + 256].astype(F32) - tops[1]) * scales[1]
             )
-            column = (t % 4) * 256
             value = (scale * (draft - target)).astype(BF16)
-            gbuf[g, t // 4, :, column : column + 256] = value
+            for k in range(8):
+                gbuf[g, k % 2, k // 2 * 16 : k // 2 * 16 + 16, t * 256 : t * 256 + 256] = value[
+                    k * 16 : k * 16 + 16
+                ]
             acc = acc + value.astype(F32) * lg[t]
         gather.start()
         dot_v[v] = row_tile(jnp.sum(acc, axis=1, keepdims=True))
         tell_all(dot_v, dv_s, dv_r)
 
-    steps = (0, 3, 1, 2)
-
-    def block_of(k):
-        return (x + steps[k]) % NX
+    units = (((0, 0), (0, 1)), ((3, 0), (1, 1)), ((3, 1), (1, 0)), ((2, 0), (2, 1)))
+
+    def block_of(step):
+        return (x + step) % NX
 
     def backward(k):
-        block = pl.ds(block_of(k) * NC, 2)
+        for step, half in units[k]:
+            gather.paired(step, half)
 
         @pl.loop(0, 4)
         def _(n):
             columns = pl.ds(pl.multiple_of(n * 256, 256), 256)
-            part = jnp.zeros((256, 256), F32)
-            for half in range(2):
-                part = part + jnp.dot(
-                    gbuf[block, half].reshape(256, 1024),
-                    weight[half * 1024 : half * 1024 + 1024, columns],
-                    preferred_element_type=F32,
-                )
-            for which in range(2):
-                for dest in range(NY):
-                    row = which * 128 + dest * 32
-                    pf[k, dest, which, :, columns] = part[row : row + 32]
+            rows = jnp.concatenate(
+                [
+                    gbuf[pl.ds(2 * block_of(step), 2), half].reshape(128, 2048)
+                    for step, half in units[k]
+                ],
+                axis=0,
+            )
+            part = jnp.dot(rows, weight[:, columns], preferred_element_type=F32)
+            for p in range(2):
+                for which in range(2):
+                    for dest in range(NY):
+                        row = p * 128 + which * 64 + dest * 16
+                        pf[k, dest, p, which, :, columns] = part[row : row + 16]
 
         way = 1 if k % 2 == 0 else 3
         ysb[k, 0] = pf[k, (y + 2) % NY].astype(BF16)
@@ -530,9 +553,9 @@
             arrived(yfin.at[k, j], yfin_r.at[k, j], up_y, yfin_r.at[k, j])
         value = pf[k, y] + yfin[k, 0].astype(F32) + yfin[k, 1].astype(F32)
         for owner in range(NZ):
-            piece = value[:, :, 128 * owner : 128 * owner + 128]
-            qf[k, owner] = piece
-            qs[k, owner] = piece.astype(BF16)
+            part = value[:, :, :, 128 * owner : 128 * owner + 128]
+            qf[k, owner] = part
+            qs[k, owner] = part.astype(BF16)
         for shift in far_first:
             z_send(k, (z + shift) % NZ).start()
 
@@ -540,7 +563,7 @@
 
     def piece_of(k, owner):
         columns = pl.ds(pl.multiple_of(owner * 128, 128), 128)
-        return grad_out.at[pl.ds(2 * block_of(k), 2), y, :, columns]
+        return grad_out.at[k, y, :, :, :, columns]
 
     def z_fourth(k):
         total = qf[k, z]
@@ -548,14 +571,15 @@
             other = (z + j) % NZ
             arrived(zrs.at[k, other], zs_r.at[k, other], up_y, zs_r.at[k, other])
             total = total + zrs[k, other].astype(F32)
-        rows = pl.ds(pl.multiple_of(y * 32, 32), 32)
         lanes = pl.ds(pl.multiple_of((z % 2) * 128, 128), 128)
-        for which in range(2):
-            i = 2 * block_of(k) + which
-            values = xall[z // 2, i, rows, lanes].astype(F32)
-            grad = cols[i, rows, :] * gain[:, own_columns] * total[which]
-            grad = grad - values * scols[i, rows, :]
-            grad_out[i, y, :, own_columns] = grad.astype(BF16)
+        for p, (step, half) in enumerate(units[k]):
+            rows = pl.ds(pl.multiple_of(y * 32 + half * 16, 16), 16)
+            for which in range(2):
+                i = 2 * block_of(step) + which
+                values = xall[z // 2, i, rows, lanes].astype(F32)
+                grad = cols[i, rows, :] * gain[:, own_columns] * total[p, which]
+                grad = grad - values * scols[i, rows, :]
+                grad_out[k, y, p, which, :, own_columns] = grad.astype(BF16)
         mine = piece_of(k, z)
         for shift in far_first:
             send(mine, mine, a_z.at[k, z], at.at_z((z + shift) % NZ))
@@ -564,34 +588,41 @@
         for j in (1, 7, 2, 6, 3, 5, 4):
             other = (z + j) % NZ
             arrived(piece_of(k, other), a_z.at[k, other], up_y, a_z.at[k, other])
-        mine = grad_out.at[pl.ds(2 * block_of(k), 2), y]
+        mine = grad_out.at[k, y]
         send(mine, mine, a_y.at[0, k], up_y)
         send(mine, mine, a_y.at[1, k], down_y)
 
     def across_relay(k):
         for side, step in ((0, 3), (1, 1)):
-            block = grad_out.at[pl.ds(2 * block_of(k), 2), (y + step) % NY]
+            block = grad_out.at[k, (y + step) % NY]
             arrived(block, a_y.at[side, k], up_y, a_y.at[side, k])
-            half = grad_out.at[2 * block_of(k) + side, (y + step) % NY]
+            half = grad_out.at[k, (y + step) % NY, side]
             send(half, half, a_y2.at[side, k], up_y if side == 0 else down_y)
+
+    def to_hbm(k):
+        return pltpu.make_async_copy(grad_out.at[k], grad_hbm.at[k], local_sems.at[2 + k])
 
     def across_far(k):
         for side in range(2):
-            half = grad_out.at[2 * block_of(k) + side, (y + 2) % NY]
+            half = grad_out.at[k, (y + 2) % NY, side]
             arrived(half, a_y2.at[side, k], up_y, a_y2.at[side, k])
+        to_hbm(k).start()
+
+    feat_to_hbm = pltpu.make_async_copy(feat_out, feat_hbm, local_sems.at[6])
 
     with phase("G_bw0"):
-        gather.paired(0)
         backward(0)
     with phase("G_feat"):
         spread.last()
-        spread.paired(0)
-        spread.paired(1)
-        spread.paired(3)
+        for step in (0, 1, 3):
+            for half in range(2):
+                spread.paired(step, half)
     with phase("G_mid"):
         gather.middle(True)
     with phase("G_ys0"):
         y_second(0)
+    with phase("G_bw1"):
+        backward(1)
     with phase("G_dot"):
         hear_all(dot_v, dv_r)
         dot = jnp.sum(dot_v[:, 0, :], axis=0, keepdims=True)
@@ -603,11 +634,9 @@
         y_third(0)
     with phase("G_mid2"):
         gather.middle(False)
-        gather.paired(3)
-    with phase("G_bw1"):
-        backward(1)
+    with phase("G_ys1"):
+        y_second(1)
     with phase("G_bw2"):
-        gather.paired(1)
         backward(2)
     with phase("G_s"):
         for k in range(1, 8):
@@ -617,49 +646,69 @@
             scols[i] = column_tile(srow[i, 0:1])
     with phase("G_z0"):
         z_fourth(0)
+    with phase("G_yt1"):
+        y_third(1)
     with phase("G_last"):
         gather.last()
-        y_second(1)
-        gather.paired(2)
+    with phase("G_ys2"):
+        y_second(2)
     with phase("G_bw3"):
         backward(3)
     with phase("H_ax0"):
         across(0)
-    with phase("H_ys2"):
-        y_second(2)
-    with phase("H_yt1"):
-        y_third(1)
+    with phase("H_z1"):
+        z_fourth(1)
+    with phase("H_yt2"):
+        y_third(2)
+    with phase("H_feat"):
+        spread.paired(2, 0)
+        spread.paired(2, 1)
+        for k in range(4):
+            for p, (step, half) in enumerate(units[k]):
+                for which in range(2):
+                    for dest in range(NY):
+                        row = dest % 2 * 32 + half * 16
+                        feat_out[k, dest, p, which] = fall[
+                            2 * block_of(step) + which, dest // 2, row : row + 16, :
+                        ]
+        feat_to_hbm.start()
     with phase("H_ys3"):
         y_second(3)
     with phase("H_ar0"):
         across_relay(0)
-    with phase("H_yt2"):
-        y_third(2)
-    with phase("H_z1"):
-        z_fourth(1)
-    with phase("H_yt3"):
-        y_third(3)
     with phase("H_ax1"):
         across(1)
     with phase("H_z2"):
         z_fourth(2)
+    with phase("H_yt3"):
+        y_third(3)
+    with phase("H_ar1"):
+        across_far(0)
+        across_relay(1)
+    with phase("H_ax2"):
+        across(2)
     with phase("H_z3"):
         z_fourth(3)
-    with phase("H_ax2"):
-        across(2)
-    with phase("H_ar1"):
-        across_relay(1)
+    with phase("H_ar2"):
+        across_far(1)
+        across_relay(2)
     with phase("H_ax3"):
         across(3)
-    with phase("H_ar2"):
-        across_relay(2)
+    with phase("H_far2"):
+        across_far(2)
     with phase("H_ar3"):
         across_relay(3)
     with phase("H_far"):
+        across_far(3)
+        away = (z // 2 + NX - x) % NX
+        odd, side = away % 2, away // 2
+        for half in range(2):
+            k = odd * (1 + (half + side + 1) % 2) + (1 - odd) * 3 * side
+            p = odd * (1 - side) + (1 - odd) * half
+            share_out[16 * half : 16 * half + 16, :] = grad_out[k, y, p, z % 2]
         for k in range(4):
-            across_far(k)
-        share_out[...] = grad_out[z, y]
-        spread.paired(2)
+            to_hbm(k).wait()
+        feat_to_hbm.wait()
 
     with phase("H_drain"):
 
@@ -700,12 +749,15 @@
         kernel,
         out_shape=(
             jax.ShapeDtypeStruct((32, 1024), BF16),
-            jax.ShapeDtypeStruct((8, NY, 32, 1024), BF16),
-            jax.ShapeDtypeStruct((8, 2, 64, 768), BF16),
+            jax.ShapeDtypeStruct((4, NY, 2, 2, 16, 1024), BF16),
+            jax.ShapeDtypeStruct((4, NY, 2, 2, 16, 768), BF16),
         ),
         in_specs=[VMEM] * 5 + [HBM] * 2,
-        out_specs=[VMEM] * 3,
+        out_specs=[VMEM, HBM, HBM],
         scratch_shapes=[
+            pltpu.VMEM((4, NY, 2, 2, 16, 1024), BF16),
+            pltpu.VMEM((4, NY, 2, 2, 16, 768), BF16),
+            pltpu.VMEM((8, 2, 64, 768), BF16),
             pltpu.VMEM((2048, 1024), BF16),
             pltpu.VMEM((128, 2048), BF16),
             pltpu.VMEM((NZ, 128, 256), BF16),
@@ -726,18 +778,18 @@
             pltpu.VMEM((8, 128), F32),
             pltpu.VMEM((32, 8, 128), F32),
             pltpu.VMEM((32, 8, 128), F32),
-            pltpu.VMEM((8, 2, 128, 1024), BF16),
-            pltpu.VMEM((4, NY, 2, 32, 1024), F32),
-            pltpu.VMEM((4, 3, 2, 32, 1024), BF16),
-            pltpu.VMEM((4, 2, 32, 1024), BF16),
-            pltpu.VMEM((4, 2, 2, 32, 1024), BF16),
-            pltpu.VMEM((4, NZ, 2, 32, 128), F32),
-            pltpu.VMEM((4, NZ, 2, 32, 128), BF16),
-            pltpu.VMEM((4, NZ, 2, 32, 128), BF16),
-            DMA((2,)),
-            DMA((120,)),
+            pltpu.VMEM((8, 2, 64, 2048), BF16),
+            pltpu.VMEM((4, NY, 2, 2, 16, 1024), F32),
+            pltpu.VMEM((4, 3, 2, 2, 16, 1024), BF16),
+            pltpu.VMEM((4, 2, 2, 16, 1024), BF16),
+            pltpu.VMEM((4, 2, 2, 2, 16, 1024), BF16),
+            pltpu.VMEM((4, NZ, 2, 2, 16, 128), F32),
+            pltpu.VMEM((4, NZ, 2, 2, 16, 128), BF16),
+            pltpu.VMEM((4, NZ, 2, 2, 16, 128), BF16),
+            DMA((7,)),
+            DMA((140,)),
             DMA((GATHER_SENDS,)),
-            DMA((NZ,)),
+            DMA((4, NZ)),
             DMA((8,)),
             DMA((8,)),
             DMA((2, 8)),

time: 153 us -> 147 us (0.961); the launches traced: 151 us -> 147 us
  Pallas kernels: 144 us -> 140 us
    pallas_call x1, Pallas kernels: 144 us -> 140 us  [call(): pl.pallas_call(kernel, out_shape=(jax.ShapeDtypeStruct((32, 1024), BF16),...]
where the time goes in v4:
time: 147 us
  Pallas kernels  140 us (95%)
  matrix products  5.6 us (4%)
    pallas_call x1, Pallas kernels, call(): pl.pallas_call(kernel, out_shape=(jax.ShapeDtypeStruct((32, 1024), BF16),...  140 us
    dot_general x1, matrix products, body(): lax.dot_general(grad.reshape(1024, 1024), parent_features.reshape(1024, 7...  5.6 us

profile of v4, /device:TPU:24, one launch (start us, length us, event | category | flops | bytes accessed | tf_op | source)
XLA Modules:
  0.0 146.9 jit_solution(8421000383260857512)
XLA Ops:
  0.6 140.0 %shard_map.86 = (bf16[32,1024]{1,0:T(8,128)(2,1)}, bf16[4,4,2,2,16,1024]{5,4,3,2,1,0:T(8,128)(2,1)}, bf16[4,4,2,2,16,768]{5,4,3,2,1,0:T(8,128)(2,1)}) custom-call(bf16[128,256]{1,0:T(8,128)(2,1)} %hid.1, s32[1,128]{1,0:T(1,128)} %bitcast.10, s32[1,128]{1,0:T(1,128)} %bitcast.11, bf16[128,768]{1,0:T(8,128)(2,1)} %feat.1, f32[8,8,128]{2,1,0:T(8,128)} %bitcast.9, ...), custom_call_target="tpu_custom_call" | custom-call | tf_op jit(solution)/shard_map/pallas_call | solution.py:748
  140.7 0.0 copy-start
  140.7 5.6 %convolution_bitcast_fusion = f32[1024,768]{1,0:T(8,128)} fusion(bf16[4,4,2,2,16,1024]{5,4,3,2,1,0:T(8,128)(2,1)} %get-tuple-element.6, bf16[4,4,2,2,16,768]{5,4,3,2,1,0:T(8,128)(2,1)} %get-tuple-element.7), kind=kOutput, calls=%fused_computation | convolution fusion | flops 1610612736 | bytes 6815744 | tf_op jit(solution)/shard_map/dot_general | solution.py:840
  146.3 0.0 copy-done
  146.3 0.6 copy.11
Async XLA Ops:
  140.7 5.6 %copy-start = (bf16[32,1024]{1,0:T(8,128)(2,1)S(1)}, bf16[32,1024]{1,0:T(8,128)(2,1)}, u32[]{:S(2)}) copy-start(bf16[32,1024]{1,0:T(8,128)(2,1)} %get-tuple-element.10) | copy-start | bytes 196612

commit v5 on v4

--- a/solution.py
+++ b/solution.py
@@ -134,8 +134,8 @@
 
 def kernel(
     hid, valid, parents, feat, gains, weight_hbm, targets_hbm,
-    share_out, grad_hbm, feat_hbm,
-    grad_out, feat_out, fall,
+    share_out, joined_hbm, grad_hbm, feat_hbm,
+    joined, grad_out, feat_out, fall,
     weight, targets, zbuf, xall, normed, stat, cols, scols, rf, srow, gain,
     pk, pr, sb, rl, fin, lg, tst, stat_v, dot_v, gbuf, pf, ysb, yrl, yfin,
     qf, qs, zrs,
@@ -366,22 +366,25 @@
         y_far(1)
         normalise(0)
         normalise(1)
+    def run(low, high, *stages):
+        @pl.loop(low, high)
+        def _(t):
+            for stage, lag in stages:
+                stage(t - lag)
+
+    def hop(t):
+        encode(t, 0, total_of(2, t))
+        first_hop(t).start()
+
     with phase("F_hop"):
-
-        @pl.loop(0, 9)
-        def _(t):
-            @pl.when(t < 8)
-            def _():
-                multiply(2, t)
-
-            @pl.when(t > 0)
-            def _():
-                encode(t - 1, 0, total_of(2, t - 1))
-                first_hop(t - 1).start()
-
-    with phase("A_y56"):
+        far_rows = (lambda t: multiply(2, t)), 0
+        run(0, 3, far_rows)
+        run(3, 6, far_rows, (hop, 3))
         y_relay(4)
+        run(6, 8, far_rows, (hop, 3))
         y_relay(5)
+        run(5, 8, (hop, 0))
+    with phase("A_y6"):
         y_relay(6)
     with phase("A_far2345"):
         for k in range(2, 6):
@@ -397,30 +400,18 @@
             encode(t, 2, total_of(ahead, t) + decode(rl.at[t]))
             onward(t).start()
 
-        @pl.loop(0, 9)
-        def _(t):
-            @pl.when(t < 8)
-            def _():
-                multiply(1, t)
-                multiply(3, t)
-
-            @pl.when(t > 0)
-            def _():
-                both(t - 1)
-
+        def near_rows(t):
+            multiply(1, t)
+            multiply(3, t)
+
+        run(0, 3, (near_rows, 0))
+        run(3, 5, (near_rows, 0), (both, 3))
         y_relay(7)
+        run(5, 8, (near_rows, 0), (both, 3))
+        run(5, 8, (both, 0))
 
     with phase("A_far67"):
         spread.middle(False)
-        for k in range(6, 8):
-            y_far(k)
-            normalise(k)
-    with phase("F_mul0"):
-
-        @pl.loop(0, 8)
-        def _(t):
-            multiply(0, t)
-
         top = jnp.max(targets[...].astype(F32), axis=1, keepdims=True)
         part = jnp.zeros((128, 256), F32)
         for k in range(8):
@@ -431,15 +422,21 @@
             row_tile(top)[0:1],
             row_tile(jnp.sum(part, axis=1, keepdims=True))[0:1],
         )
+        for k in range(6, 8):
+            y_far(k)
+            normalise(k)
+
+    def finish(t):
+        own = total_of(0, t)
+        for k in range(2):
+            arrived(fin.at[t, k], fin_r.at[t, k], at.partner(), fin_r.at[t, k])
+        lg[t] = own + decode(fin.at[t, 0]) + decode(fin.at[t, 1])
 
     with phase("F_fin"):
-
-        @pl.loop(0, 8)
-        def _(t):
-            own = total_of(0, t)
-            for k in range(2):
-                arrived(fin.at[t, k], fin_r.at[t, k], at.partner(), fin_r.at[t, k])
-            lg[t] = own + decode(fin.at[t, 0]) + decode(fin.at[t, 1])
+        own_rows = (lambda t: multiply(0, t)), 0
+        run(0, 3, own_rows)
+        run(3, 8, own_rows, (finish, 3))
+        run(5, 8, (finish, 0))
 
     def tell_all(tile, send_sem, recv_sem):
         @pl.loop(1, 32)
@@ -599,16 +596,29 @@
             half = grad_out.at[k, (y + step) % NY, side]
             send(half, half, a_y2.at[side, k], up_y if side == 0 else down_y)
 
-    def to_hbm(k):
-        return pltpu.make_async_copy(grad_out.at[k], grad_hbm.at[k], local_sems.at[2 + k])
+    grad_to_hbm = pltpu.make_async_copy(grad_out.at[3], grad_hbm, local_sems.at[2])
+    feat_to_hbm = pltpu.make_async_copy(feat_out.at[3], feat_hbm, local_sems.at[3])
+    acc_to_hbm = pltpu.make_async_copy(joined, joined_hbm, local_sems.at[4])
+
+    def fold(k):
+        @pl.loop(0, 4)
+        def _(n):
+            columns = pl.ds(pl.multiple_of(n * 256, 256), 256)
+            part = lax.dot_general(
+                grad_out[k, :, :, :, :, columns].reshape(256, 256),
+                feat_out[k].reshape(256, 768),
+                (((0,), (0,)), ((), ())),
+                preferred_element_type=F32,
+            )
+            if k == 0:
+                joined[columns, :] = part
+            else:
+                joined[columns, :] += part
 
     def across_far(k):
         for side in range(2):
             half = grad_out.at[k, (y + 2) % NY, side]
             arrived(half, a_y2.at[side, k], up_y, a_y2.at[side, k])
-        to_hbm(k).start()
-
-    feat_to_hbm = pltpu.make_async_copy(feat_out, feat_hbm, local_sems.at[6])
 
     with phase("G_bw0"):
         backward(0)
@@ -617,12 +627,6 @@
         for step in (0, 1, 3):
             for half in range(2):
                 spread.paired(step, half)
-    with phase("G_mid"):
-        gather.middle(True)
-    with phase("G_ys0"):
-        y_second(0)
-    with phase("G_bw1"):
-        backward(1)
     with phase("G_dot"):
         hear_all(dot_v, dv_r)
         dot = jnp.sum(dot_v[:, 0, :], axis=0, keepdims=True)
@@ -630,6 +634,12 @@
         srow[g] = jnp.broadcast_to(factor * factor * dot / (1024.0 * 8), (8, 128))
         for k in range(1, 8):
             send(srow.at[g], srow.at[g], sd_r.at[g], at.dp((g + k) % 8))
+    with phase("G_mid"):
+        gather.middle(True)
+    with phase("G_ys0"):
+        y_second(0)
+    with phase("G_bw1"):
+        backward(1)
     with phase("G_yt0"):
         y_third(0)
     with phase("G_mid2"):
@@ -682,33 +692,43 @@
         z_fourth(2)
     with phase("H_yt3"):
         y_third(3)
+    with phase("H_far0"):
+        across_far(0)
+    with phase("H_fold0"):
+        fold(0)
     with phase("H_ar1"):
-        across_far(0)
         across_relay(1)
     with phase("H_ax2"):
         across(2)
     with phase("H_z3"):
         z_fourth(3)
+    with phase("H_far1"):
+        across_far(1)
+    with phase("H_fold1"):
+        fold(1)
     with phase("H_ar2"):
-        across_far(1)
         across_relay(2)
     with phase("H_ax3"):
         across(3)
     with phase("H_far2"):
         across_far(2)
+    with phase("H_fold2"):
+        fold(2)
+        acc_to_hbm.start()
     with phase("H_ar3"):
         across_relay(3)
     with phase("H_far"):
         across_far(3)
+        grad_to_hbm.start()
         away = (z // 2 + NX - x) % NX
         odd, side = away % 2, away // 2
         for half in range(2):
             k = odd * (1 + (half + side + 1) % 2) + (1 - odd) * 3 * side
             p = odd * (1 - side) + (1 - odd) * half
             share_out[16 * half : 16 * half + 16, :] = grad_out[k, y, p, z % 2]
-        for k in range(4):
-            to_hbm(k).wait()
+        grad_to_hbm.wait()
         feat_to_hbm.wait()
+        acc_to_hbm.wait()
 
     with phase("H_drain"):
 
@@ -749,12 +769,14 @@
         kernel,
         out_shape=(
             jax.ShapeDtypeStruct((32, 1024), BF16),
-            jax.ShapeDtypeStruct((4, NY, 2, 2, 16, 1024), BF16),
-            jax.ShapeDtypeStruct((4, NY, 2, 2, 16, 768), BF16),
+            jax.ShapeDtypeStruct((1024, 768), F32),
+            jax.ShapeDtypeStruct((NY, 2, 2, 16, 1024), BF16),
+            jax.ShapeDtypeStruct((NY, 2, 2, 16, 768), BF16),
         ),
         in_specs=[VMEM] * 5 + [HBM] * 2,
-        out_specs=[VMEM, HBM, HBM],
+        out_specs=[VMEM, HBM, HBM, HBM],
         scratch_shapes=[
+            pltpu.VMEM((1024, 768), F32),
             pltpu.VMEM((4, NY, 2, 2, 16, 1024), BF16),
             pltpu.VMEM((4, NY, 2, 2, 16, 768), BF16),
             pltpu.VMEM((8, 2, 64, 768), BF16),
@@ -828,7 +850,7 @@
 
 
 def body(hidden, norm_gain, head_weight, target_logits, valid_rows, parents, features):
-    share, grad, parent_features = call(
+    share, joined, grad, parent_features = call(
         hidden,
         valid_rows.reshape(1, 128),
         parents.reshape(1, 128),
@@ -837,9 +859,10 @@
         head_weight,
         target_logits,
     )
-    grad_joining = lax.dot_general(
-        grad.reshape(1024, 1024),
-        parent_features.reshape(1024, 768),
+    grad_joining = joined + lax.dot_general(
+        *lax.optimization_barrier(
+            (grad.reshape(256, 1024), parent_features.reshape(256, 768))
+        ),
         (((0,), (0,)), ((), ())),
         preferred_element_type=F32,
     )

time: 147 us -> 143 us (0.973)
  Pallas kernels: 140 us -> 137 us
    pallas_call x1, Pallas kernels: 140 us -> 137 us  [call(): pl.pallas_call(kernel, out_shape=(jax.ShapeDtypeStruct((32, 1024), BF16),...]
where the time goes in v5:
time: 143 us; the launch traced here: 142 us
  Pallas kernels  137 us (96%)
  matrix products  4.5 us (3%)
    pallas_call x1, Pallas kernels, call(): pl.pallas_call(kernel, out_shape=(jax.ShapeDtypeStruct((32, 1024), BF16),...  137 us
    dot_general x1, matrix products, body(): lax.dot_general(*lax.optimization_barrier((grad.reshape(256, 1024), paren...  4.5 us

profile of v5, /device:TPU:24, one launch (start us, length us, event | category | flops | bytes accessed | tf_op | source)
XLA Modules:
  0.0 142.3 jit_solution(18150136905921384725)
XLA Ops:
  0.6 136.6 %shard_map.86 = (bf16[32,1024]{1,0:T(8,128)(2,1)}, f32[1024,768]{1,0:T(8,128)}, bf16[4,2,2,16,1024]{4,3,2,1,0:T(8,128)(2,1)}, bf16[4,2,2,16,768]{4,3,2,1,0:T(8,128)(2,1)}) custom-call(bf16[128,256]{1,0:T(8,128)(2,1)} %hid.1, s32[1,128]{1,0:T(1,128)} %bitcast.10, s32[1,128]{1,0:T(1,128)} %bitcast.11, bf16[128,768]{1,0:T(8,128)(2,1)} %feat.1, ...), custom_call_target="tpu_custom_call" | custom-call | tf_op jit(solution)/shard_map/pallas_call | solution.py:768
  137.2 0.0 copy-start
  137.2 4.5 %convolution_add_fusion = f32[1024,768]{1,0:T(8,128)} fusion(f32[1024,768]{1,0:T(8,128)} %get-tuple-element.9, bf16[256,1024]{1,0:T(8,128)(2,1)} %bitcast.7, bf16[256,768]{1,0:T(8,128)(2,1)} %bitcast.8), kind=kOutput, calls=%fused_computation | convolution fusion | flops 403439616 | bytes 7208960 | tf_op jit(solution)/shard_map/dot_general | solution.py:862
  141.7 0.0 copy-done
  141.7 0.6 copy.10
Async XLA Ops:
  137.2 4.5 %copy-start = (bf16[32,1024]{1,0:T(8,128)(2,1)S(1)}, bf16[32,1024]{1,0:T(8,128)(2,1)}, u32[]{:S(2)}) copy-start(bf16[32,1024]{1,0:T(8,128)(2,1)} %get-tuple-element.16) | copy-start | bytes 196612

commit v6 on v5

--- a/solution.py
+++ b/solution.py
@@ -323,15 +323,23 @@
         )
 
     def encode(t, k, value):
-        top = jnp.max(jnp.abs(value), axis=0, keepdims=True)
+        left, right = value[:, :128], value[:, 128:]
+        top = jnp.max(jnp.maximum(jnp.abs(left), jnp.abs(right)), axis=0, keepdims=True)
         step = (120.0 / jnp.maximum(top, 1e-30)).astype(BF16)
-        sb[t, k, 128:] = jnp.broadcast_to(step, (16, 256))
-        step = sb[t, k, 128:].astype(F32)[0:1]
-        sb[t, k, :128] = jnp.exp2(value * step).astype(BF16)
+        sb[t, k, 256:] = jnp.broadcast_to(step, (16, 128))
+        step = sb[t, k, 256:].astype(F32)[0:1]
+        sb[t, k, :128] = jnp.exp2(left * step).astype(BF16)
+        sb[t, k, 128:256] = jnp.exp2(right * step).astype(BF16)
 
     def decode(block):
-        step = block[128:].astype(F32)[0:1]
-        return jnp.log2(block[:128].astype(F32)) * (1.0 / step)
+        size = 1.0 / block[256:].astype(F32)[0:1]
+        return jnp.concatenate(
+            [
+                jnp.log2(block[:128].astype(F32)) * size,
+                jnp.log2(block[128:256].astype(F32)) * size,
+            ],
+            axis=1,
+        )
 
     with phase("A_ysend"):
         for k in range(3):
@@ -585,15 +593,20 @@
         for j in (1, 7, 2, 6, 3, 5, 4):
             other = (z + j) % NZ
             arrived(piece_of(k, other), a_z.at[k, other], up_y, a_z.at[k, other])
-        mine = grad_out.at[k, y]
-        send(mine, mine, a_y.at[0, k], up_y)
-        send(mine, mine, a_y.at[1, k], down_y)
+        for turn in range(2):
+            for side, device in ((0, up_y), (1, down_y)):
+                p = side if turn == 0 else 1 - side
+                mine = grad_out.at[k, y, p]
+                send(mine, mine, a_y.at[side, k, p], device)
+
+    def across_near(k, side, p):
+        half = grad_out.at[k, (y + (3 if side == 0 else 1)) % NY, p]
+        arrived(half, a_y.at[side, k, p], up_y, a_y.at[side, k, p])
+        return half
 
     def across_relay(k):
-        for side, step in ((0, 3), (1, 1)):
-            block = grad_out.at[k, (y + step) % NY]
-            arrived(block, a_y.at[side, k], up_y, a_y.at[side, k])
-            half = grad_out.at[k, (y + step) % NY, side]
+        for side in range(2):
+            half = across_near(k, side, side)
             send(half, half, a_y2.at[side, k], up_y if side == 0 else down_y)
 
     grad_to_hbm = pltpu.make_async_copy(grad_out.at[3], grad_hbm, local_sems.at[2])
@@ -616,6 +629,8 @@
                 joined[columns, :] += part
 
     def across_far(k):
+        for side in range(2):
+            across_near(k, side, 1 - side)
         for side in range(2):
             half = grad_out.at[k, (y + 2) % NY, side]
             arrived(half, a_y2.at[side, k], up_y, a_y2.at[side, k])
@@ -656,20 +671,16 @@
             scols[i] = column_tile(srow[i, 0:1])
     with phase("G_z0"):
         z_fourth(0)
+    with phase("G_last"):
+        gather.last()
+    with phase("G_bw3"):
+        backward(3)
     with phase("G_yt1"):
         y_third(1)
-    with phase("G_last"):
-        gather.last()
     with phase("G_ys2"):
         y_second(2)
-    with phase("G_bw3"):
-        backward(3)
     with phase("H_ax0"):
         across(0)
-    with phase("H_z1"):
-        z_fourth(1)
-    with phase("H_yt2"):
-        y_third(2)
     with phase("H_feat"):
         spread.paired(2, 0)
         spread.paired(2, 1)
@@ -686,22 +697,26 @@
         y_second(3)
     with phase("H_ar0"):
         across_relay(0)
+    with phase("H_yt2"):
+        y_third(2)
+    with phase("H_z1"):
+        z_fourth(1)
+    with phase("H_yt3"):
+        y_third(3)
+    with phase("H_z2"):
+        z_fourth(2)
     with phase("H_ax1"):
         across(1)
-    with phase("H_z2"):
-        z_fourth(2)
-    with phase("H_yt3"):
-        y_third(3)
     with phase("H_far0"):
         across_far(0)
     with phase("H_fold0"):
         fold(0)
     with phase("H_ar1"):
         across_relay(1)
+    with phase("H_z3"):
+        z_fourth(3)
     with phase("H_ax2"):
         across(2)
-    with phase("H_z3"):
-        z_fourth(3)
     with phase("H_far1"):
         across_far(1)
     with phase("H_fold1"):
@@ -712,11 +727,11 @@
         across(3)
     with phase("H_far2"):
         across_far(2)
+    with phase("H_ar3"):
+        across_relay(3)
     with phase("H_fold2"):
         fold(2)
         acc_to_hbm.start()
-    with phase("H_ar3"):
-        across_relay(3)
     with phase("H_far"):
         across_far(3)
         grad_to_hbm.start()
@@ -793,9 +808,9 @@
             pltpu.VMEM((1, 1024), F32),
             pltpu.VMEM((NX, 8, 2, 128, 256), F32),
             pltpu.VMEM((NX, 8, 128, 256), F32),
-            pltpu.VMEM((8, 3, 144, 256), BF16),
-            pltpu.VMEM((8, 144, 256), BF16),
-            pltpu.VMEM((8, 2, 144, 256), BF16),
+            pltpu.VMEM((8, 3, 272, 128), BF16),
+            pltpu.VMEM((8, 272, 128), BF16),
+            pltpu.VMEM((8, 2, 272, 128), BF16),
             pltpu.VMEM((8, 128, 256), F32),
             pltpu.VMEM((8, 128), F32),
             pltpu.VMEM((32, 8, 128), F32),
@@ -809,7 +824,7 @@
             pltpu.VMEM((4, NZ, 2, 2, 16, 128), BF16),
             pltpu.VMEM((4, NZ, 2, 2, 16, 128), BF16),
             DMA((7,)),
-            DMA((140,)),
+            DMA((148,)),
             DMA((GATHER_SENDS,)),
             DMA((4, NZ)),
             DMA((8,)),
@@ -840,7 +855,7 @@
             DMA((4, NZ)),
             DMA((4, NZ)),
             DMA((4, NZ)),
-            DMA((2, 4)),
+            DMA((2, 4, 2)),
             DMA((2, 4)),
         ],
         compiler_params=pltpu.CompilerParams(

time: 143 us -> 144 us (level)
    pallas_call x1, Pallas kernels: 137 us -> 138 us  [call(): pl.pallas_call(kernel, out_shape=(jax.ShapeDtypeStruct((32, 1024), BF16),...]
where the time goes in v6:
time: 144 us
  Pallas kernels  138 us (96%)
  matrix products  4.5 us (3%)
    pallas_call x1, Pallas kernels, call(): pl.pallas_call(kernel, out_shape=(jax.ShapeDtypeStruct((32, 1024), BF16),...  138 us
    dot_general x1, matrix products, body(): lax.dot_general(*lax.optimization_barrier((grad.reshape(256, 1024), paren...  4.5 us

profile of v6, /device:TPU:24, one launch (start us, length us, event | category | flops | bytes accessed | tf_op | source)
XLA Modules:
  0.0 144.1 jit_solution(5199529558409431390)
XLA Ops:
  0.6 138.3 %shard_map.86 = (bf16[32,1024]{1,0:T(8,128)(2,1)}, f32[1024,768]{1,0:T(8,128)}, bf16[4,2,2,16,1024]{4,3,2,1,0:T(8,128)(2,1)}, bf16[4,2,2,16,768]{4,3,2,1,0:T(8,128)(2,1)}) custom-call(bf16[128,256]{1,0:T(8,128)(2,1)} %hid.1, s32[1,128]{1,0:T(1,128)} %bitcast.10, s32[1,128]{1,0:T(1,128)} %bitcast.11, bf16[128,768]{1,0:T(8,128)(2,1)} %feat.1, ...), custom_call_target="tpu_custom_call" | custom-call | tf_op jit(solution)/shard_map/pallas_call | solution.py:783
  138.9 0.0 copy-start
  138.9 4.5 %convolution_add_fusion = f32[1024,768]{1,0:T(8,128)} fusion(f32[1024,768]{1,0:T(8,128)} %get-tuple-element.9, bf16[256,1024]{1,0:T(8,128)(2,1)} %bitcast.7, bf16[256,768]{1,0:T(8,128)(2,1)} %bitcast.8), kind=kOutput, calls=%fused_computation | convolution fusion | flops 403439616 | bytes 7208960 | tf_op jit(solution)/shard_map/dot_general | solution.py:877
  143.4 0.0 copy-done
  143.4 0.6 copy.10
Async XLA Ops:
  138.9 4.5 %copy-start = (bf16[32,1024]{1,0:T(8,128)(2,1)S(1)}, bf16[32,1024]{1,0:T(8,128)(2,1)}, u32[]{:S(2)}) copy-start(bf16[32,1024]{1,0:T(8,128)(2,1)} %get-tuple-element.16) | copy-start | bytes 196612

commit v7 on v6

--- a/solution.py
+++ b/solution.py
@@ -133,8 +133,9 @@
 
 
 def kernel(
-    hid, valid, parents, feat, gains, weight_hbm, targets_hbm,
-    share_out, joined_hbm, grad_hbm, feat_hbm,
+    hid_hbm, valid_hbm, parents_hbm, feat_hbm_in, gains_hbm, weight_hbm, targets_hbm,
+    share_hbm, joined_hbm, grad_hbm, feat_hbm,
+    hid, valid, parents, feat, gains, share_out,
     joined, grad_out, feat_out, fall,
     weight, targets, zbuf, xall, normed, stat, cols, scols, rf, srow, gain,
     pk, pr, sb, rl, fin, lg, tst, stat_v, dot_v, gbuf, pf, ysb, yrl, yfin,
@@ -150,12 +151,50 @@
     up_z, down_z = at.at_z((z + 1) % NZ), at.at_z((z + NZ - 1) % NZ)
     up_y, down_y = at.at_y((y + 1) % NY), at.at_y((y + 3) % NY)
 
+    loads = [
+        pltpu.make_async_copy(src, dst, local_sems.at[5 + k])
+        for k, (src, dst) in enumerate(
+            (
+                (hid_hbm, hid),
+                (parents_hbm, parents),
+                (feat_hbm_in, feat),
+                (valid_hbm, valid),
+                (gains_hbm, gains),
+            )
+        )
+    ]
+    for load in loads:
+        load.start()
     load_weight = pltpu.make_async_copy(weight_hbm, weight, local_sems.at[0])
     load_targets = pltpu.make_async_copy(targets_hbm, targets, local_sems.at[1])
     load_weight.start()
     load_targets.start()
 
     with phase("A_feat"):
+        barrier = pltpu.get_barrier_semaphore()
+
+        @pl.loop(1, 32)
+        def _(k):
+            pl.semaphore_signal(
+                barrier,
+                inc=1,
+                device_id=(g, (v + k) % 32),
+                device_id_type=pl.DeviceIdType.MESH,
+            )
+
+        @pl.loop(1, 8)
+        def _(k):
+            pl.semaphore_signal(
+                barrier,
+                inc=1,
+                device_id=((g + k) % 8, v),
+                device_id_type=pl.DeviceIdType.MESH,
+            )
+
+    with phase("A_load"):
+        for load in loads:
+            load.wait()
+    with phase("A_own"):
         live = (valid[...] == 1).astype(F32)
         row = lax.broadcasted_iota(jnp.int32, (128, 128), 0)
         lane = lax.broadcasted_iota(jnp.int32, (128, 128), 1)
@@ -168,26 +207,6 @@
         gain[...] = jnp.concatenate([own_gain[k : k + 1] for k in range(8)], axis=1)
 
     with phase("A_greet"):
-        barrier = pltpu.get_barrier_semaphore()
-
-        @pl.loop(1, 32)
-        def _(k):
-            pl.semaphore_signal(
-                barrier,
-                inc=1,
-                device_id=(g, (v + k) % 32),
-                device_id_type=pl.DeviceIdType.MESH,
-            )
-
-        @pl.loop(1, 8)
-        def _(k):
-            pl.semaphore_signal(
-                barrier,
-                inc=1,
-                device_id=((g + k) % 8, v),
-                device_id_type=pl.DeviceIdType.MESH,
-            )
-
         pl.semaphore_wait(barrier, 38)
     send = Sender(send_sems)
     spread = Gather(at, fall, Sender(f_sems), f_near, f_far, f_pair)
@@ -611,6 +630,7 @@
 
     grad_to_hbm = pltpu.make_async_copy(grad_out.at[3], grad_hbm, local_sems.at[2])
     feat_to_hbm = pltpu.make_async_copy(feat_out.at[3], feat_hbm, local_sems.at[3])
+    share_to_hbm = pltpu.make_async_copy(share_out, share_hbm, local_sems.at[10])
     acc_to_hbm = pltpu.make_async_copy(joined, joined_hbm, local_sems.at[4])
 
     def fold(k):
@@ -642,6 +662,10 @@
         for step in (0, 1, 3):
             for half in range(2):
                 spread.paired(step, half)
+    with phase("G_mid"):
+        gather.middle(True)
+    with phase("G_ys0"):
+        y_second(0)
     with phase("G_dot"):
         hear_all(dot_v, dv_r)
         dot = jnp.sum(dot_v[:, 0, :], axis=0, keepdims=True)
@@ -649,10 +673,6 @@
         srow[g] = jnp.broadcast_to(factor * factor * dot / (1024.0 * 8), (8, 128))
         for k in range(1, 8):
             send(srow.at[g], srow.at[g], sd_r.at[g], at.dp((g + k) % 8))
-    with phase("G_mid"):
-        gather.middle(True)
-    with phase("G_ys0"):
-        y_second(0)
     with phase("G_bw1"):
         backward(1)
     with phase("G_yt0"):
@@ -673,10 +693,10 @@
         z_fourth(0)
     with phase("G_last"):
         gather.last()
+    with phase("G_yt1"):
+        y_third(1)
     with phase("G_bw3"):
         backward(3)
-    with phase("G_yt1"):
-        y_third(1)
     with phase("G_ys2"):
         y_second(2)
     with phase("H_ax0"):
@@ -693,38 +713,38 @@
                             2 * block_of(step) + which, dest // 2, row : row + 16, :
                         ]
         feat_to_hbm.start()
-    with phase("H_ys3"):
+    with phase("H_z1"):
+        z_fourth(1)
+    with phase("G_ys3"):
         y_second(3)
+    with phase("G_yt2"):
+        y_third(2)
+    with phase("H_ax1"):
+        across(1)
+    with phase("G_yt3"):
+        y_third(3)
     with phase("H_ar0"):
         across_relay(0)
-    with phase("H_yt2"):
-        y_third(2)
-    with phase("H_z1"):
-        z_fourth(1)
-    with phase("H_yt3"):
-        y_third(3)
     with phase("H_z2"):
         z_fourth(2)
-    with phase("H_ax1"):
-        across(1)
     with phase("H_far0"):
         across_far(0)
-    with phase("H_fold0"):
-        fold(0)
     with phase("H_ar1"):
         across_relay(1)
     with phase("H_z3"):
         z_fourth(3)
     with phase("H_ax2"):
         across(2)
+    with phase("H_fold0"):
+        fold(0)
     with phase("H_far1"):
         across_far(1)
-    with phase("H_fold1"):
-        fold(1)
     with phase("H_ar2"):
         across_relay(2)
     with phase("H_ax3"):
         across(3)
+    with phase("H_fold1"):
+        fold(1)
     with phase("H_far2"):
         across_far(2)
     with phase("H_ar3"):
@@ -741,6 +761,8 @@
             k = odd * (1 + (half + side + 1) % 2) + (1 - odd) * 3 * side
             p = odd * (1 - side) + (1 - odd) * half
             share_out[16 * half : 16 * half + 16, :] = grad_out[k, y, p, z % 2]
+        share_to_hbm.start()
+        share_to_hbm.wait()
         grad_to_hbm.wait()
         feat_to_hbm.wait()
         acc_to_hbm.wait()
@@ -788,9 +810,15 @@
             jax.ShapeDtypeStruct((NY, 2, 2, 16, 1024), BF16),
             jax.ShapeDtypeStruct((NY, 2, 2, 16, 768), BF16),
         ),
-        in_specs=[VMEM] * 5 + [HBM] * 2,
-        out_specs=[VMEM, HBM, HBM, HBM],
+        in_specs=[HBM] * 7,
+        out_specs=[HBM] * 4,
         scratch_shapes=[
+            pltpu.VMEM((128, 256), BF16),
+            pltpu.VMEM((1, 128), jnp.int32),
+            pltpu.VMEM((1, 128), jnp.int32),
+            pltpu.VMEM((128, 768), BF16),
+            pltpu.VMEM((8, 8, 128), F32),
+            pltpu.VMEM((32, 1024), BF16),
             pltpu.VMEM((1024, 768), F32),
             pltpu.VMEM((4, NY, 2, 2, 16, 1024), BF16),
             pltpu.VMEM((4, NY, 2, 2, 16, 768), BF16),
@@ -823,7 +851,7 @@
             pltpu.VMEM((4, NZ, 2, 2, 16, 128), F32),
             pltpu.VMEM((4, NZ, 2, 2, 16, 128), BF16),
             pltpu.VMEM((4, NZ, 2, 2, 16, 128), BF16),
-            DMA((7,)),
+            DMA((11,)),
             DMA((148,)),
             DMA((GATHER_SENDS,)),
             DMA((4, NZ)),

time: 144 us -> 141 us (0.979)
  Pallas kernels: 138 us -> 135 us
    pallas_call x1, Pallas kernels: 138 us -> 135 us  [call(): pl.pallas_call(kernel, out_shape=(jax.ShapeDtypeStruct((32, 1024), BF16),...]
where the time goes in v7:
time: 141 us; the launch traced here: 140 us
  Pallas kernels  135 us (96%)
  matrix products  4.5 us (3%)
    pallas_call x1, Pallas kernels, call(): pl.pallas_call(kernel, out_shape=(jax.ShapeDtypeStruct((32, 1024), BF16),...  135 us
    dot_general x1, matrix products, body(): lax.dot_general(*lax.optimization_barrier((grad.reshape(256, 1024), paren...  4.5 us

profile of v7, /device:TPU:24, one launch (start us, length us, event | category | flops | bytes accessed | tf_op | source)
XLA Modules:
  0.0 140.4 jit_solution(15430200713025181454)
XLA Ops:
  0.6 134.6 %shard_map.86 = (bf16[32,1024]{1,0:T(8,128)(2,1)}, f32[1024,768]{1,0:T(8,128)}, bf16[4,2,2,16,1024]{4,3,2,1,0:T(8,128)(2,1)}, bf16[4,2,2,16,768]{4,3,2,1,0:T(8,128)(2,1)}) custom-call(bf16[128,256]{1,0:T(8,128)(2,1)} %hid_hbm.1, s32[1,128]{1,0:T(1,128)} %bitcast.10, s32[1,128]{1,0:T(1,128)} %bitcast.11, bf16[128,768]{1,0:T(8,128)(2,1)} %feat_hbm_in.1, ...), custom_call_target="tpu_custom_call" | custom-call | tf_op jit(solution)/shard_map/pallas_call | solution.py:805
  135.2 0.0 copy-start
  135.2 4.5 %convolution_add_fusion = f32[1024,768]{1,0:T(8,128)} fusion(f32[1024,768]{1,0:T(8,128)} %get-tuple-element.9, bf16[256,1024]{1,0:T(8,128)(2,1)} %bitcast.7, bf16[256,768]{1,0:T(8,128)(2,1)} %bitcast.8), kind=kOutput, calls=%fused_computation | convolution fusion | flops 403439616 | bytes 7208960 | tf_op jit(solution)/shard_map/dot_general | solution.py:905
  139.7 0.0 copy-done
  139.7 0.6 copy.10
Async XLA Ops:
  135.2 4.5 %copy-start = (bf16[32,1024]{1,0:T(8,128)(2,1)S(1)}, bf16[32,1024]{1,0:T(8,128)(2,1)}, u32[]{:S(2)}) copy-start(bf16[32,1024]{1,0:T(8,128)(2,1)} %get-tuple-element.16) | copy-start | bytes 196612

commit v8 on v7

--- a/solution.py
+++ b/solution.py
@@ -65,6 +65,18 @@
     def drain(self):
         for copy in self.copies:
             copy.wait_send()
+        self.used, self.copies = 0, []
+
+
+class Group:
+    def __init__(self, sem):
+        self.sem = sem
+
+    def __call__(self, src, dst, recv_sem, device):
+        remote(src, dst, self.sem, recv_sem, device).start()
+
+    def drain(self, like, device):
+        remote(like, like, self.sem, self.sem, device).wait_send()
 
 
 def arrived(dst, recv_sem, device, any_sem):
@@ -113,9 +125,6 @@
         arrived(block, self.pair.at[step, half], at.partner(), self.pair.at[step, half])
 
 
-GATHER_SENDS = 14
-
-
 def row_tile(column):
     return jnp.transpose(jnp.broadcast_to(column, (128, 128)))[0:8]
 
@@ -140,11 +149,11 @@
     weight, targets, zbuf, xall, normed, stat, cols, scols, rf, srow, gain,
     pk, pr, sb, rl, fin, lg, tst, stat_v, dot_v, gbuf, pf, ysb, yrl, yfin,
     qf, qs, zrs,
-    local_sems, send_sems, f_sems, zr, xs, xr, yr, y2, sr, fr,
+    local_sems, send_sems, group_sems, zr, xs, xr, yr, y2, sr, fr,
     f_near, f_far, f_pair,
     pair_s, pair_r, sb_s, rl_r, fin_r,
-    sv_s, sv_r, dv_s, dv_r, sd_r, g_sems, g_near, g_far, g_pair,
-    yrl_r, yfin_r, zs_s, zs_r, a_z, a_y, a_y2,
+    sv_r, dv_r, sd_r, g_near, g_far, g_pair,
+    yrl_r, yfin_r, zs_s, zs_r, az_s, a_z, a_y, a_y2,
 ):
     at = Place()
     x, c, y, z, g, v = at.x, at.c, at.y, at.z, at.g, at.v
@@ -209,7 +218,7 @@
     with phase("A_greet"):
         pl.semaphore_wait(barrier, 38)
     send = Sender(send_sems)
-    spread = Gather(at, fall, Sender(f_sems), f_near, f_far, f_pair)
+    spread = Gather(at, fall, Group(group_sems.at[0]), f_near, f_far, f_pair)
 
     def to_slice(src, j):
         @pl.when(j != g)
@@ -221,17 +230,17 @@
             pltpu.make_async_copy(src, xall.at[y, g], xs.at[j]).start()
 
     def piece(ref, q):
-        return ref.at[32 * q : 32 * q + 32]
+        return ref.at[64 * q : 64 * q + 64]
 
     with phase("A_z"):
-        for q in range(4):
+        for q in range(2):
             send(piece(hid, q), piece(zbuf.at[z], q), zr.at[q, z], up_z)
             send(piece(hid, q), piece(zbuf.at[z], q), zr.at[q, z], down_z)
         to_slice(hid, z)
         spread.start()
         for step in range(1, 5):
             low, high = (z + NZ - step) % NZ, (z + step) % NZ
-            for q in range(4):
+            for q in range(2):
                 block = piece(zbuf.at[low], q)
                 arrived(block, zr.at[q, low], up_z, zr.at[q, low])
                 if step < 4:
@@ -245,12 +254,13 @@
                 to_slice(zbuf.at[high], high)
 
     with phase("A_stat"):
+        small = Group(group_sems.at[2])
         squares = jnp.square(hid[...].astype(F32))
         for k in range(1, NZ):
             squares = squares + jnp.square(zbuf[(z + k) % NZ].astype(F32))
         stat[y] = row_tile(jnp.sum(squares, axis=1, keepdims=True))
         for k in range(1, NY):
-            send(stat.at[y], stat.at[y], sr.at[y], at.at_y((y + k) % NY))
+            small(stat.at[y], stat.at[y], sr.at[0], at.at_y((y + k) % NY))
 
     turns = (2, 1, 3, 0)
 
@@ -301,7 +311,7 @@
     def pair_copy(step, t):
         return remote(
             pk.at[step, t, 1 - c], pr.at[step, t],
-            pair_s.at[step, t], pair_r.at[step, t], at.partner(),
+            pair_s.at[step], pair_r.at[step, t], at.partner(),
         )
 
     def multiply(step, t):
@@ -327,18 +337,18 @@
 
     def first_hop(t):
         ahead, _ = ways(t)
-        return remote(sb.at[t, 0], rl.at[t], sb_s.at[t, 0], rl_r.at[t], at.at_x((x + ahead) % NX))
+        return remote(sb.at[t, 0], rl.at[t], sb_s.at[0], rl_r.at[t], at.at_x((x + ahead) % NX))
 
     def direct(t):
         _, back = ways(t)
         return remote(
-            sb.at[t, 1], fin.at[t, 0], sb_s.at[t, 1], fin_r.at[t, 0], at.at_x((x + back) % NX)
+            sb.at[t, 1], fin.at[t, 0], sb_s.at[1], fin_r.at[t, 0], at.at_x((x + back) % NX)
         )
 
     def onward(t):
         ahead, _ = ways(t)
         return remote(
-            sb.at[t, 2], fin.at[t, 1], sb_s.at[t, 2], fin_r.at[t, 1], at.at_x((x + ahead) % NX)
+            sb.at[t, 2], fin.at[t, 1], sb_s.at[2], fin_r.at[t, 1], at.at_x((x + ahead) % NX)
         )
 
     def encode(t, k, value):
@@ -365,24 +375,22 @@
             y_send(k)
 
     with phase("A_rf"):
+        arrived(stat.at[0:3], sr.at[0], up_y, sr.at[0])
         total = stat[y]
         for k in range(1, NY):
-            other = (y + k) % NY
-            arrived(stat.at[other], sr.at[other], up_y, sr.at[other])
-            total = total + stat[other]
+            total = total + stat[(y + k) % NY]
         factor = lax.rsqrt(total / (1024.0 * 8) + 1e-05)
         rf[g] = stack_rows(factor[0:1], live)
+        factors = Group(group_sems.at[3])
         for k in range(1, 8):
-            send(rf.at[g], rf.at[g], fr.at[g], at.dp((g + k) % 8))
+            factors(rf.at[g], rf.at[g], fr.at[0], at.dp((g + k) % 8))
 
     with phase("A_y0123"):
         y_relay(0)
         y_relay(1)
         spread.middle(True)
         y_relay(2)
-        for k in range(1, 8):
-            other = (g + k) % 8
-            arrived(rf.at[other], fr.at[other], up_y, fr.at[other])
+        arrived(rf.at[0:7], fr.at[0], up_y, fr.at[0])
         for i in range(8):
             cols[i] = column_tile(rf[i, 0:1])
         y_relay(3)
@@ -469,14 +477,11 @@
         @pl.loop(1, 32)
         def _(k):
             remote(
-                tile.at[v], tile.at[v], send_sem.at[k], recv_sem.at[v], (g, (v + k) % 32)
+                tile.at[v], tile.at[v], send_sem, recv_sem.at[0], (g, (v + k) % 32)
             ).start()
 
     def hear_all(tile, recv_sem):
-        @pl.loop(1, 32)
-        def _(k):
-            other = (v + k) % 32
-            arrived(tile.at[other], recv_sem.at[other], up_y, recv_sem.at[other])
+        arrived(tile.at[0:31], recv_sem.at[0], up_y, recv_sem.at[0])
 
     with phase("B_stat"):
         top = lg[0]
@@ -492,7 +497,8 @@
             tst[2:3],
             tst[3:4],
         )
-        tell_all(stat_v, sv_s, sv_r)
+        tell_all(stat_v, group_sems.at[5], sv_r)
+        send.drain()
 
     with phase("B_statv"):
         hear_all(stat_v, sv_r)
@@ -509,7 +515,7 @@
         count = jnp.sum(count, axis=1, keepdims=True)
         scale = wide(1048576.0 * live / count)
 
-    gather = Gather(at, gbuf, Sender(g_sems), g_near, g_far, g_pair)
+    gather = Gather(at, gbuf, Group(group_sems.at[1]), g_near, g_far, g_pair)
     with phase("B_G"):
         acc = jnp.zeros((128, 256), F32)
         for t in range(8):
@@ -525,7 +531,7 @@
             acc = acc + value.astype(F32) * lg[t]
         gather.start()
         dot_v[v] = row_tile(jnp.sum(acc, axis=1, keepdims=True))
-        tell_all(dot_v, dv_s, dv_r)
+        tell_all(dot_v, group_sems.at[6], dv_r)
 
     units = (((0, 0), (0, 1)), ((3, 0), (1, 1)), ((3, 1), (1, 0)), ((2, 0), (2, 1)))
 
@@ -567,7 +573,7 @@
 
     def z_send(k, dest):
         return remote(
-            qs.at[k, dest], zrs.at[k, z], zs_s.at[k, dest], zs_r.at[k, z], at.at_z(dest)
+            qs.at[k, dest], zrs.at[k, z], zs_s.at[k], zs_r.at[k], at.at_z(dest)
         )
 
     far_first = (4, 3, 5, 2, 6, 1, 7)
@@ -589,12 +595,14 @@
         columns = pl.ds(pl.multiple_of(owner * 128, 128), 128)
         return grad_out.at[k, y, :, :, :, columns]
 
+    def seven(k):
+        return grad_out.at[k, y, :, :, :, 0:896]
+
     def z_fourth(k):
         total = qf[k, z]
+        arrived(zrs.at[k, 0:7], zs_r.at[k], up_y, zs_r.at[k])
         for j in range(1, NZ):
-            other = (z + j) % NZ
-            arrived(zrs.at[k, other], zs_r.at[k, other], up_y, zs_r.at[k, other])
-            total = total + zrs[k, other].astype(F32)
+            total = total + zrs[k, (z + j) % NZ].astype(F32)
         lanes = pl.ds(pl.multiple_of((z % 2) * 128, 128), 128)
         for p, (step, half) in enumerate(units[k]):
             rows = pl.ds(pl.multiple_of(y * 32 + half * 16, 16), 16)
@@ -606,12 +614,10 @@
                 grad_out[k, y, p, which, :, own_columns] = grad.astype(BF16)
         mine = piece_of(k, z)
         for shift in far_first:
-            send(mine, mine, a_z.at[k, z], at.at_z((z + shift) % NZ))
+            remote(mine, mine, az_s.at[k], a_z.at[k], at.at_z((z + shift) % NZ)).start()
 
     def across(k):
-        for j in (1, 7, 2, 6, 3, 5, 4):
-            other = (z + j) % NZ
-            arrived(piece_of(k, other), a_z.at[k, other], up_y, a_z.at[k, other])
+        arrived(seven(k), a_z.at[k], up_y, a_z.at[k])
         for turn in range(2):
             for side, device in ((0, up_y), (1, down_y)):
                 p = side if turn == 0 else 1 - side
@@ -671,8 +677,9 @@
         dot = jnp.sum(dot_v[:, 0, :], axis=0, keepdims=True)
         factor = rf[g][0:1]
         srow[g] = jnp.broadcast_to(factor * factor * dot / (1024.0 * 8), (8, 128))
+        pulls = Group(group_sems.at[4])
         for k in range(1, 8):
-            send(srow.at[g], srow.at[g], sd_r.at[g], at.dp((g + k) % 8))
+            pulls(srow.at[g], srow.at[g], sd_r.at[0], at.dp((g + k) % 8))
     with phase("G_bw1"):
         backward(1)
     with phase("G_yt0"):
@@ -684,9 +691,7 @@
     with phase("G_bw2"):
         backward(2)
     with phase("G_s"):
-        for k in range(1, 8):
-            other = (g + k) % 8
-            arrived(srow.at[other], sd_r.at[other], up_y, sd_r.at[other])
+        arrived(srow.at[0:7], sd_r.at[0], up_y, sd_r.at[0])
         for i in range(8):
             scols[i] = column_tile(srow[i, 0:1])
     with phase("G_z0"):
@@ -768,27 +773,26 @@
         acc_to_hbm.wait()
 
     with phase("H_drain"):
-
-        @pl.loop(0, 8)
-        def _(t):
-            for step in range(4):
-                pair_copy(step, t).wait_send()
-            first_hop(t).wait_send()
-            direct(t).wait_send()
-            onward(t).wait_send()
-
-        @pl.loop(1, 32)
-        def _(k):
-            other = (g, (v + k) % 32)
-            remote(stat_v.at[v], stat_v.at[v], sv_s.at[k], sv_r.at[v], other).wait_send()
-            remote(dot_v.at[v], dot_v.at[v], dv_s.at[k], dv_r.at[v], other).wait_send()
-
+        there = at.partner()
+        for step in range(NX):
+            remote(
+                pr.at[step], pr.at[step], pair_s.at[step], pair_r.at[step, 0], there
+            ).wait_send()
+        for k in range(3):
+            remote(rl, rl, sb_s.at[k], rl_r.at[0], there).wait_send()
+        for k, like in enumerate(
+            (
+                fall.at[0:7], gbuf.at[0:7], stat.at[0:3], rf.at[0:7],
+                srow.at[0:7], stat_v.at[0:31], dot_v.at[0:31],
+            )
+        ):
+            Group(group_sems.at[k]).drain(like, there)
         send.drain()
-        spread.send.drain()
-        gather.send.drain()
         for k in range(4):
-            for j in range(1, NZ):
-                z_send(k, (z + j) % NZ).wait_send()
+            remote(
+                qs.at[k, 0:7], zrs.at[k, 0:7], zs_s.at[k], zs_r.at[k], there
+            ).wait_send()
+            remote(seven(k), seven(k), az_s.at[k], a_z.at[k], there).wait_send()
         for j in range(8):
 
             @pl.when(g != j)
@@ -852,37 +856,35 @@
             pltpu.VMEM((4, NZ, 2, 2, 16, 128), BF16),
             pltpu.VMEM((4, NZ, 2, 2, 16, 128), BF16),
             DMA((11,)),
-            DMA((148,)),
-            DMA((GATHER_SENDS,)),
-            DMA((4, NZ)),
+            DMA((38,)),
+            DMA((7,)),
+            DMA((2, NZ)),
             DMA((8,)),
             DMA((8,)),
             DMA((2, 8)),
             DMA((8,)),
-            DMA((NY,)),
-            DMA((8,)),
+            DMA((1,)),
+            DMA((1,)),
             DMA((2, 2)),
             DMA((2,)),
             DMA((4, 2)),
+            DMA((NX,)),
             DMA((NX, 8)),
-            DMA((NX, 8)),
-            DMA((8, 3)),
+            DMA((3,)),
             DMA((8,)),
             DMA((8, 2)),
-            DMA((32,)),
-            DMA((32,)),
-            DMA((32,)),
-            DMA((32,)),
-            DMA((8,)),
-            DMA((GATHER_SENDS,)),
+            DMA((1,)),
+            DMA((1,)),
+            DMA((1,)),
             DMA((2, 2)),
             DMA((2,)),
             DMA((4, 2)),
             DMA((4,)),
             DMA((4, 2)),
-            DMA((4, NZ)),
-            DMA((4, NZ)),
-            DMA((4, NZ)),
+            DMA((4,)),
+            DMA((4,)),
+            DMA((4,)),
+            DMA((4,)),
             DMA((2, 4, 2)),
             DMA((2, 4)),
         ],

time: 141 us -> 136 us (0.965); the launches traced: 140 us -> 134 us
  Pallas kernels: 135 us -> 128 us
    pallas_call x1, Pallas kernels: 135 us -> 128 us  [call(): pl.pallas_call(kernel, out_shape=(jax.ShapeDtypeStruct((32, 1024), BF16),...]
where the time goes in v8:
time: 136 us; the launch traced here: 134 us
  Pallas kernels  128 us (94%)
  matrix products  4.5 us (3%)
    pallas_call x1, Pallas kernels, call(): pl.pallas_call(kernel, out_shape=(jax.ShapeDtypeStruct((32, 1024), BF16),...  128 us
    dot_general x1, matrix products, body(): lax.dot_general(*lax.optimization_barrier((grad.reshape(256, 1024), paren...  4.5 us

profile of v8, /device:TPU:24, one launch (start us, length us, event | category | flops | bytes accessed | tf_op | source)
XLA Modules:
  0.0 133.9 jit_solution(16085987663861496704)
XLA Ops:
  0.6 128.1 %shard_map.86 = (bf16[32,1024]{1,0:T(8,128)(2,1)}, f32[1024,768]{1,0:T(8,128)}, bf16[4,2,2,16,1024]{4,3,2,1,0:T(8,128)(2,1)}, bf16[4,2,2,16,768]{4,3,2,1,0:T(8,128)(2,1)}) custom-call(bf16[128,256]{1,0:T(8,128)(2,1)} %hid_hbm.1, s32[1,128]{1,0:T(1,128)} %bitcast.10, s32[1,128]{1,0:T(1,128)} %bitcast.11, bf16[128,768]{1,0:T(8,128)(2,1)} %feat_hbm_in.1, ...), custom_call_target="tpu_custom_call" | custom-call | tf_op jit(solution)/shard_map/pallas_call | solution.py:809
  128.7 0.0 copy-start
  128.7 4.5 %convolution_add_fusion = f32[1024,768]{1,0:T(8,128)} fusion(f32[1024,768]{1,0:T(8,128)} %get-tuple-element.9, bf16[256,1024]{1,0:T(8,128)(2,1)} %bitcast.7, bf16[256,768]{1,0:T(8,128)(2,1)} %bitcast.8), kind=kOutput, calls=%fused_computation | convolution fusion | flops 403439616 | bytes 7208960 | tf_op jit(solution)/shard_map/dot_general | solution.py:907
  133.2 0.0 copy-done
  133.2 0.6 copy.10
Async XLA Ops:
  128.7 4.5 %copy-start = (bf16[32,1024]{1,0:T(8,128)(2,1)S(1)}, bf16[32,1024]{1,0:T(8,128)(2,1)}, u32[]{:S(2)}) copy-start(bf16[32,1024]{1,0:T(8,128)(2,1)} %get-tuple-element.16) | copy-start | bytes 196612

commit v9 on v8

--- a/solution.py
+++ b/solution.py
@@ -49,23 +49,6 @@
 
     def at_z(self, z):
         return (self.g, z * NY + self.y)
-
-
-class Sender:
-    def __init__(self, sems):
-        self.sems, self.used, self.copies = sems, 0, []
-
-    def __call__(self, src, dst, recv_sem, device):
-        assert self.used < self.sems.shape[0]
-        copy = remote(src, dst, self.sems.at[self.used], recv_sem, device)
-        self.used += 1
-        copy.start()
-        self.copies.append(copy)
-
-    def drain(self):
-        for copy in self.copies:
-            copy.wait_send()
-        self.used, self.copies = 0, []
 
 
 class Group:
@@ -149,7 +132,7 @@
     weight, targets, zbuf, xall, normed, stat, cols, scols, rf, srow, gain,
     pk, pr, sb, rl, fin, lg, tst, stat_v, dot_v, gbuf, pf, ysb, yrl, yfin,
     qf, qs, zrs,
-    local_sems, send_sems, group_sems, zr, xs, xr, yr, y2, sr, fr,
+    local_sems, group_sems, zr, xs, xr, yr, y2, sr, fr,
     f_near, f_far, f_pair,
     pair_s, pair_r, sb_s, rl_r, fin_r,
     sv_r, dv_r, sd_r, g_near, g_far, g_pair,
@@ -217,25 +200,27 @@
 
     with phase("A_greet"):
         pl.semaphore_wait(barrier, 38)
-    send = Sender(send_sems)
+    send_z, send_y = Group(group_sems.at[7]), Group(group_sems.at[8])
+    send_part, send_grad = Group(group_sems.at[9]), Group(group_sems.at[10])
+    send_x = Group(group_sems.at[11])
     spread = Gather(at, fall, Group(group_sems.at[0]), f_near, f_far, f_pair)
 
     def to_slice(src, j):
         @pl.when(j != g)
         def _():
-            remote(src, xall.at[y, g], xs.at[j], xr.at[g], at.dp(j)).start()
+            send_x(src, xall.at[y, g], xr.at[g], at.dp(j))
 
         @pl.when(j == g)
         def _():
-            pltpu.make_async_copy(src, xall.at[y, g], xs.at[j]).start()
+            pltpu.make_async_copy(src, xall.at[y, g], xs.at[0]).start()
 
     def piece(ref, q):
         return ref.at[64 * q : 64 * q + 64]
 
     with phase("A_z"):
         for q in range(2):
-            send(piece(hid, q), piece(zbuf.at[z], q), zr.at[q, z], up_z)
-            send(piece(hid, q), piece(zbuf.at[z], q), zr.at[q, z], down_z)
+            send_z(piece(hid, q), piece(zbuf.at[z], q), zr.at[q, z], up_z)
+            send_z(piece(hid, q), piece(zbuf.at[z], q), zr.at[q, z], down_z)
         to_slice(hid, z)
         spread.start()
         for step in range(1, 5):
@@ -244,11 +229,11 @@
                 block = piece(zbuf.at[low], q)
                 arrived(block, zr.at[q, low], up_z, zr.at[q, low])
                 if step < 4:
-                    send(block, block, zr.at[q, low], up_z)
+                    send_z(block, block, zr.at[q, low], up_z)
                     block = piece(zbuf.at[high], q)
                     arrived(block, zr.at[q, high], up_z, zr.at[q, high])
                     if step < 3:
-                        send(block, block, zr.at[q, high], down_z)
+                        send_z(block, block, zr.at[q, high], down_z)
             to_slice(zbuf.at[low], low)
             if step < 4:
                 to_slice(zbuf.at[high], high)
@@ -280,17 +265,17 @@
 
             @pl.when(c == k % 2)
             def _():
-                pltpu.make_async_copy(hid, block, xs.at[g]).wait()
-
-        send(block, block, yr.at[0, k], up_y)
-        send(block, block, yr.at[1, k], down_y)
+                pltpu.make_async_copy(hid, block, xs.at[0]).wait()
+
+        send_y(block, block, yr.at[0, k], up_y)
+        send_y(block, block, yr.at[1, k], down_y)
 
     def y_relay(k):
         for side, step in ((0, 3), (1, 1)):
             block = xall.at[(y + step) % NY, group(k)]
             arrived(block, yr.at[side, k], up_y, yr.at[side, k])
             if k % 2 == side:
-                send(block, block, y2.at[k], up_y if side == 0 else down_y)
+                send_y(block, block, y2.at[k], up_y if side == 0 else down_y)
         if k + 3 < 8:
             y_send(k + 3)
 
@@ -498,7 +483,6 @@
             tst[3:4],
         )
         tell_all(stat_v, group_sems.at[5], sv_r)
-        send.drain()
 
     with phase("B_statv"):
         hear_all(stat_v, sv_r)
@@ -561,15 +545,15 @@
 
         way = 1 if k % 2 == 0 else 3
         ysb[k, 0] = pf[k, (y + 2) % NY].astype(BF16)
-        send(ysb.at[k, 0], yrl.at[k], yrl_r.at[k], at.at_y((y + way) % NY))
+        send_part(ysb.at[k, 0], yrl.at[k], yrl_r.at[k], at.at_y((y + way) % NY))
         ysb[k, 1] = pf[k, (y + 4 - way) % NY].astype(BF16)
-        send(ysb.at[k, 1], yfin.at[k, 0], yfin_r.at[k, 0], at.at_y((y + 4 - way) % NY))
+        send_part(ysb.at[k, 1], yfin.at[k, 0], yfin_r.at[k, 0], at.at_y((y + 4 - way) % NY))
 
     def y_second(k):
         way = 1 if k % 2 == 0 else 3
         arrived(yrl.at[k], yrl_r.at[k], up_y, yrl_r.at[k])
         ysb[k, 2] = (pf[k, (y + way) % NY] + yrl[k].astype(F32)).astype(BF16)
-        send(ysb.at[k, 2], yfin.at[k, 1], yfin_r.at[k, 1], at.at_y((y + way) % NY))
+        send_part(ysb.at[k, 2], yfin.at[k, 1], yfin_r.at[k, 1], at.at_y((y + way) % NY))
 
     def z_send(k, dest):
         return remote(
@@ -622,7 +606,7 @@
             for side, device in ((0, up_y), (1, down_y)):
                 p = side if turn == 0 else 1 - side
                 mine = grad_out.at[k, y, p]
-                send(mine, mine, a_y.at[side, k, p], device)
+                send_grad(mine, mine, a_y.at[side, k, p], device)
 
     def across_near(k, side, p):
         half = grad_out.at[k, (y + (3 if side == 0 else 1)) % NY, p]
@@ -632,7 +616,7 @@
     def across_relay(k):
         for side in range(2):
             half = across_near(k, side, side)
-            send(half, half, a_y2.at[side, k], up_y if side == 0 else down_y)
+            send_grad(half, half, a_y2.at[side, k], up_y if side == 0 else down_y)
 
     grad_to_hbm = pltpu.make_async_copy(grad_out.at[3], grad_hbm, local_sems.at[2])
     feat_to_hbm = pltpu.make_async_copy(feat_out.at[3], feat_hbm, local_sems.at[3])
@@ -738,22 +722,22 @@
         across_relay(1)
     with phase("H_z3"):
         z_fourth(3)
+    with phase("H_fold0"):
+        fold(0)
     with phase("H_ax2"):
         across(2)
-    with phase("H_fold0"):
-        fold(0)
     with phase("H_far1"):
         across_far(1)
-    with phase("H_ar2"):
-        across_relay(2)
     with phase("H_ax3"):
         across(3)
     with phase("H_fold1"):
         fold(1)
+    with phase("H_ar2"):
+        across_relay(2)
+    with phase("H_ar3"):
+        across_relay(3)
     with phase("H_far2"):
         across_far(2)
-    with phase("H_ar3"):
-        across_relay(3)
     with phase("H_fold2"):
         fold(2)
         acc_to_hbm.start()
@@ -784,20 +768,15 @@
             (
                 fall.at[0:7], gbuf.at[0:7], stat.at[0:3], rf.at[0:7],
                 srow.at[0:7], stat_v.at[0:31], dot_v.at[0:31],
+                zbuf.at[0:7], xall.at[0:3], ysb, grad_out.at[0:3], zbuf.at[0:7],
             )
         ):
             Group(group_sems.at[k]).drain(like, there)
-        send.drain()
         for k in range(4):
             remote(
                 qs.at[k, 0:7], zrs.at[k, 0:7], zs_s.at[k], zs_r.at[k], there
             ).wait_send()
             remote(seven(k), seven(k), az_s.at[k], a_z.at[k], there).wait_send()
-        for j in range(8):
-
-            @pl.when(g != j)
-            def _():
-                remote(hid, xall.at[y, g], xs.at[j], xr.at[g], at.dp(j)).wait_send()
 
 
 VMEM = pl.BlockSpec(memory_space=pltpu.VMEM)
@@ -856,10 +835,9 @@
             pltpu.VMEM((4, NZ, 2, 2, 16, 128), BF16),
             pltpu.VMEM((4, NZ, 2, 2, 16, 128), BF16),
             DMA((11,)),
-            DMA((38,)),
-            DMA((7,)),
+            DMA((12,)),
             DMA((2, NZ)),
-            DMA((8,)),
+            DMA((1,)),
             DMA((8,)),
             DMA((2, 8)),
             DMA((8,)),

time: 136 us -> 134 us (0.985)
  no operation moved by 1% of the time
where the time goes in v9:
time: 134 us; the launch traced here: 133 us
  Pallas kernels  127 us (95%)
  matrix products  4.5 us (3%)
    pallas_call x1, Pallas kernels, call(): pl.pallas_call(kernel, out_shape=(jax.ShapeDtypeStruct((32, 1024), BF16),...  127 us
    dot_general x1, matrix products, body(): lax.dot_general(*lax.optimization_barrier((grad.reshape(256, 1024), paren...  4.5 us

profile of v9, /device:TPU:24, one launch (start us, length us, event | category | flops | bytes accessed | tf_op | source)
XLA Modules:
  0.0 132.9 jit_solution(3462334083584034364)
XLA Ops:
  0.6 127.1 %shard_map.86 = (bf16[32,1024]{1,0:T(8,128)(2,1)}, f32[1024,768]{1,0:T(8,128)}, bf16[4,2,2,16,1024]{4,3,2,1,0:T(8,128)(2,1)}, bf16[4,2,2,16,768]{4,3,2,1,0:T(8,128)(2,1)}) custom-call(bf16[128,256]{1,0:T(8,128)(2,1)} %hid_hbm.1, s32[1,128]{1,0:T(1,128)} %bitcast.10, s32[1,128]{1,0:T(1,128)} %bitcast.11, bf16[128,768]{1,0:T(8,128)(2,1)} %feat_hbm_in.1, ...), custom_call_target="tpu_custom_call" | custom-call | tf_op jit(solution)/shard_map/pallas_call | solution.py:788
  127.8 0.0 copy-start
  127.8 4.5 %convolution_add_fusion = f32[1024,768]{1,0:T(8,128)} fusion(f32[1024,768]{1,0:T(8,128)} %get-tuple-element.9, bf16[256,1024]{1,0:T(8,128)(2,1)} %bitcast.7, bf16[256,768]{1,0:T(8,128)(2,1)} %bitcast.8), kind=kOutput, calls=%fused_computation | convolution fusion | flops 403439616 | bytes 7208960 | tf_op jit(solution)/shard_map/dot_general | solution.py:885
  132.3 0.0 copy-done
  132.3 0.6 copy.10
Async XLA Ops:
  127.8 4.5 %copy-start = (bf16[32,1024]{1,0:T(8,128)(2,1)S(1)}, bf16[32,1024]{1,0:T(8,128)(2,1)}, u32[]{:S(2)}) copy-start(bf16[32,1024]{1,0:T(8,128)(2,1)} %get-tuple-element.16) | copy-start | bytes 196612

commit v10 on v9

--- a/solution.py
+++ b/solution.py
@@ -688,8 +688,6 @@
         backward(3)
     with phase("G_ys2"):
         y_second(2)
-    with phase("H_ax0"):
-        across(0)
     with phase("H_feat"):
         spread.paired(2, 0)
         spread.paired(2, 1)
@@ -702,10 +700,12 @@
                             2 * block_of(step) + which, dest // 2, row : row + 16, :
                         ]
         feat_to_hbm.start()
+    with phase("G_ys3"):
+        y_second(3)
+    with phase("H_ax0"):
+        across(0)
     with phase("H_z1"):
         z_fourth(1)
-    with phase("G_ys3"):
-        y_second(3)
     with phase("G_yt2"):
         y_third(2)
     with phase("H_ax1"):

time: 134 us -> 134 us (level)
  no operation moved by 1% of the time
where the time goes in v10:
time: 134 us; the launch traced here: 133 us
  Pallas kernels  127 us (95%)
  matrix products  4.5 us (3%)
    pallas_call x1, Pallas kernels, call(): pl.pallas_call(kernel, out_shape=(jax.ShapeDtypeStruct((32, 1024), BF16),...  127 us
    dot_general x1, matrix products, body(): lax.dot_general(*lax.optimization_barrier((grad.reshape(256, 1024), paren...  4.5 us

profile of v10, /device:TPU:24, one launch (start us, length us, event | category | flops | bytes accessed | tf_op | source)
XLA Modules:
  0.0 133.0 jit_solution(528293747407861378)
XLA Ops:
  0.6 127.2 %shard_map.86 = (bf16[32,1024]{1,0:T(8,128)(2,1)}, f32[1024,768]{1,0:T(8,128)}, bf16[4,2,2,16,1024]{4,3,2,1,0:T(8,128)(2,1)}, bf16[4,2,2,16,768]{4,3,2,1,0:T(8,128)(2,1)}) custom-call(bf16[128,256]{1,0:T(8,128)(2,1)} %hid_hbm.1, s32[1,128]{1,0:T(1,128)} %bitcast.10, s32[1,128]{1,0:T(1,128)} %bitcast.11, bf16[128,768]{1,0:T(8,128)(2,1)} %feat_hbm_in.1, ...), custom_call_target="tpu_custom_call" | custom-call | tf_op jit(solution)/shard_map/pallas_call | solution.py:788
  127.9 0.0 copy-start
  127.9 4.5 %convolution_add_fusion = f32[1024,768]{1,0:T(8,128)} fusion(f32[1024,768]{1,0:T(8,128)} %get-tuple-element.9, bf16[256,1024]{1,0:T(8,128)(2,1)} %bitcast.7, bf16[256,768]{1,0:T(8,128)(2,1)} %bitcast.8), kind=kOutput, calls=%fused_computation | convolution fusion | flops 403439616 | bytes 7208960 | tf_op jit(solution)/shard_map/dot_general | solution.py:885
  132.4 0.0 copy-done
  132.4 0.6 copy.10
Async XLA Ops:
  127.9 4.5 %copy-start = (bf16[32,1024]{1,0:T(8,128)(2,1)S(1)}, bf16[32,1024]{1,0:T(8,128)(2,1)}, u32[]{:S(2)}) copy-start(bf16[32,1024]{1,0:T(8,128)(2,1)} %get-tuple-element.16) | copy-start | bytes 196612
